TPU v7x, 32 devices: a whole 2x2x4 slice. The times are simulated.
32 devices in a mesh: dp: 8 (over z, x), seq: 4 (over y, core).
Axes of the slice: x: 2, y: 2, z: 4, core: 2. Of those that a mesh axis runs over, the one named last changes fastest.
Arguments:
- pixels: bfloat16 [16, 1024, 768], P('dp', 'seq'), may hold values from -6 to 6
- lengths: int32 [16, 3], P('dp'), may hold values from 66 to 578, as said below
- labels: int32 [16, 3], P('dp'), may hold values from 0 to 999
- teacher: float32 [16, 3, 1000], P('dp'), may hold values from -15 to 15
- embedder: float32 [768, 768], P(('dp', 'seq')), may hold values from -0.21875 to 0.21875
- embedder_mean: float32 [768, 768], P(('dp', 'seq')), may hold values from -1.1444092e-05 to 1.1444092e-05
- embedder_square: float32 [768, 768], P(('dp', 'seq')), may hold values from 2.7144834e-13 to 1.0857933e-12
- attend: float32 [1, 768, 2304], P(None, ('dp', 'seq')), may hold values from -0.21875 to 0.21875
- attend_mean: float32 [1, 768, 2304], P(None, ('dp', 'seq')), may hold values from -1.1444092e-05 to 1.1444092e-05
- attend_square: float32 [1, 768, 2304], P(None, ('dp', 'seq')), may hold values from 2.7144834e-13 to 1.0857933e-12
- merger: float32 [1, 768, 768], P(None, ('dp', 'seq')), may hold values from -0.875 to 0.875
- merger_mean: float32 [1, 768, 768], P(None, ('dp', 'seq')), may hold values from -1.1444092e-05 to 1.1444092e-05
- merger_square: float32 [1, 768, 768], P(None, ('dp', 'seq')), may hold values from 2.7144834e-13 to 1.0857933e-12
- expand: float32 [1, 768, 3072], P(None, ('dp', 'seq')), may hold values from -0.21875 to 0.21875
- expand_mean: float32 [1, 768, 3072], P(None, ('dp', 'seq')), may hold values from -1.1444092e-05 to 1.1444092e-05
- expand_square: float32 [1, 768, 3072], P(None, ('dp', 'seq')), may hold values from 2.7144834e-13 to 1.0857933e-12
- shrink: float32 [1, 3072, 768], P(None, ('dp', 'seq')), may hold values from -0.109375 to 0.109375
- shrink_mean: float32 [1, 3072, 768], P(None, ('dp', 'seq')), may hold values from -1.1444092e-05 to 1.1444092e-05
- shrink_square: float32 [1, 3072, 768], P(None, ('dp', 'seq')), may hold values from 2.7144834e-13 to 1.0857933e-12
- readout: float32 [2, 768, 1000], P(None, ('dp', 'seq')), may hold values from -0.21875 to 0.21875
- readout_mean: float32 [2, 768, 1000], P(None, ('dp', 'seq')), may hold values from -1.1444092e-05 to 1.1444092e-05
- readout_square: float32 [2, 768, 1000], P(None, ('dp', 'seq')), may hold values from 2.7144834e-13 to 1.0857933e-12
- vectors: float32 [8, 768], P(None, ('dp', 'seq')), may hold values from 0.5 to 1.5
- vectors_mean: float32 [8, 768], P(None, ('dp', 'seq')), may hold values from -4.5776367e-05 to 4.5776367e-05
- vectors_square: float32 [8, 768], P(None, ('dp', 'seq')), may hold values from 4.3431734e-12 to 1.7372694e-11
Outputs:
- embedder_next: float32 [768, 768], P(('dp', 'seq'))
- embedder_mean_next: float32 [768, 768], P(('dp', 'seq'))
- embedder_square_next: float32 [768, 768], P(('dp', 'seq'))
- attend_next: float32 [1, 768, 2304], P(None, ('dp', 'seq'))
- attend_mean_next: float32 [1, 768, 2304], P(None, ('dp', 'seq'))
- attend_square_next: float32 [1, 768, 2304], P(None, ('dp', 'seq'))
- merger_next: float32 [1, 768, 768], P(None, ('dp', 'seq'))
- merger_mean_next: float32 [1, 768, 768], P(None, ('dp', 'seq'))
- merger_square_next: float32 [1, 768, 768], P(None, ('dp', 'seq'))
- expand_next: float32 [1, 768, 3072], P(None, ('dp', 'seq'))
- expand_mean_next: float32 [1, 768, 3072], P(None, ('dp', 'seq'))
- expand_square_next: float32 [1, 768, 3072], P(None, ('dp', 'seq'))
- shrink_next: float32 [1, 3072, 768], P(None, ('dp', 'seq'))
- shrink_mean_next: float32 [1, 3072, 768], P(None, ('dp', 'seq'))
- shrink_square_next: float32 [1, 3072, 768], P(None, ('dp', 'seq'))
- readout_next: float32 [2, 768, 1000], P(None, ('dp', 'seq'))
- readout_mean_next: float32 [2, 768, 1000], P(None, ('dp', 'seq'))
- readout_square_next: float32 [2, 768, 1000], P(None, ('dp', 'seq'))
- vectors_mean_next: float32 [8, 768], P(None, ('dp', 'seq'))
- vectors_square_next: float32 [8, 768], P(None, ('dp', 'seq'))
- loss: float32 [], replicated
- grad_norm: float32 [], replicated
Inputs may be any that keep to these rules, and one draw needn't show every extreme that they name: `lengths`: each row holds 3 images in order and then padding; in every row one image has exactly 578 tokens and the others at most (446) // 2.
All inputs are finite; a program needn't handle non-finite values.
Results may differ from a plain program's by a relative error of at most 0.006.
The roundings to bfloat16 on the way count: a program that leaves them out, or rounds other values in their place, can miss the bound.
Values may be sent and summed in bfloat16 or wider, within the bound.
No kernel may reach another device: no remote copies, remote signals or barrier semaphores. Data moves between devices by JAX's collectives and lax.ppermute only.
A program may use at most 192 MiB of HBM per device.

v0:
```python
from functools import partial

import jax
import jax.numpy as jnp
from jax import lax
from jax.sharding import PartitionSpec as P

HEADS = 12
HD = 64
L = 1
ROW_LEN = 1024
IMGS = 3
STEP_COUNT = 7


NORM_EPS = 1e-06
MASKED = -1000000000.0
SCALE = 0.125
BETA_ONE = 0.9
BETA_TWO = 0.999
ADAM_EPS = 1e-08
DECAY = 0.05
BASE_RATE = 0.05
LAYER_RATE = 0.75
CLIP_AT = 0.05
HIGH = lax.Precision.HIGHEST
exact_gelu = partial(jax.nn.gelu, approximate=False)


def layer_norm(x, gain, shift):
    centre = x - jnp.mean(x, -1, keepdims=True)
    spread = jnp.mean(centre * centre, -1, keepdims=True)
    return centre * lax.rsqrt(spread + NORM_EPS) * gain + shift


def token_kinds(lengths, first, count):
    ends = jnp.cumsum(lengths, axis=1)
    starts = ends - lengths
    places = first + jnp.arange(count, dtype=jnp.int32)
    segment = jnp.sum((places[None, :, None] >= ends[:, None, :]).astype(jnp.int32), 2)
    is_cls = jnp.sum((places[None, :, None] == starts[:, None, :]).astype(jnp.float32), 2)
    is_dist = jnp.sum((places[None, :, None] == starts[:, None, :] + 1).astype(jnp.float32), 2)
    is_patch = (segment < IMGS).astype(jnp.float32) - is_cls - is_dist
    return (segment, is_cls, is_dist, is_patch, starts)


def split_heads(x):
    return x.reshape(x.shape[0], x.shape[1], HEADS, HD)


def merge_heads(x):
    return x.reshape(x.shape[0], x.shape[1], HEADS * HD)


def outer(left, right):
    return jnp.einsum("rti,rto->io", left, right, preferred_element_type=jnp.float32)


def inner(grad, weight):
    return jnp.einsum("rto,io->rti", grad, weight, preferred_element_type=jnp.float32)


def scores(queries, keys, seg_query, seg_key):
    raw = (
        jnp.einsum(
            "rqhd,rkhd->rhqk",
            split_heads(queries),
            split_heads(keys),
            preferred_element_type=jnp.float32,
        )
        * SCALE
    )
    return jnp.where(seg_query[:, None, :, None] == seg_key[:, None, None, :], raw, MASKED)


def layer_forward(x, weights, gains, seg_local, seg_whole):
    attend_w, merger_w, expand_w, shrink_w = weights
    a = layer_norm(x, gains[0], gains[1]).astype(jnp.bfloat16)
    projected = jnp.dot(a, attend_w, preferred_element_type=jnp.float32).astype(jnp.bfloat16)
    query, keys, values = jnp.split(projected, 3, axis=2)
    keys_all, values_all = (
        lax.all_gather(keys, "seq", axis=1, tiled=True),
        lax.all_gather(values, "seq", axis=1, tiled=True),
    )
    logits = scores(query, keys_all, seg_local, seg_whole)
    biggest = jnp.max(logits, -1, keepdims=True)
    log_total = biggest[..., 0] + jnp.log(jnp.sum(jnp.exp(logits - biggest), -1))
    shares = jnp.exp(logits - log_total[..., None]).astype(jnp.bfloat16)
    mixed = jnp.einsum(
        "rhqk,rkhd->rqhd", shares, split_heads(values_all), preferred_element_type=jnp.float32
    )
    mixed = merge_heads(mixed).astype(jnp.bfloat16)
    x_mid = x + jnp.dot(mixed, merger_w, preferred_element_type=jnp.float32)
    normed = layer_norm(x_mid, gains[2], gains[3]).astype(jnp.bfloat16)
    hidden_in = jnp.dot(normed, expand_w, preferred_element_type=jnp.float32)
    hidden = exact_gelu(hidden_in).astype(jnp.bfloat16)
    result = x_mid + jnp.dot(hidden, shrink_w, preferred_element_type=jnp.float32)
    return (
        result,
        (
            x,
            a,
            query,
            keys,
            values,
            keys_all,
            values_all,
            log_total,
            mixed,
            x_mid,
            normed,
            hidden_in,
            hidden,
        ),
    )


def layer_backward(grad_out, kept, weights, gains, seg_local, seg_whole):
    (
        x,
        a,
        query,
        keys,
        values,
        keys_all,
        values_all,
        log_total,
        mixed,
        x_mid,
        normed,
        hidden_in,
        hidden,
    ) = kept
    attend_w, merger_w, expand_w, shrink_w = weights
    grad_branch = grad_out.astype(jnp.bfloat16)
    grad_shrink = outer(hidden, grad_branch)
    _, gelu_back = jax.vjp(exact_gelu, hidden_in)
    grad_pre = gelu_back(inner(grad_branch, shrink_w))[0].astype(jnp.bfloat16)
    grad_expand = outer(normed, grad_pre)
    _, second_back = jax.vjp(layer_norm, x_mid, gains[2], gains[3])
    grad_normed, gain_two, shift_two = second_back(inner(grad_pre, expand_w))
    grad_mid = grad_out + grad_normed
    grad_attn = grad_mid.astype(jnp.bfloat16)
    grad_merger = outer(mixed, grad_attn)
    grad_mixed = inner(grad_attn, merger_w).astype(jnp.bfloat16)
    shares = jnp.exp(scores(query, keys_all, seg_local, seg_whole) - log_total[..., None])
    grad_shares = jnp.einsum(
        "rqhd,rkhd->rhqk",
        split_heads(grad_mixed),
        split_heads(values_all),
        preferred_element_type=jnp.float32,
    )
    spread = jnp.sum(grad_shares * shares, -1)
    grad_logits = (shares * (grad_shares - spread[..., None])).astype(jnp.bfloat16)
    grad_query = (
        merge_heads(
            jnp.einsum(
                "rhqk,rkhd->rqhd",
                grad_logits,
                split_heads(keys_all),
                preferred_element_type=jnp.float32,
            )
        )
        * SCALE
    )
    part_keys = (
        jnp.einsum(
            "rhqk,rqhd->rkhd", grad_logits, split_heads(query), preferred_element_type=jnp.float32
        )
        * SCALE
    )
    part_values = jnp.einsum(
        "rhqk,rqhd->rkhd",
        shares.astype(jnp.bfloat16),
        split_heads(grad_mixed),
        preferred_element_type=jnp.float32,
    )
    grad_keys, grad_values = (
        lax.psum_scatter(
            merge_heads(part_keys).astype(jnp.bfloat16), "seq", scatter_dimension=1, tiled=True
        ).astype(jnp.float32),
        lax.psum_scatter(
            merge_heads(part_values).astype(jnp.bfloat16), "seq", scatter_dimension=1, tiled=True
        ).astype(jnp.float32),
    )
    grad_proj = jnp.concatenate([grad_query, grad_keys, grad_values], 2).astype(jnp.bfloat16)
    grad_attend = outer(a, grad_proj)
    _, first_back = jax.vjp(layer_norm, x, gains[0], gains[1])
    grad_input, gain_one, shift_one = first_back(inner(grad_proj, attend_w))
    gain_grads = jnp.stack([gain_one, shift_one, gain_two, shift_two])
    return (grad_mid + grad_input, (grad_attend, grad_merger, grad_expand, grad_shrink), gain_grads)


def pick(x, index):
    local_len = x.shape[1]
    inside = ((index >= 0) & (index < local_len)).astype(jnp.float32)
    clamped = jnp.clip(index, 0, local_len - 1)
    picked = jnp.take_along_axis(
        x, jnp.broadcast_to(clamped[..., None], clamped.shape + (x.shape[2],)), 1
    )
    return (picked, inside)


def place(grad_rows, index, inside, local_len):
    hits = (
        (index[..., None] == jnp.arange(local_len, dtype=jnp.int32)) & (inside[..., None] > 0)
    ).astype(jnp.float32)
    return jnp.einsum("rit,rid->rtd", hits, grad_rows, precision=HIGH)


def head_terms(
    class_rows,
    distill_rows,
    class_in,
    distill_in,
    readout_w,
    gain,
    shift,
    labels,
    teacher,
    image_count,
):
    class_norm, class_back = jax.vjp(layer_norm, class_rows, gain, shift)
    distill_norm, distill_back = jax.vjp(layer_norm, distill_rows, gain, shift)
    class_low = class_norm.astype(jnp.bfloat16)
    distill_low = distill_norm.astype(jnp.bfloat16)
    class_logits = jnp.einsum(
        "rid,dc->ric", class_low, readout_w[0], preferred_element_type=jnp.float32
    )
    distill_logits = jnp.einsum(
        "rid,dc->ric", distill_low, readout_w[1], preferred_element_type=jnp.float32
    )
    class_total = jax.scipy.special.logsumexp(class_logits, axis=-1)
    label_hot = (labels[..., None] == jnp.arange(class_logits.shape[2], dtype=jnp.int32)).astype(
        jnp.float32
    )
    cross = class_total - jnp.sum(class_logits * label_hot, -1)
    teach_log = jax.nn.log_softmax(teacher, -1)
    teach_prob = jnp.exp(teach_log)
    distill_log = jax.nn.log_softmax(distill_logits, -1)
    diverge = jnp.sum(teach_prob * (teach_log - distill_log), -1)
    loss_local = jnp.sum(0.5 * cross * class_in + 0.5 * diverge * distill_in)
    grad_class = (
        0.5
        * (jnp.exp(class_logits - class_total[..., None]) - label_hot)
        * (class_in / image_count)[..., None]
    )
    grad_distill = 0.5 * (jnp.exp(distill_log) - teach_prob) * (distill_in / image_count)[..., None]
    table = readout_w.astype(jnp.float32)
    grad_readout = jnp.stack(
        [
            jnp.einsum("rid,ric->dc", class_low.astype(jnp.float32), grad_class, precision=HIGH),
            jnp.einsum(
                "rid,ric->dc", distill_low.astype(jnp.float32), grad_distill, precision=HIGH
            ),
        ]
    )
    class_rows_grad, gain_a, shift_a = class_back(
        jnp.einsum("ric,dc->rid", grad_class, table[0], precision=HIGH)
    )
    distill_rows_grad, gain_b, shift_b = distill_back(
        jnp.einsum("ric,dc->rid", grad_distill, table[1], precision=HIGH)
    )
    return (
        loss_local,
        class_rows_grad,
        distill_rows_grad,
        grad_readout,
        gain_a + gain_b,
        shift_a + shift_b,
    )


def rates():
    layer_scale = jnp.power(LAYER_RATE, (L - jnp.arange(L)).astype(jnp.float32))[:, None, None]
    return (LAYER_RATE ** (L + 1), layer_scale, layer_scale, layer_scale, layer_scale, 1.0)


def adamw(weight, mean, square, grad, scale, decay):
    mean_next = BETA_ONE * mean + (1.0 - BETA_ONE) * grad
    square_next = BETA_TWO * square + (1.0 - BETA_TWO) * grad * grad
    mean_hat = mean_next / (1.0 - BETA_ONE**STEP_COUNT)
    square_hat = square_next / (1.0 - BETA_TWO**STEP_COUNT)
    weight_next = weight - BASE_RATE * scale * (
        mean_hat / (jnp.sqrt(square_hat) + ADAM_EPS) + decay * weight
    )
    return (weight_next, mean_next, square_next)


def moments(mean, square, grad):
    return (
        BETA_ONE * mean + (1.0 - BETA_ONE) * grad,
        BETA_TWO * square + (1.0 - BETA_TWO) * grad * grad,
    )


def on_device(
    pixels,
    lengths,
    labels,
    teacher,
    embedder,
    embedder_mean,
    embedder_square,
    attend,
    attend_mean,
    attend_square,
    merger,
    merger_mean,
    merger_square,
    expand,
    expand_mean,
    expand_square,
    shrink,
    shrink_mean,
    shrink_square,
    readout,
    readout_mean,
    readout_square,
    vectors,
    vectors_mean,
    vectors_square,
):
    masters = (embedder, attend, merger, expand, shrink, readout)
    means = (embedder_mean, attend_mean, merger_mean, expand_mean, shrink_mean, readout_mean)
    squares = (
        embedder_square,
        attend_square,
        merger_square,
        expand_square,
        shrink_square,
        readout_square,
    )
    embed_w, attend_w, merger_w, expand_w, shrink_w, readout_w, vector_w = (
        lax.all_gather(embedder.astype(jnp.bfloat16), ("dp", "seq"), axis=0, tiled=True),
        lax.all_gather(attend.astype(jnp.bfloat16), ("dp", "seq"), axis=1, tiled=True),
        lax.all_gather(merger.astype(jnp.bfloat16), ("dp", "seq"), axis=1, tiled=True),
        lax.all_gather(expand.astype(jnp.bfloat16), ("dp", "seq"), axis=1, tiled=True),
        lax.all_gather(shrink.astype(jnp.bfloat16), ("dp", "seq"), axis=1, tiled=True),
        lax.all_gather(readout.astype(jnp.bfloat16), ("dp", "seq"), axis=1, tiled=True),
        lax.all_gather(vectors.astype(jnp.bfloat16), ("dp", "seq"), axis=1, tiled=True),
    )
    vector_f = vector_w.astype(jnp.float32)
    local_len = pixels.shape[1]
    first = lax.axis_index("seq") * local_len
    seg_local, is_cls, is_dist, is_patch, starts = token_kinds(lengths, first, local_len)
    seg_whole = token_kinds(lengths, 0, ROW_LEN)[0]
    patches = jnp.dot(pixels, embed_w, preferred_element_type=jnp.float32)
    x = (
        is_patch[..., None] * patches
        + is_cls[..., None] * vector_f[4 * L + 2]
        + is_dist[..., None] * vector_f[4 * L + 3]
    )
    layer = 0
    weights = (attend_w[layer], merger_w[layer], expand_w[layer], shrink_w[layer])
    x, kept = layer_forward(x, weights, vector_f[4 * layer : 4 * layer + 4], seg_local, seg_whole)
    kept_all = [kept]
    image_count = lengths.shape[0] * lax.axis_size("dp") * IMGS
    class_rows, class_in = pick(x, starts - first)
    distill_rows, distill_in = pick(x, starts + 1 - first)
    loss_local, class_grad, distill_grad, grad_readout, final_gain, final_shift = head_terms(
        class_rows,
        distill_rows,
        class_in,
        distill_in,
        readout_w,
        vector_f[4 * L],
        vector_f[4 * L + 1],
        labels,
        teacher,
        image_count,
    )
    loss_sum = lax.psum(loss_local, ("dp", "seq"))
    grad_x = place(class_grad, starts - first, class_in, local_len) + place(
        distill_grad, starts + 1 - first, distill_in, local_len
    )
    layer_grads = [None] * L
    gain_grads = [None] * L
    for layer in reversed(range(L)):
        weights = (attend_w[layer], merger_w[layer], expand_w[layer], shrink_w[layer])
        grad_x, layer_grads[layer], gain_grads[layer] = layer_backward(
            grad_x,
            kept_all[layer],
            weights,
            vector_f[4 * layer : 4 * layer + 4],
            seg_local,
            seg_whole,
        )
    grad_patch = (grad_x * is_patch[..., None]).astype(jnp.bfloat16)
    grad_embed = jnp.einsum("rtp,rtd->pd", pixels, grad_patch, preferred_element_type=jnp.float32)
    class_token = jnp.sum(grad_x * is_cls[..., None], (0, 1))
    distill_token = jnp.sum(grad_x * is_dist[..., None], (0, 1))
    grad_vectors = jnp.concatenate(
        gain_grads + [jnp.stack([final_gain, final_shift, class_token, distill_token])], 0
    )
    grad_attend = jnp.stack([g[0] for g in layer_grads])
    grad_merger = jnp.stack([g[1] for g in layer_grads])
    grad_expand = jnp.stack([g[2] for g in layer_grads])
    grad_shrink = jnp.stack([g[3] for g in layer_grads])
    reduced = (
        lax.psum_scatter(grad_embed, ("dp", "seq"), scatter_dimension=0, tiled=True),
        lax.psum_scatter(grad_attend, ("dp", "seq"), scatter_dimension=1, tiled=True),
        lax.psum_scatter(grad_merger, ("dp", "seq"), scatter_dimension=1, tiled=True),
        lax.psum_scatter(grad_expand, ("dp", "seq"), scatter_dimension=1, tiled=True),
        lax.psum_scatter(grad_shrink, ("dp", "seq"), scatter_dimension=1, tiled=True),
        lax.psum_scatter(grad_readout, ("dp", "seq"), scatter_dimension=1, tiled=True),
        lax.psum_scatter(grad_vectors, ("dp", "seq"), scatter_dimension=1, tiled=True),
    )
    square_sum = sum((jnp.sum(g * g) for g in reduced))
    norm_square = lax.psum(square_sum, ("dp", "seq"))
    grad_norm = jnp.sqrt(norm_square)
    factor = jnp.minimum(1.0, CLIP_AT / (grad_norm + 1e-06))
    scales = rates()
    fresh = [
        adamw(masters[j], means[j], squares[j], reduced[j] * factor, scales[j], DECAY)
        for j in range(6)
    ]
    vec_mean, vec_square = moments(vectors_mean, vectors_square, reduced[6] * factor)
    return (
        fresh[0][0],
        fresh[0][1],
        fresh[0][2],
        fresh[1][0],
        fresh[1][1],
        fresh[1][2],
        fresh[2][0],
        fresh[2][1],
        fresh[2][2],
        fresh[3][0],
        fresh[3][1],
        fresh[3][2],
        fresh[4][0],
        fresh[4][1],
        fresh[4][2],
        fresh[5][0],
        fresh[5][1],
        fresh[5][2],
        vec_mean,
        vec_square,
        loss_sum / image_count,
        grad_norm,
    )


def solution(mesh):
    return jax.shard_map(
        on_device,
        mesh=mesh,
        in_specs=(
            P("dp", "seq", None),
            P("dp", None),
            P("dp", None),
            P("dp", None, None),
            P(("dp", "seq"), None),
            P(("dp", "seq"), None),
            P(("dp", "seq"), None),
            P(None, ("dp", "seq"), None),
            P(None, ("dp", "seq"), None),
            P(None, ("dp", "seq"), None),
            P(None, ("dp", "seq"), None),
            P(None, ("dp", "seq"), None),
            P(None, ("dp", "seq"), None),
            P(None, ("dp", "seq"), None),
            P(None, ("dp", "seq"), None),
            P(None, ("dp", "seq"), None),
            P(None, ("dp", "seq"), None),
            P(None, ("dp", "seq"), None),
            P(None, ("dp", "seq"), None),
            P(None, ("dp", "seq"), None),
            P(None, ("dp", "seq"), None),
            P(None, ("dp", "seq"), None),
            P(None, ("dp", "seq")),
            P(None, ("dp", "seq")),
            P(None, ("dp", "seq")),
        ),
        out_specs=(
            P(("dp", "seq"), None),
            P(("dp", "seq"), None),
            P(("dp", "seq"), None),
            P(None, ("dp", "seq"), None),
            P(None, ("dp", "seq"), None),
            P(None, ("dp", "seq"), None),
            P(None, ("dp", "seq"), None),
            P(None, ("dp", "seq"), None),
            P(None, ("dp", "seq"), None),
            P(None, ("dp", "seq"), None),
            P(None, ("dp", "seq"), None),
            P(None, ("dp", "seq"), None),
            P(None, ("dp", "seq"), None),
            P(None, ("dp", "seq"), None),
            P(None, ("dp", "seq"), None),
            P(None, ("dp", "seq"), None),
            P(None, ("dp", "seq"), None),
            P(None, ("dp", "seq"), None),
            P(None, ("dp", "seq")),
            P(None, ("dp", "seq")),
            P(),
            P(),
        ),
        check_vma=False,
    )
```

profile of v0, /device:TPU:0, one launch (start us, length us, event | category | flops | bytes accessed | tf_op | source)
XLA Modules:
  0.0 1506.8 jit_solution(1288263295019450983)
XLA Ops:
  14.9 43.5 %all-gather = bf16[32,24,8]{1,2,0:T(8,128)(2,1)S(1)} all-gather(bf16[1,24,8]{1,2,0:T(8,128)(2,1)S(1)} %convert_bitcast_fusion), channel_id=1, replica_groups=mesh['dp'=8,'seq'=4] {'dp','seq'}, dimensions={0}, use_global_device_ids=true | all-gather | bytes 12672 | tf_op jit(solution)/shard_map/all_gather | solution.py:341
  59.1 9.2 all-gather.10.cloned.1.call-done
  70.8 59.8 %all-gather.12.cloned.1.call-done = bf16[1,768,2304]{2,1,0:T(8,128)(2,1)} async-done(((bf16[1,24,2304]{2,1,0:T(8,128)(2,1)}), bf16[1,768,2304]{2,1,0:T(8,128)(2,1)}) %all-gather.12.cloned.1.call-update) | async-done | bytes 3538960 | tf_op jit(solution)/shard_map/all_gather | solution.py:336
  140.3 51.8 %all-gather.24.cloned.1.call-done = bf16[2,768,1000]{2,0,1:T(2,128)(2,1)} async-done(((bf16[2,24,1000]{2,0,1:T(2,128)(2,1)}), bf16[2,768,1000]{2,0,1:T(2,128)(2,1)}) %all-gather.24.cloned.1.call-update) | async-done | bytes 3072016 | tf_op jit(solution)/shard_map/all_gather | solution.py:340
  192.1 9.4 fusion.124
  209.7 8.2 copy.213
  225.4 14.8 fusion.3
  240.3 10.4 all-gather.14.cloned.1.call-done
  255.4 11.9 exponential_reduce_fusion
  267.3 12.1 convolution_convert_fusion.3
  279.4 28.6 %all-gather.18.cloned.1.call-done = bf16[1,768,768]{2,1,0:T(8,128)(2,1)} async-done(((bf16[1,24,768]{2,1,0:T(8,128)(2,1)}), bf16[1,768,768]{2,1,0:T(8,128)(2,1)}) %all-gather.18.cloned.1.call-update) | async-done | bytes 1179664 | tf_op jit(solution)/shard_map/all_gather | solution.py:337
  312.0 62.1 %all-gather.20.cloned.1.call-done = bf16[1,768,3072]{2,1,0:T(8,128)(2,1)} async-done(((bf16[1,24,3072]{2,1,0:T(8,128)(2,1)}), bf16[1,768,3072]{2,1,0:T(8,128)(2,1)}) %all-gather.20.cloned.1.call-update) | async-done | bytes 4718608 | tf_op jit(solution)/shard_map/all_gather | solution.py:338
  384.1 15.3 %multiply_convert_fusion.2 = (bf16[2,256,3072]{2,1,0:T(8,128)(2,1)}, f32[2,256,3072]{2,1,0:T(8,128)}) fusion(f32[2,256,3072]{2,1,0:T(8,128)S(1)} %get-tuple-element.200, u8[256,3072]{1,0:T(8,128)(4,1)S(1)} %get-tuple-element.113, u8[256,3072]{1,0:T(8,128)(4,1)S(1)} %get-tuple-element.112), kind=kLoop, calls=%fused_computation.21 | loop fusion | flops 110100480 | bytes 17301504 | tf_op jit(solution)/shard_map/convert_element_type | solution.py:96
  399.4 40.1 %all-gather.22.cloned.1.call-done = bf16[1,3072,768]{2,1,0:T(8,128)(2,1)} async-done(((bf16[1,96,768]{2,1,0:T(8,128)(2,1)}), bf16[1,3072,768]{2,1,0:T(8,128)(2,1)}) %all-gather.22.cloned.1.call-update) | async-done | bytes 4718608 | tf_op jit(solution)/shard_map/all_gather | solution.py:339
  445.8 43.8 %gather_fusion.1 = f32[4608]{0:T(1024)S(1)} fusion(f32[2,256,768]{2,1,0:T(8,128)S(1)} %fusion.34, s32[4608]{0:T(1024)S(1)} %reshape.344), kind=kCustom, calls=%fused_computation.1.clone | custom fusion | bytes 92160 | tf_op jit(solution)/shard_map/jit(take_along_axis)/gather | solution.py:198
  489.7 44.2 %gather_fusion = f32[4608]{0:T(1024)S(1)} fusion(f32[2,256,768]{2,1,0:T(8,128)S(1)} %fusion.34, s32[4608]{0:T(1024)S(1)} %reshape.339), kind=kCustom, calls=%fused_computation.clone | custom fusion | bytes 92160 | tf_op jit(solution)/shard_map/jit(take_along_axis)/gather | solution.py:198
  543.8 9.0 add_convert_fusion
  561.5 12.7 convolution_convert_fusion.1
  578.9 20.0 %multiply_reduce_fusion = (f32[2,12,256]{2,1,0:T(8,128)S(1)}, f32[2,12,256,1024]{3,2,1,0:T(8,128)}) fusion(f32[2,12,256,1024]{3,2,1,0:T(8,128)} %get-tuple-element.197, f32[2,12,256]{2,1,0:T(8,128)S(1)} %log_add_fusion, pred[2,256,1024]{2,1,0:T(8,128)(4,1)S(1)} %broadcast_compare_fusion, bf16[2,256,12,64]{1,3,2,0:T(8,128)(2,1)S(1)} %bitcast.151, ...), kind=kOutput, calls=%fused_computation.6 | convolution fusion | flops 836757504 | bytes 54837248 | tf_op jit(solution)/shard_map/rqhd,rkhd->rhqk/dot_general | solution.py:147
  598.8 17.1 %multiply_convert_fusion = bf16[2,12,256,1024]{3,2,1,0:T(8,128)(2,1)S(1)} fusion(f32[2,12,256,1024]{3,2,1,0:T(8,128)} %get-tuple-element.208, f32[2,12,256,1024]{3,2,1,0:T(8,128)} %get-tuple-element.197, f32[2,12,256]{2,1,0:T(8,128)S(1)} %get-tuple-element.207, f32[2,12,256]{2,1,0:T(8,128)S(1)} %log_add_fusion, pred[2,256,1024]{2,1,0:T(8,128)(4,1)S(1)} %broadcast_compare_fusion), kind=kLoop, calls=%fused_computation.5 | loop fusion | flops 37748736 | bytes 63488000 | tf_op jit(solution)/shard_map/convert_element_type | solution.py:154
  632.7 10.5 copy.201
  646.6 9.6 multiply_convert_fusion.4
  676.5 8.9 convolution_bitcast_fusion.2
  685.5 8.8 convolution_bitcast_fusion.1
  702.1 122.0 %all-reduce.5.cloned.1.call-done = f32[2,768,1000]{2,0,1:T(2,128)} async-done(((f32[2,768,1000]{2,0,1:T(2,128)}), f32[2,768,1000]{2,0,1:T(2,128)}) %all-reduce.5.cloned.1.call-update) | async-done | bytes 6144016
  825.8 102.8 %reduce-scatter.17.cloned.1.call-done = f32[1,24,768]{2,1,0:T(8,128)} async-done(((f32[1,768,768]{2,1,0:T(8,128)}), f32[1,24,768]{2,1,0:T(8,128)}) %reduce-scatter.17.cloned.1.call-update) | async-done | bytes 73744 | tf_op jit(solution)/shard_map/reduce_scatter | solution.py:403
  930.2 40.3 %all-reduce.1 = f32[8,768]{1,0:T(8,128)S(1)} all-reduce(f32[8,768]{1,0:T(8,128)S(1)} %concatenate.8), channel_id=10, replica_groups=mesh['dp'=8,'seq'=4] {'dp','seq'}, use_global_device_ids=true, to_apply=%region_52.55.clone | all-reduce | flops 6144 | bytes 49152
  971.2 61.3 %reduce-scatter.23.cloned.1.call-done = f32[24,768]{1,0:T(8,128)} async-done(((f32[768,768]{1,0:T(8,128)}), f32[24,768]{1,0:T(8,128)}) %reduce-scatter.23.cloned.1.call-update) | async-done | bytes 73744 | tf_op jit(solution)/shard_map/reduce_scatter | solution.py:401
  1034.4 139.2 %reduce-scatter.19.cloned.1.call-done = f32[1,24,3072]{2,1,0:T(8,128)} async-done(((f32[1,768,3072]{2,1,0:T(8,128)}), f32[1,24,3072]{2,1,0:T(8,128)}) %reduce-scatter.19.cloned.1.call-update) | async-done | bytes 294928 | tf_op jit(solution)/shard_map/reduce_scatter | solution.py:404
  1175.2 139.5 %reduce-scatter.21.cloned.1.call-done = f32[1,96,768]{2,1,0:T(8,128)} async-done(((f32[1,3072,768]{2,1,0:T(8,128)}), f32[1,96,768]{2,1,0:T(8,128)}) %reduce-scatter.21.cloned.1.call-update) | async-done | bytes 294928 | tf_op jit(solution)/shard_map/reduce_scatter | solution.py:405
  1316.5 122.4 %reduce-scatter.15.cloned.1.call-done = f32[1,24,2304]{2,1,0:T(8,128)} async-done(((f32[1,768,2304]{2,1,0:T(8,128)}), f32[1,24,2304]{2,1,0:T(8,128)}) %reduce-scatter.15.cloned.1.call-update) | async-done | bytes 221200 | tf_op jit(solution)/shard_map/reduce_scatter | solution.py:402
  1444.9 40.0 %all-reduce.2 = (f32[]{:T(128)}, f32[]{:T(128)}) all-reduce(f32[]{:T(128)S(6)} %add.338, f32[]{:T(128)} %get-tuple-element.163), channel_id=1, replica_groups=mesh['dp'=8,'seq'=4] {'dp','seq'}, use_global_device_ids=true, to_apply=%region_54.57 | all-reduce | flops 2 | bytes 16 | tf_op jit(solution)/shard_map/psum | solution.py:410
  (271 shorter events, 154.0 us)
Async XLA Ops:
  7.2 61.0 %all-gather.10.cloned.1.call-start = ((), (), s32[]{:S(2)}) async-start(), calls=%async_computation.7 | async-start | bytes 1216512 | tf_op jit(solution)/shard_map/all_gather | solution.py:335
  8.8 121.8 %all-gather.12.cloned.1.call-start = ((), (), s32[]{:S(2)}) async-start(), calls=%async_computation.8 | async-start | bytes 3649536 | tf_op jit(solution)/shard_map/all_gather | solution.py:336
  10.5 181.6 %all-gather.24.cloned.1.call-start = ((), (), s32[]{:S(2)}) async-start(), calls=%async_computation.14 | async-start | bytes 3244032 | tf_op jit(solution)/shard_map/all_gather | solution.py:340
  12.3 208.5 %all-gather.16.cloned.1.call-start = ((), (), s32[]{:S(2)}) async-start(), calls=%async_computation.10 | async-start | bytes 3932160 | tf_op jit(solution)/shard_map/all_gather | solution.py:82
  59.0 71.6 %copy-start.32 = (f32[768]{0:T(1024)}, f32[768]{0:T(1024)S(1)}, u32[]{:S(2)}) copy-start(f32[768]{0:T(1024)S(1)} %get-tuple-element.138) | copy-start | bytes 9220
  59.0 71.6 %copy-start.38 = (f32[768]{0:T(1024)}, f32[768]{0:T(1024)S(1)}, u32[]{:S(2)}) copy-start(f32[768]{0:T(1024)S(1)} %get-tuple-element.137) | copy-start | bytes 9220
  70.4 237.6 %copy-start.2 = (f32[2,256,768]{2,1,0:T(8,128)}, f32[2,256,768]{2,1,0:T(8,128)S(1)}, u32[]{:S(2)}) copy-start(f32[2,256,768]{2,1,0:T(8,128)S(1)} %get-tuple-element.195) | copy-start | bytes 4718596
  136.3 114.4 %all-gather.14.cloned.1.call-start = ((), (), s32[]{:S(2)}) async-start(), calls=%async_computation.9 | async-start | bytes 3932160 | tf_op jit(solution)/shard_map/all_gather | solution.py:83
  136.9 171.1 %all-gather.18.cloned.1.call-start = ((), (), s32[]{:S(2)}) async-start(), calls=%async_computation.11 | async-start | bytes 1216512 | tf_op jit(solution)/shard_map/all_gather | solution.py:337
  137.6 236.4 %all-gather.20.cloned.1.call-start = ((), (), s32[]{:S(2)}) async-start(), calls=%async_computation.12 | async-start | bytes 4866048 | tf_op jit(solution)/shard_map/all_gather | solution.py:338
  138.4 301.1 %all-gather.22.cloned.1.call-start = ((), (), s32[]{:S(2)}) async-start(), calls=%async_computation.13 | async-start | bytes 4866048 | tf_op jit(solution)/shard_map/all_gather | solution.py:339
  139.2 518.3 %reduce-scatter.13.cloned.1.call-start = ((), (), s32[]{:S(2)}) async-start(), calls=%async_computation.16 | async-start | bytes 3932160 | tf_op jit(solution)/shard_map/reduce_scatter | solution.py:182
  578.8 83.5 %reduce-scatter.11.cloned.1.call-start = ((), (), s32[]{:S(2)}) async-start(), calls=%async_computation.15 | async-start | bytes 3932160 | tf_op jit(solution)/shard_map/reduce_scatter | solution.py:179
  626.0 198.1 %all-reduce.5.cloned.1.call-start = ((), (), s32[]{:S(2)}) async-start(), calls=%async_computation.22 | async-start | bytes 12582912
  643.3 285.4 %reduce-scatter.17.cloned.1.call-start = ((), (), s32[]{:S(2)}) async-start(), calls=%async_computation.18 | async-start | bytes 2433024 | tf_op jit(solution)/shard_map/reduce_scatter | solution.py:403
  646.6 385.9 %reduce-scatter.23.cloned.1.call-start = ((), (), s32[]{:S(2)}) async-start(), calls=%async_computation.21 | async-start | bytes 2433024 | tf_op jit(solution)/shard_map/reduce_scatter | solution.py:401
  676.2 497.3 %reduce-scatter.19.cloned.1.call-start = ((), (), s32[]{:S(2)}) async-start(), calls=%async_computation.19 | async-start | bytes 9732096 | tf_op jit(solution)/shard_map/reduce_scatter | solution.py:404
  685.4 629.3 %reduce-scatter.21.cloned.1.call-start = ((), (), s32[]{:S(2)}) async-start(), calls=%async_computation.20 | async-start | bytes 9732096 | tf_op jit(solution)/shard_map/reduce_scatter | solution.py:405
  694.3 744.5 %reduce-scatter.15.cloned.1.call-start = ((), (), s32[]{:S(2)}) async-start(), calls=%async_computation.17 | async-start | bytes 7299072 | tf_op jit(solution)/shard_map/reduce_scatter | solution.py:402
  702.0 784.4 %copy-start.50 = (f32[8,24]{1,0:T(8,128)S(1)}, f32[8,24]{1,0:T(8,128)}, u32[]{:S(2)}) copy-start(f32[8,24]{1,0:T(8,128)} %param.52) | copy-start | bytes 2308
  702.0 784.4 %copy-start.51 = (f32[8,24]{1,0:T(8,128)S(1)}, f32[8,24]{1,0:T(8,128)}, u32[]{:S(2)}) copy-start(f32[8,24]{1,0:T(8,128)} %param.51) | copy-start | bytes 2308
  702.0 785.1 %copy-start.25 = (f32[2,24,1000]{2,1,0:T(8,128)S(1)}, f32[2,24,1000]{2,1,0:T(8,128)}, u32[]{:S(2)}) copy-start(f32[2,24,1000]{2,1,0:T(8,128)} %param.47) | copy-start | bytes 576004
  702.0 787.0 %copy-start.30 = (f32[1,24,768]{2,1,0:T(8,128)S(1)}, f32[1,24,768]{2,1,0:T(8,128)}, u32[]{:S(2)}) copy-start(f32[1,24,768]{2,1,0:T(8,128)} %param.38) | copy-start | bytes 221188
  702.0 788.7 %copy-start.31 = (f32[24,768]{1,0:T(8,128)S(1)}, f32[24,768]{1,0:T(8,128)}, u32[]{:S(2)}) copy-start(f32[24,768]{1,0:T(8,128)} %param.32) | copy-start | bytes 221188
  702.0 790.3 %copy-start.24 = (f32[1,24,2304]{2,1,0:T(8,128)S(1)}, f32[1,24,2304]{2,1,0:T(8,128)}, u32[]{:S(2)}) copy-start(f32[1,24,2304]{2,1,0:T(8,128)} %param.35) | copy-start | bytes 663556
  702.1 792.3 %copy-start.18 = (f32[1,96,768]{2,1,0:T(8,128)S(1)}, f32[1,96,768]{2,1,0:T(8,128)}, u32[]{:S(2)}) copy-start(f32[1,96,768]{2,1,0:T(8,128)} %param.44) | copy-start | bytes 884740
  702.1 792.3 %copy-start.26 = (f32[1,96,768]{2,1,0:T(8,128)S(1)}, f32[1,96,768]{2,1,0:T(8,128)}, u32[]{:S(2)}) copy-start(f32[1,96,768]{2,1,0:T(8,128)} %param.45) | copy-start | bytes 884740
  702.1 792.3 %copy-start.27 = (f32[1,96,768]{2,1,0:T(8,128)S(1)}, f32[1,96,768]{2,1,0:T(8,128)}, u32[]{:S(2)}) copy-start(f32[1,96,768]{2,1,0:T(8,128)} %param.46) | copy-start | bytes 884740
  1032.5 458.2 %copy-start.28 = (f32[24,768]{1,0:T(8,128)S(1)}, f32[24,768]{1,0:T(8,128)}, u32[]{:S(2)}) copy-start(f32[24,768]{1,0:T(8,128)} %reduce-scatter.23.cloned.1.call-done) | copy-start | bytes 221188
  1314.7 179.7 %copy-start.22 = (f32[1,96,768]{2,1,0:T(8,128)S(1)}, f32[1,96,768]{2,1,0:T(8,128)}, u32[]{:S(2)}) copy-start(f32[1,96,768]{2,1,0:T(8,128)} %reduce-scatter.21.cloned.1.call-done) | copy-start | bytes 884740
  1316.4 179.0 %copy-start.20 = (f32[1,24,3072]{2,1,0:T(8,128)S(1)}, f32[1,24,3072]{2,1,0:T(8,128)}, u32[]{:S(2)}) copy-start(f32[1,24,3072]{2,1,0:T(8,128)} %param.41) | copy-start | bytes 884740
  1316.4 179.0 %copy-start.21 = (f32[1,24,3072]{2,1,0:T(8,128)S(1)}, f32[1,24,3072]{2,1,0:T(8,128)}, u32[]{:S(2)}) copy-start(f32[1,24,3072]{2,1,0:T(8,128)} %reduce-scatter.19.cloned.1.call-done) | copy-start | bytes 884740
  (39 other events, 468.5 us)
Sparse Core Ops, SparseCore 0:
  11.5 56.6 all-gather.9
  71.7 58.9 all-gather.11
  134.1 57.9 all-gather.23
  193.5 27.2 all-gather.15
  222.2 28.4 all-gather.13
  254.1 53.9 all-gather.17
  311.5 62.4 all-gather.19
  377.5 61.9 all-gather.21
  578.9 36.1 reduce-scatter.12
  626.1 36.1 reduce-scatter.10
  668.0 156.0 all-reduce.4
  829.2 99.3 reduce-scatter.16
  933.9 98.5 reduce-scatter.22
  1038.3 135.2 reduce-scatter.18
  1179.3 135.3 reduce-scatter.20
  1320.3 118.5 reduce-scatter.14
where the time goes:
time: 1510 us
  waiting for transfers between devices  955 us (63%)
  local copies, waits for them, and re-layouts  167 us (11%)
  matrix products  154 us (10%)
  blocking collectives  124 us (8%)
  other arithmetic  81.9 us (5%)
  between operations  23.5 us (2%)
    reduce_scatter x1, waiting for transfers between devices, on_device(): lax.psum_scatter(grad_shrink, ('dp', 'seq'), scatter_dimension=1, tiled=T...  140 us
    reduce_scatter x1, waiting for transfers between devices, on_device(): lax.psum_scatter(grad_expand, ('dp', 'seq'), scatter_dimension=1, tiled=T...  139 us
    unnamed x17, waiting for transfers between devices  123 us
    reduce_scatter x1, waiting for transfers between devices, on_device(): lax.psum_scatter(grad_attend, ('dp', 'seq'), scatter_dimension=1, tiled=T...  122 us
    reduce_scatter x1, waiting for transfers between devices, on_device(): lax.psum_scatter(grad_merger, ('dp', 'seq'), scatter_dimension=1, tiled=T...  103 us
    gather x6, local copies, waits for them, and re-layouts, pick(): jnp.take_along_axis(x, jnp.broadcast_to(clamped[..., None], clamped.shape...  88.2 us
    all_gather x1, waiting for transfers between devices, on_device(): lax.all_gather(expand.astype(jnp.bfloat16), ('dp', 'seq'), axis=1, tiled=...  62.1 us
    reduce_scatter x1, waiting for transfers between devices, on_device(): lax.psum_scatter(grad_embed, ('dp', 'seq'), scatter_dimension=0, tiled=True)  61.3 us
  transfers between devices with their start and end apart: 16, of which 15 were waited for; matrix products, arithmetic and copies ran while one was open for 16% of the time, Pallas kernels for 0%

commit v1 on v0

v1 whole, which is shorter than its diff:
```python
from functools import partial

import jax
import jax.numpy as jnp
from jax import lax
from jax.experimental import pallas as pl
from jax.experimental.pallas import tpu as pltpu
from jax.sharding import PartitionSpec as P

HEADS = 12
HD = 64
L = 1
IMGS = 3
STEP_COUNT = 7

NORM_EPS = 1e-06
MASKED = -1000000000.0
SCALE = 0.125
BETA_ONE = 0.9
BETA_TWO = 0.999
ADAM_EPS = 1e-08
DECAY = 0.05
BASE_RATE = 0.05
LAYER_RATE = 0.75
CLIP_AT = 0.05
HIGH = lax.Precision.HIGHEST
BF = jnp.bfloat16
F32 = jnp.float32
AXES = ("dp", "seq")
PANEL = 768
RATES = (LAYER_RATE ** (L + 1), LAYER_RATE, LAYER_RATE, LAYER_RATE, LAYER_RATE, 1.0)


def pairs(dp_size, seq_size, move):
    return [
        (d * seq_size + s, move(d, s)[0] * seq_size + move(d, s)[1])
        for d in range(dp_size)
        for s in range(seq_size)
    ]


def exchange(value, move):
    return lax.ppermute(value, AXES, pairs(lax.axis_size("dp"), lax.axis_size("seq"), move))


def along_z(step):
    return lambda d, s: (d ^ (2 * step), s)


def across_core(d, s):
    return (d, s ^ 1)


def across_first(d, s):
    return (d ^ 1, s) if s % 2 == 0 else (d, s ^ 2)


def across_second(d, s):
    return (d, s ^ 2) if s % 2 == 0 else (d ^ 1, s)


def spot():
    dp, seq = lax.axis_index("dp"), lax.axis_index("seq")
    return (dp // 2, dp % 2, seq // 2, seq % 2)


def total_of(value):
    for bit in range((lax.axis_size("seq") - 1).bit_length()):
        value = value + exchange(value, lambda d, s, bit=bit: (d, s ^ (1 << bit)))
    for bit in range((lax.axis_size("dp") - 1).bit_length()):
        value = value + exchange(value, lambda d, s, bit=bit: (d ^ (1 << bit), s))
    return value


def assemble(pieces, places, z, plan, shapes):
    count, outs = len(pieces), len(shapes)
    leads = [len(s) - 6 for s in shapes]

    def body(where, *refs):
        ins, out_refs = refs[:count], refs[count:]
        for i in range(count):
            x, y, c = where[3 * i + 1], where[3 * i + 2], where[3 * i + 3]
            for row, rows, o, lead, lo, hi, at in plan:
                out_refs[o][lead + (0, x, y, c, slice(None), slice(at, at + hi - lo))] = ins[i][
                    0, row : row + rows, lo:hi
                ]

    def out_spec(shape, lead):
        block = shape[:lead] + (1,) + shape[lead + 1 :]
        rest = len(shape) - lead - 1
        return pl.BlockSpec(block, lambda j, where: (0,) * lead + (where[0] ^ j,) + (0,) * rest)

    slab = (1,) + pieces[0].shape[1:]
    return pl.pallas_call(
        body,
        out_shape=[jax.ShapeDtypeStruct(s, BF) for s in shapes],
        grid_spec=pltpu.PrefetchScalarGridSpec(
            num_scalar_prefetch=1,
            grid=(pieces[0].shape[0],),
            in_specs=[pl.BlockSpec(slab, lambda j, where: (j, 0, 0))] * count,
            out_specs=[out_spec(s, n) for s, n in zip(shapes, leads)],
        ),
        name="assemble",
    )(jnp.concatenate([jnp.stack([z]), places]).astype(jnp.int32), *pieces)


def gather_group(packed, plan, shapes):
    z, x, y, c = spot()
    depth = lax.axis_size("dp") // 2
    parts = [packed] + [exchange(packed, along_z(j)) for j in range(1, depth)]
    own = jnp.stack(parts)
    near = exchange(own, across_first)
    side = exchange(own, across_second)
    far = exchange(near, across_second)
    pieces = [own, near, side, far]
    pieces = pieces + [exchange(p, across_core) for p in pieces]
    one = jnp.int32(1)
    places = []
    for k in (c, 1 - c):
        fx, fy = 1 - k, k
        places += [x, y, k, x ^ fx, y ^ fy, k, x ^ fy, y ^ fx, k, x ^ one, y ^ one, k]
    places = jnp.stack(places).astype(jnp.int32)
    return assemble(pieces, places, z, plan, shapes)


def at(value, index, axis):
    return lax.dynamic_index_in_dim(value, index, axis, keepdims=False)


def scatter_group(panels):
    z, x, y, c = spot()
    depth = lax.axis_size("dp") // 2
    first = c == 0

    def pick_core(k):
        return jnp.concatenate([at(p, k, 3) for p in panels], 3)

    got = exchange(pick_core(1 - c), across_core)
    total = pick_core(c).astype(F32) + got.astype(F32)
    give = jnp.where(first, at(total, 1 - y, 2), at(total, 1 - x, 1)).astype(BF)
    keep = jnp.where(first, at(total, y, 2), at(total, x, 1))
    total = keep + exchange(give, across_second).astype(F32)
    here = jnp.where(first, x, y)
    give = at(total, 1 - here, 1).astype(BF)
    total = at(total, here, 1) + exchange(give, across_first).astype(F32)
    result = at(total, z, 0)
    for j in range(1, depth):
        result = result + exchange(at(total, z ^ j, 0).astype(BF), along_z(j)).astype(F32)
    return result


def blocks(grad):
    shards = lax.axis_size("dp") * lax.axis_size("seq")
    return grad.reshape(shards // 8, 2, 2, 2, grad.shape[0] // shards, PANEL)


def attend_forward(q_ref, k_ref, v_ref, sq_ref, sk_ref, out_ref, lse_ref):
    step = 256 if q_ref.shape[0] % 256 == 0 else q_ref.shape[0]
    lane = lax.broadcasted_iota(jnp.int32, (1, 2 * HD), 1)
    keys, values = k_ref[...], v_ref[...]
    seg_keys = sk_ref[...]
    for start in range(0, q_ref.shape[0], step):
        rows = slice(start, start + step)
        query = q_ref[rows, :] * jnp.asarray(SCALE, BF)
        same = seg_keys == sq_ref[:, rows]
        mixed = None
        for h in range(2):
            mine = (lane // HD) == h
            raw = lax.dot_general(
                keys,
                jnp.where(mine, query, jnp.zeros_like(query)),
                (((1,), (1,)), ((), ())),
                preferred_element_type=F32,
            )
            raw = jnp.where(same, raw, MASKED)
            top = jnp.max(raw, 0, keepdims=True)
            heavy = jnp.exp(raw - top)
            mass = jnp.sum(heavy, 0, keepdims=True)
            shares = (heavy * (1.0 / mass)).astype(BF)
            part = lax.dot_general(
                jnp.where(mine, values, jnp.zeros_like(values)),
                shares,
                (((0,), (0,)), ((), ())),
                preferred_element_type=F32,
            )
            mixed = part if mixed is None else mixed + part
            lse_ref[0, h : h + 1, rows] = top + jnp.log(mass)
        out_ref[rows, :] = mixed.T.astype(BF)


def attend_backward(
    q_ref, k_ref, v_ref, do_ref, lse_ref, sq_ref, sk_ref, dq_ref, dk_ref, dv_ref
):
    step = 256 if q_ref.shape[0] % 256 == 0 else q_ref.shape[0]
    lane = lax.broadcasted_iota(jnp.int32, (1, 2 * HD), 1)
    keys, values = k_ref[...], v_ref[...]
    seg_keys = sk_ref[...]
    for start in range(0, q_ref.shape[0], step):
        rows = slice(start, start + step)
        query = q_ref[rows, :] * jnp.asarray(SCALE, BF)
        grad = do_ref[rows, :]
        same = seg_keys == sq_ref[:, rows]
        grad_query = None
        grad_keys = None
        grad_values = None
        for h in range(2):
            mine = (lane // HD) == h
            query_h = jnp.where(mine, query, jnp.zeros_like(query))
            grad_h = jnp.where(mine, grad, jnp.zeros_like(grad))
            raw = lax.dot_general(
                keys, query_h, (((1,), (1,)), ((), ())), preferred_element_type=F32
            )
            shares = jnp.exp(jnp.where(same, raw, MASKED) - lse_ref[0, h : h + 1, rows])
            grad_shares = lax.dot_general(
                values, grad_h, (((1,), (1,)), ((), ())), preferred_element_type=F32
            )
            spread = jnp.sum(grad_shares * shares, 0, keepdims=True)
            grad_raw = (shares * (grad_shares - spread)).astype(BF)
            part = lax.dot_general(
                jnp.where(mine, keys, jnp.zeros_like(keys)),
                grad_raw,
                (((0,), (0,)), ((), ())),
                preferred_element_type=F32,
            )
            part_k = jnp.dot(grad_raw, query_h, preferred_element_type=F32)
            part_v = jnp.dot(shares.astype(BF), grad_h, preferred_element_type=F32)
            grad_query = part if grad_query is None else grad_query + part
            grad_keys = part_k if grad_keys is None else grad_keys + part_k
            grad_values = part_v if grad_values is None else grad_values + part_v
        dq_ref[rows, :] = (grad_query.T * SCALE).astype(BF)
        if start == 0:
            dk_ref[...] = grad_keys
            dv_ref[...] = grad_values
        else:
            dk_ref[...] += grad_keys
            dv_ref[...] += grad_values


def head_pair(rows):
    return pl.BlockSpec((rows, 2 * HD), lambda i: (0, i))


def whole(shape):
    return pl.BlockSpec(shape, lambda i: (0,) * len(shape))


def mix_tokens(query, keys, values, seg_q, seg_k):
    nq, nk = query.shape[0], keys.shape[0]
    return pl.pallas_call(
        attend_forward,
        grid=(HEADS // 2,),
        in_specs=[head_pair(nq), head_pair(nk), head_pair(nk), whole((1, nq)), whole((nk, 1))],
        out_specs=[head_pair(nq), pl.BlockSpec((1, 2, nq), lambda i: (i, 0, 0))],
        out_shape=[
            jax.ShapeDtypeStruct((nq, HEADS * HD), BF),
            jax.ShapeDtypeStruct((HEADS // 2, 2, nq), F32),
        ],
        name="attend_forward",
    )(query, keys, values, seg_q, seg_k)


def mix_back(query, keys, values, grad, lse, seg_q, seg_k):
    nq, nk = query.shape[0], keys.shape[0]
    return pl.pallas_call(
        attend_backward,
        grid=(HEADS // 2,),
        in_specs=[
            head_pair(nq),
            head_pair(nk),
            head_pair(nk),
            head_pair(nq),
            pl.BlockSpec((1, 2, nq), lambda i: (i, 0, 0)),
            whole((1, nq)),
            whole((nk, 1)),
        ],
        out_specs=[head_pair(nq), head_pair(nk), head_pair(nk)],
        out_shape=[
            jax.ShapeDtypeStruct((nq, HEADS * HD), BF),
            jax.ShapeDtypeStruct((nk, HEADS * HD), F32),
            jax.ShapeDtypeStruct((nk, HEADS * HD), F32),
        ],
        name="attend_backward",
    )(query, keys, values, grad, lse, seg_q, seg_k)


def norm_parts(x):
    centre = x - jnp.mean(x, -1, keepdims=True)
    rate = lax.rsqrt(jnp.mean(centre * centre, -1, keepdims=True) + NORM_EPS)
    return (centre * rate, rate)


def layer_norm(x, gain, shift):
    return norm_parts(x)[0] * gain + shift


def norm_back(x, gain, grad):
    unit, rate = norm_parts(x)
    inner_grad = grad * gain
    back = rate * (
        inner_grad
        - jnp.mean(inner_grad, -1, keepdims=True)
        - unit * jnp.mean(inner_grad * unit, -1, keepdims=True)
    )
    return (back, jnp.sum(grad * unit, 0), jnp.sum(grad, 0))


def matmul(left, right):
    return jnp.dot(left, right, preferred_element_type=F32)


def outer(left, right):
    return lax.dot_general(left, right, (((0,), (0,)), ((), ())), preferred_element_type=F32)


def inner(grad, weight):
    return lax.dot_general(grad, weight, (((1,), (1,)), ((), ())), preferred_element_type=F32)


def row_swap(seq_size):
    return [(s, s ^ (seq_size // 2)) for s in range(seq_size)]


def rel_bits(seq_size):
    return [1 << b for b in range((seq_size // 2 - 1).bit_length())]


def share_rows(value):
    size = lax.axis_size("seq")
    for bit in rel_bits(size):
        other = lax.ppermute(value, "seq", [(s, s ^ bit) for s in range(size)])
        value = jnp.concatenate([value, other], 0)
    return value


def return_rows(value):
    size = lax.axis_size("seq")
    for bit in reversed(rel_bits(size)):
        half = value.shape[0] // 2
        other = lax.ppermute(value[half:].astype(BF), "seq", [(s, s ^ bit) for s in range(size)])
        value = value[:half] + other.astype(F32)
    return value


def head_terms(rows, inside, readout_w, gain, shift, target, classes, image_count):
    unit, rate = norm_parts(rows)
    low = (unit * gain + shift).astype(BF)
    logits = matmul(low, readout_w)[:, :classes]
    log_share = jax.nn.log_softmax(logits, -1)
    grad = 0.5 * (jnp.exp(log_share) - target) * (inside / image_count)[:, None]
    grad = jnp.pad(grad, ((0, 0), (0, readout_w.shape[1] - classes)))
    grad_readout = lax.dot_general(
        low.astype(F32), grad, (((0,), (0,)), ((), ())), precision=HIGH
    )
    grad_norm = lax.dot_general(
        grad, readout_w.astype(F32), (((1,), (1,)), ((), ())), precision=HIGH
    )
    back, gain_grad, shift_grad = norm_back(rows, gain, grad_norm)
    return (log_share, grad_readout, back, gain_grad, shift_grad)


def adamw(weight, mean, square, grad, scale, decay):
    mean_next = BETA_ONE * mean + (1.0 - BETA_ONE) * grad
    square_next = BETA_TWO * square + (1.0 - BETA_TWO) * grad * grad
    mean_hat = mean_next / (1.0 - BETA_ONE**STEP_COUNT)
    square_hat = square_next / (1.0 - BETA_TWO**STEP_COUNT)
    weight_next = weight - BASE_RATE * scale * (
        mean_hat / (jnp.sqrt(square_hat) + ADAM_EPS) + decay * weight
    )
    return (weight_next, mean_next, square_next)


def moments(mean, square, grad):
    return (
        BETA_ONE * mean + (1.0 - BETA_ONE) * grad,
        BETA_TWO * square + (1.0 - BETA_TWO) * grad * grad,
    )


def side_by_side(shard):
    return [shard[:, k : k + PANEL] for k in range(0, shard.shape[1], PANEL)]


def gather_weights(embedder, attend, merger, expand, shrink, readout, vectors, fast):
    low = [w.astype(BF) for w in (embedder, attend, merger, expand, shrink, readout, vectors)]
    if not fast:
        full = [
            lax.all_gather(w, AXES, axis=0 if n == 0 else 1, tiled=True) for n, w in enumerate(low)
        ]
        return (full[0], full[1][0], full[2][0], full[3][0], full[4][0], full[5], full[6])
    embedder, attend, merger, expand, shrink, readout, vectors = low
    depth = lax.axis_size("dp") // 2
    front = (depth, 2, 2, 2)
    rows, long = embedder.shape[0], shrink.shape[1]
    tall = vectors.shape[0]
    width = PANEL * (-(-readout.shape[2] // 256) * 256 // PANEL) + 256
    readout = jnp.pad(readout, ((0, 0), (0, 0), (0, width - readout.shape[2])))

    wide = jnp.pad(vectors, ((0, 0), (0, PANEL - vectors.shape[1])))
    pack = jnp.concatenate([wide, embedder] + side_by_side(attend[0]), 0)
    plan = [(0, tall, 0, (), 0, 128, 0), (tall, rows, 1, (), 0, PANEL, 0)]
    plan += [(tall + rows * (n + 1), rows, 2, (), 0, PANEL, PANEL * n) for n in range(3)]
    vec, emb, att = gather_group(
        pack, plan, [front + (tall, 128), front + (rows, PANEL), front + (rows, attend.shape[2])]
    )
    vec = vec.reshape(-1, tall, 128)[:, :, : vectors.shape[1]].transpose(1, 0, 2)

    count = expand.shape[2] // PANEL
    pack = jnp.concatenate([merger[0]] + side_by_side(expand[0]), 0)
    plan = [(0, rows, 0, (), 0, PANEL, 0)]
    plan += [(rows * (n + 1), rows, 1, (), 0, PANEL, PANEL * n) for n in range(count)]
    mer, exp = gather_group(
        pack, plan, [front + (rows, PANEL), front + (rows, expand.shape[2])]
    )

    rest = jnp.concatenate([readout[0][:, PANEL:], readout[1][:, PANEL:]], 1)
    rest = jnp.pad(rest, ((0, 0), (0, PANEL - rest.shape[1])))
    pack = jnp.concatenate([shrink[0], readout[0][:, :PANEL], readout[1][:, :PANEL], rest], 0)
    plan = [(0, long, 0, (), 0, PANEL, 0)]
    for head in range(2):
        plan += [
            (long + rows * head, rows, 1, (head,), 0, PANEL, 0),
            (long + rows * 2, rows, 1, (head,), 256 * head, 256 * head + 256, PANEL),
        ]
    shr, rea = gather_group(pack, plan, [front + (long, PANEL), (2,) + front + (rows, width)])
    return (
        emb.reshape(-1, PANEL),
        att.reshape(-1, attend.shape[2]),
        mer.reshape(-1, PANEL),
        exp.reshape(-1, expand.shape[2]),
        shr.reshape(-1, PANEL),
        rea.reshape(2, -1, width),
        vec.reshape(tall, -1),
    )


def scatter_early(merger, expand, shrink, readout, classes, fast):
    if not fast:
        reduced = [
            lax.psum_scatter(g.astype(BF), AXES, scatter_dimension=n, tiled=True).astype(F32)
            for g, n in ((merger, 0), (expand, 0), (shrink, 0), (readout, 1))
        ]
        return (reduced[0], reduced[1], reduced[2], reduced[3][:, :, :classes])
    merger, expand, shrink, readout = [g.astype(BF) for g in (merger, expand, shrink, readout)]
    rest = jnp.concatenate([readout[0][:, PANEL:], readout[1][:, PANEL:]], 1)
    rest = jnp.pad(rest, ((0, 0), (0, PANEL - rest.shape[1])))
    panels = [merger] + side_by_side(expand) + [shrink]
    panels += [readout[0][:, :PANEL], readout[1][:, :PANEL], rest]
    mine = scatter_group([blocks(p) for p in panels])
    parts, row = [], 0
    for p in panels:
        count = p.shape[0] // (lax.axis_size("dp") * lax.axis_size("seq"))
        parts.append(mine[row : row + count])
        row += count
    count = len(parts) - 5
    tails = [parts[-1][:, :256], parts[-1][:, 256:512]]
    reads = [jnp.concatenate([parts[-3 + n], tails[n]], 1)[:, :classes] for n in range(2)]
    return (parts[0], jnp.concatenate(parts[1 : 1 + count], 1), parts[-4], jnp.stack(reads))


def scatter_late(embedder, attend, vectors, fast):
    shards = lax.axis_size("dp") * lax.axis_size("seq")
    if not fast:
        return tuple(
            lax.psum_scatter(g.astype(BF), AXES, scatter_dimension=n, tiled=True).astype(F32)
            for g, n in ((embedder, 0), (attend, 0), (vectors, 1))
        )
    tall, width = vectors.shape[0], vectors.shape[1] // shards
    wide = vectors.astype(BF).reshape(tall, shards, width).transpose(1, 0, 2)
    wide = jnp.pad(wide, ((0, 0), (0, 0), (0, PANEL - width)))
    panels = [wide.reshape(-1, PANEL), embedder.astype(BF)] + side_by_side(attend.astype(BF))
    mine = scatter_group([blocks(p) for p in panels])
    rows = embedder.shape[0] // shards
    parts = [mine[tall + rows * n : tall + rows * (n + 1)] for n in range(4)]
    return (parts[0], jnp.concatenate(parts[1:], 1), mine[:tall, :width])


def on_device(
    pixels,
    lengths,
    labels,
    teacher,
    embedder,
    embedder_mean,
    embedder_square,
    attend,
    attend_mean,
    attend_square,
    merger,
    merger_mean,
    merger_square,
    expand,
    expand_mean,
    expand_square,
    shrink,
    shrink_mean,
    shrink_square,
    readout,
    readout_mean,
    readout_square,
    vectors,
    vectors_mean,
    vectors_square,
):
    seq_size, dp_size = lax.axis_size("seq"), lax.axis_size("dp")
    fast = seq_size == 4 and dp_size % 2 == 0 and embedder.shape[0] % 8 == 0
    seq = lax.axis_index("seq")
    local = pixels.shape[1]
    classes = readout.shape[2]
    image_count = lengths.shape[0] * dp_size * IMGS

    side = seq // (seq_size // 2)
    pixels_mine = lax.dynamic_index_in_dim(pixels, side, 0, False)
    pixels_give = lax.dynamic_index_in_dim(pixels, 1 - side, 0, False)
    pixels_got = lax.ppermute(pixels_give, "seq", row_swap(seq_size))
    tokens = jnp.concatenate([pixels_mine, pixels_got], 0)
    row_lengths = lax.dynamic_index_in_dim(lengths, side, 0, False)
    row_labels = lax.dynamic_index_in_dim(labels, side, 0, False)
    row_teacher = lax.dynamic_index_in_dim(teacher, side, 0, False)

    def places_of(where):
        span = jnp.arange(local, dtype=jnp.int32)
        return jnp.concatenate([where * local + span, (where ^ (seq_size // 2)) * local + span])

    places = places_of(seq)
    all_places = jnp.concatenate([places_of(seq ^ j) for j in range(seq_size // 2)])
    ends = jnp.cumsum(row_lengths)
    starts = ends - row_lengths
    seg_q = jnp.sum((places[:, None] >= ends[None, :]).astype(jnp.int32), 1)
    seg_k = jnp.sum((all_places[:, None] >= ends[None, :]).astype(jnp.int32), 1)
    class_hit = (starts[:, None] == places[None, :]).astype(F32)
    distill_hit = (starts[:, None] + 1 == places[None, :]).astype(F32)
    is_cls, is_dist = jnp.sum(class_hit, 0), jnp.sum(distill_hit, 0)
    is_patch = (seg_q < IMGS).astype(F32) - is_cls - is_dist

    embed_w, attend_w, merger_w, expand_w, shrink_w, readout_w, vector_w = gather_weights(
        embedder, attend, merger, expand, shrink, readout, vectors, fast
    )
    vector_f = vector_w.astype(F32)

    patches = matmul(tokens, embed_w)
    x = (
        is_patch[:, None] * patches
        + is_cls[:, None] * vector_f[4 * L + 2]
        + is_dist[:, None] * vector_f[4 * L + 3]
    )
    a = layer_norm(x, vector_f[0], vector_f[1]).astype(BF)
    projected = matmul(a, attend_w).astype(BF)
    query = projected[:, :PANEL]
    shared = share_rows(projected[:, PANEL:])
    keys, values = shared[:, :PANEL], shared[:, PANEL:]
    mixed, lse = mix_tokens(query, keys, values, seg_q[None, :], seg_k[:, None])
    x_mid = x + matmul(mixed, merger_w)
    normed = layer_norm(x_mid, vector_f[2], vector_f[3]).astype(BF)
    hidden_in = matmul(normed, expand_w)
    cdf = 0.5 * (1.0 + lax.erf(hidden_in * (0.5**0.5)))
    hidden = (hidden_in * cdf).astype(BF)
    slope = cdf + hidden_in * jnp.exp(-0.5 * hidden_in * hidden_in) * ((0.5 / jnp.pi) ** 0.5)
    x_last = x_mid + matmul(hidden, shrink_w)

    class_in, distill_in = jnp.sum(class_hit, 1), jnp.sum(distill_hit, 1)
    class_rows = jnp.dot(class_hit, x_last, precision=HIGH)
    distill_rows = jnp.dot(distill_hit, x_last, precision=HIGH)
    label_hot = (row_labels[:, None] == jnp.arange(classes, dtype=jnp.int32)).astype(F32)
    teach_log = jax.nn.log_softmax(row_teacher, -1)
    teach = jnp.exp(teach_log)
    gain, shift = vector_f[4 * L], vector_f[4 * L + 1]
    class_log, read_a, class_back, gain_a, shift_a = head_terms(
        class_rows, class_in, readout_w[0], gain, shift, label_hot, classes, image_count
    )
    distill_log, read_b, distill_back, gain_b, shift_b = head_terms(
        distill_rows, distill_in, readout_w[1], gain, shift, teach, classes, image_count
    )
    cross = -jnp.sum(class_log * label_hot, -1)
    diverge = jnp.sum(teach * (teach_log - distill_log), -1)
    loss_local = jnp.sum(0.5 * cross * class_in + 0.5 * diverge * distill_in)

    hits = jnp.concatenate([class_hit, distill_hit], 0)
    grad_out = lax.dot_general(
        hits,
        jnp.concatenate([class_back, distill_back], 0),
        (((0,), (0,)), ((), ())),
        precision=HIGH,
    )
    grad_branch = grad_out.astype(BF)
    grad_shrink = outer(hidden, grad_branch)
    grad_pre = (inner(grad_branch, shrink_w) * slope).astype(BF)
    grad_expand = outer(normed, grad_pre)
    grad_normed, gain_two, shift_two = norm_back(x_mid, vector_f[2], inner(grad_pre, expand_w))
    grad_mid = grad_out + grad_normed
    grad_attn = grad_mid.astype(BF)
    grad_merger = outer(mixed, grad_attn)
    early = scatter_early(
        grad_merger, grad_expand, grad_shrink, jnp.stack([read_a, read_b]), classes, fast
    )
    grad_mixed = inner(grad_attn, merger_w).astype(BF)
    grad_query, part_keys, part_values = mix_back(
        query, keys, values, grad_mixed, lse, seg_q[None, :], seg_k[:, None]
    )
    grad_shared = return_rows(jnp.concatenate([part_keys, part_values], 1))
    grad_proj = jnp.concatenate([grad_query, grad_shared.astype(BF)], 1)
    grad_attend = outer(a, grad_proj)
    grad_input, gain_one, shift_one = norm_back(x, vector_f[0], inner(grad_proj, attend_w))
    grad_x = grad_mid + grad_input
    grad_patch = (grad_x * is_patch[:, None]).astype(BF)
    grad_embed = outer(tokens, grad_patch)
    class_token = jnp.sum(grad_x * is_cls[:, None], 0)
    distill_token = jnp.sum(grad_x * is_dist[:, None], 0)
    grad_vectors = jnp.stack(
        [
            gain_one,
            shift_one,
            gain_two,
            shift_two,
            gain_a + gain_b,
            shift_a + shift_b,
            class_token,
            distill_token,
        ]
    )
    late = scatter_late(grad_embed, grad_attend, grad_vectors, fast)
    reduced = (late[0], late[1][None], early[0][None], early[1][None], early[2][None], early[3])
    square_sum = sum((jnp.sum(g * g) for g in reduced)) + jnp.sum(late[2] * late[2])
    both = total_of(jnp.stack([square_sum, loss_local])[None, :])
    grad_norm = jnp.sqrt(both[0, 0])
    factor = jnp.minimum(1.0, CLIP_AT / (grad_norm + 1e-06))

    masters = (embedder, attend, merger, expand, shrink, readout)
    means = (embedder_mean, attend_mean, merger_mean, expand_mean, shrink_mean, readout_mean)
    squares = (
        embedder_square,
        attend_square,
        merger_square,
        expand_square,
        shrink_square,
        readout_square,
    )
    outs = []
    for j in range(6):
        outs += adamw(masters[j], means[j], squares[j], reduced[j] * factor, RATES[j], DECAY)
    outs += moments(vectors_mean, vectors_square, late[2] * factor)
    return tuple(outs) + (both[0, 1] / image_count, grad_norm)


def solution(mesh):
    return jax.shard_map(
        on_device,
        mesh=mesh,
        in_specs=(
            P("dp", "seq", None),
            P("dp", None),
            P("dp", None),
            P("dp", None, None),
            P(("dp", "seq"), None),
            P(("dp", "seq"), None),
            P(("dp", "seq"), None),
            P(None, ("dp", "seq"), None),
            P(None, ("dp", "seq"), None),
            P(None, ("dp", "seq"), None),
            P(None, ("dp", "seq"), None),
            P(None, ("dp", "seq"), None),
            P(None, ("dp", "seq"), None),
            P(None, ("dp", "seq"), None),
            P(None, ("dp", "seq"), None),
            P(None, ("dp", "seq"), None),
            P(None, ("dp", "seq"), None),
            P(None, ("dp", "seq"), None),
            P(None, ("dp", "seq"), None),
            P(None, ("dp", "seq"), None),
            P(None, ("dp", "seq"), None),
            P(None, ("dp", "seq"), None),
            P(None, ("dp", "seq")),
            P(None, ("dp", "seq")),
            P(None, ("dp", "seq")),
        ),
        out_specs=(
            P(("dp", "seq"), None),
            P(("dp", "seq"), None),
            P(("dp", "seq"), None),
            P(None, ("dp", "seq"), None),
            P(None, ("dp", "seq"), None),
            P(None, ("dp", "seq"), None),
            P(None, ("dp", "seq"), None),
            P(None, ("dp", "seq"), None),
            P(None, ("dp", "seq"), None),
            P(None, ("dp", "seq"), None),
            P(None, ("dp", "seq"), None),
            P(None, ("dp", "seq"), None),
            P(None, ("dp", "seq"), None),
            P(None, ("dp", "seq"), None),
            P(None, ("dp", "seq"), None),
            P(None, ("dp", "seq"), None),
            P(None, ("dp", "seq"), None),
            P(None, ("dp", "seq"), None),
            P(None, ("dp", "seq")),
            P(None, ("dp", "seq")),
            P(),
            P(),
        ),
        check_vma=False,
    )
```

time: 1510 us -> 492 us (0.33)
  waiting for transfers between devices: 955 us -> 177 us
  blocking collectives: 124 us -> 0 us
  local copies, waits for them, and re-layouts: 167 us -> 50.4 us
  matrix products: 154 us -> 52.1 us
  Pallas kernels: 0 us -> 61.4 us
  starting transfers between devices: 1.3 us -> 52.4 us
    reduce_scatter x7 -> x0, waiting for transfers between devices: 570 us -> none  [the longest x1 140 us: on_device(): lax.psum_scatter(grad_shrink, ('dp', 'seq'), scatter_dimension=1, tiled=T...]
    all_gather x8 -> x0, waiting for transfers between devices: 263 us -> none  [the longest x1 62.1 us: on_device(): lax.all_gather(expand.astype(jnp.bfloat16), ('dp', 'seq'), axis=1, tiled=...]
    ppermute x0 -> x50, waiting for transfers between devices: none -> 177 us  [the longest x47 173 us: exchange(): lax.ppermute(value, AXES, pairs(lax.axis_size('dp'), lax.axis_size('seq')...]
    unnamed x17 -> x0, waiting for transfers between devices: 123 us -> none
    dot_general x27 -> x23, matrix products: 152 us -> 52.1 us  [the longest x7 18.2 us: matmul(): return jnp.dot(left, right, preferred_element_type=F32)]
    gather x6 -> x0, local copies, waits for them, and re-layouts: 88.2 us -> none  [pick(): jnp.take_along_axis(x, jnp.broadcast_to(clamped[..., None], clamped.shape...]
    pallas_call x0 -> x5, Pallas kernels: none -> 61.4 us  [the longest x1 24.3 us: mix_back(): pl.pallas_call(attend_backward, grid=(HEADS // 2,), in_specs=[head_pair(n...]
    ppermute x0 -> x50, starting transfers between devices: none -> 52.4 us  [the longest x47 51.5 us: exchange(): lax.ppermute(value, AXES, pairs(lax.axis_size('dp'), lax.axis_size('seq')...]
  transfers between devices with their start and end apart: 16 -> 50, of which waited for: 15 -> 21; matrix products, arithmetic and copies ran while one was open for 16% -> 15% of each run, Pallas kernels for 0% -> 9%
where the time goes in v1:
time: 492 us; the launch traced here: 483 us
  waiting for transfers between devices  177 us (36%)
  other arithmetic  79.1 us (16%)
  Pallas kernels  61.4 us (12%)
  starting transfers between devices  52.4 us (11%)
  matrix products  52.1 us (11%)
  local copies, waits for them, and re-layouts  50.4 us (10%)
  between operations  10.5 us (2%)
    ppermute x47, waiting for transfers between devices, exchange(): lax.ppermute(value, AXES, pairs(lax.axis_size('dp'), lax.axis_size('seq')...  173 us
    ppermute x47, starting transfers between devices, exchange(): lax.ppermute(value, AXES, pairs(lax.axis_size('dp'), lax.axis_size('seq')...  51.5 us
    unnamed x159, local copies, waits for them, and re-layouts  27.9 us
    pallas_call x1, Pallas kernels, mix_back(): pl.pallas_call(attend_backward, grid=(HEADS // 2,), in_specs=[head_pair(n...  24.3 us
    pallas_call x3, Pallas kernels, assemble(): pl.pallas_call(body, out_shape=[jax.ShapeDtypeStruct(s, BF) for s in shap...  20 us
    dot_general x7, matrix products, matmul(): return jnp.dot(left, right, preferred_element_type=F32)  18.2 us
    pallas_call x1, Pallas kernels, mix_tokens(): pl.pallas_call(attend_forward, grid=(HEADS // 2,), in_specs=[head_pair(nq...  17.1 us
    dot_general x4, matrix products, inner(): lax.dot_general(grad, weight, (((1,), (1,)), ((), ())), preferred_element...  12.9 us
  transfers between devices with their start and end apart: 50, of which 21 were waited for; matrix products, arithmetic and copies ran while one was open for 15% of the time, Pallas kernels for 9%

profile of v1, /device:TPU:0, one launch (start us, length us, event | category | flops | bytes accessed | tf_op | source)
XLA Modules:
  0.0 483.1 jit_solution(11373928565653423810)
XLA Ops:
  3.3 5.1 %collective-permute-start.3 = (bf16[104,768]{1,0:T(8,128)(2,1)S(1)}, bf16[104,768]{1,0:T(8,128)(2,1)S(1)}, u32[]{:S(2)}, u32[]{:S(2)}) collective-permute-start(bf16[104,768]{1,0:T(8,128)(2,1)S(1)} %constant_dynamic-update-slice_fusion), channel_id=1, source_target_pairs={{0,24},{1,25},{2,26},{3,27},{4,28},{5,29},{6,30},{7,31},{8,16},{9,... | collective-permute-start | bytes 479240 | tf_op jit(solution)/shard_map/ppermute | solution.py:43
  11.0 3.8 collective-permute-start.14
  15.8 5.1 %collective-permute-start.12 = (bf16[120,768]{1,0:T(8,128)(2,1)S(1)}, bf16[120,768]{1,0:T(8,128)(2,1)S(1)}, u32[]{:S(2)}, u32[]{:S(2)}) collective-permute-start(bf16[120,768]{1,0:T(8,128)(2,1)S(1)} %constant_dynamic-update-slice_fusion.5), channel_id=1, source_target_pairs={{0,8},{1,9},{2,10},{3,11},{4,12},{5,13},{6,14},{7,15},{8,0},{9,1},... | collective-permute-start | bytes 552968 | tf_op jit(solution)/shard_map/ppermute | solution.py:43
  20.9 9.9 %collective-permute-done.2 = bf16[104,768]{1,0:T(8,128)(2,1)S(1)} collective-permute-done((bf16[104,768]{1,0:T(8,128)(2,1)S(1)}, bf16[104,768]{1,0:T(8,128)(2,1)S(1)}, u32[]{:S(2)}, u32[]{:S(2)}) %collective-permute-start.2) | collective-permute-done | bytes 159776 | tf_op jit(solution)/shard_map/ppermute | solution.py:43
  37.1 11.1 %collective-permute-done.4.refs_1_ = bf16[4,104,768]{2,1,0:T(8,128)(2,1)S(1)} collective-permute-done((bf16[4,104,768]{2,1,0:T(8,128)(2,1)S(1)}, bf16[4,104,768]{2,1,0:T(8,128)(2,1)S(1)}, u32[]{:S(2)}, u32[]{:S(2)}) %collective-permute-start.4) | collective-permute-done | bytes 639008 | tf_op jit(solution)/shard_map/ppermute | solution.py:43
  55.6 10.0 %collective-permute-done.23 = bf16[168,768]{1,0:T(8,128)(2,1)S(1)} collective-permute-done((bf16[168,768]{1,0:T(8,128)(2,1)S(1)}, bf16[168,768]{1,0:T(8,128)(2,1)S(1)}, u32[]{:S(2)}, u32[]{:S(2)}) %collective-permute-start.23) | collective-permute-done | bytes 258080 | tf_op jit(solution)/shard_map/ppermute | solution.py:43
  80.8 6.0 %assemble.3 = (bf16[4,2,2,2,8,128]{5,4,3,2,1,0:T(8,128)(2,1)}, bf16[4,2,2,2,24,768]{5,4,3,2,1,0:T(8,128)(2,1)}, bf16[4,2,2,2,24,2304]{5,4,3,2,1,0:T(8,128)(2,1)}) custom-call(s32[25]{0:T(128)} %concatenate.122.where, bf16[4,104,768]{2,1,0:T(8,128)(2,1)} %copy-done.15, bf16[4,104,768]{2,1,0:T(8,128)(2,1)} %copy-done.26, ...), custom_call_target="tpu_custom_call" | custom-call | tf_op jit(solution)/shard_map/assemble/pallas_call | solution.py:94
  89.5 7.8 %collective-permute-done.25.refs_1_ = bf16[4,168,768]{2,1,0:T(8,128)(2,1)} collective-permute-done((bf16[4,168,768]{2,1,0:T(8,128)(2,1)S(1)}, bf16[4,168,768]{2,1,0:T(8,128)(2,1)}, u32[]{:S(2)}, u32[]{:S(2)}) %collective-permute-start.25) | collective-permute-done | bytes 1032224 | tf_op jit(solution)/shard_map/ppermute | solution.py:43
  106.5 4.9 %collective-permute-done.17.refs_3_ = bf16[4,120,768]{2,1,0:T(8,128)(2,1)} collective-permute-done((bf16[4,120,768]{2,1,0:T(8,128)(2,1)}, bf16[4,120,768]{2,1,0:T(8,128)(2,1)}, u32[]{:S(2)}, u32[]{:S(2)}) %collective-permute-start.17) | collective-permute-done | bytes 737312 | tf_op jit(solution)/shard_map/ppermute | solution.py:43
  111.6 4.2 convolution_convert_fusion.3
  117.1 5.4 %collective-permute-done.26.refs_2_ = bf16[4,168,768]{2,1,0:T(8,128)(2,1)} collective-permute-done((bf16[4,168,768]{2,1,0:T(8,128)(2,1)S(1)}, bf16[4,168,768]{2,1,0:T(8,128)(2,1)}, u32[]{:S(2)}, u32[]{:S(2)}) %collective-permute-start.26) | collective-permute-done | bytes 1032224 | tf_op jit(solution)/shard_map/ppermute | solution.py:43
  123.2 10.3 %collective-permute-done.27.refs_3_ = bf16[4,168,768]{2,1,0:T(8,128)(2,1)} collective-permute-done((bf16[4,168,768]{2,1,0:T(8,128)(2,1)}, bf16[4,168,768]{2,1,0:T(8,128)(2,1)}, u32[]{:S(2)}, u32[]{:S(2)}) %collective-permute-start.27) | collective-permute-done | bytes 1032224 | tf_op jit(solution)/shard_map/ppermute | solution.py:43
  139.0 6.5 %assemble.4 = (bf16[4,2,2,2,24,768]{5,4,3,2,1,0:T(8,128)(2,1)}, bf16[4,2,2,2,24,3072]{5,4,3,2,1,0:T(8,128)(2,1)}) custom-call(s32[25]{0:T(128)} %concatenate.122.where, bf16[4,120,768]{2,1,0:T(8,128)(2,1)} %copy-done.14, bf16[4,120,768]{2,1,0:T(8,128)(2,1)} %collective-permute-done.15.refs_1_, bf16[4,120,768]{2,1,0:T(8,128)(2,1)} %collective-permute-done.16.refs_2_, ...), custom_call_target="tpu_custom_call" | custom-call | tf_op jit(solution)/shard_map/assemble/pallas_call | solution.py:94
  145.6 7.5 %assemble.5 = (bf16[4,2,2,2,96,768]{5,4,3,2,1,0:T(8,128)(2,1)}, bf16[2,4,2,2,2,24,1024]{6,5,4,3,2,1,0:T(8,128)(2,1)}) custom-call(s32[25]{0:T(128)} %concatenate.122.where, bf16[4,168,768]{2,1,0:T(8,128)(2,1)} %copy-done.9, bf16[4,168,768]{2,1,0:T(8,128)(2,1)} %collective-permute-done.25.refs_1_, bf16[4,168,768]{2,1,0:T(8,128)(2,1)} %collective-permute-done.26.refs_2_, ...), custom_call_target="tpu_custom_call" | custom-call | tf_op jit(solution)/shard_map/assemble/pallas_call | solution.py:94
  153.1 3.5 fusion.100
  156.6 3.7 pad_maximum_fusion.1
  160.3 17.1 %attend_forward.1 = (bf16[512,768]{1,0:T(8,128)(2,1)}, f32[6,2,512]{2,1,0:T(2,128)}) custom-call(bf16[512,768]{1,0:T(8,128)(2,1)} %slice.280.q_ref, bf16[1024,768]{1,0:T(8,128)(2,1)} %get-tuple-element.107.k_ref, bf16[1024,768]{1,0:T(8,128)(2,1)} %get-tuple-element.106.v_ref, s32[1,512]{1,0:T(1,128)} %bitcast.350, s32[1024,1]{1,0:T(8,128)} %copy.112.sk_ref), custom_call_target="tpu_custom_call" | custom-call | tf_op jit(solution)/shard_map/attend_forward/pallas_call | solution.py:249
  180.1 5.7 %multiply_convert_fusion = (bf16[512,3072]{1,0:T(8,128)(2,1)S(1)}, f32[512,3072]{1,0:T(8,128)S(1)}) fusion(bf16[768,3072]{1,0:T(8,128)(2,1)} %bitcast.355, f32[512,768]{1,0:T(8,128)S(1)} %get-tuple-element.178, f32[768]{0:T(1024)S(1)} %add.484, f32[768]{0:T(1024)S(1)} %mul.797, f32[512]{0:T(512)S(1)} %add_rsqrt_fusion, f32[512]{0:T(512)S(1)} %broadcast_multiply_fusion.4), kind=kOutput, calls=%fused_computation.16 | convolution fusion | flops 2425749504 | bytes 15738880 | tf_op jit(solution)/shard_map/dot_general | solution.py:308
  196.7 4.7 fusion.7
  232.3 24.3 %attend_backward.1 = (bf16[512,768]{1,0:T(8,128)(2,1)}, f32[1024,768]{1,0:T(8,128)}, f32[1024,768]{1,0:T(8,128)}) custom-call(bf16[512,768]{1,0:T(8,128)(2,1)} %slice.280.q_ref, bf16[1024,768]{1,0:T(8,128)(2,1)} %get-tuple-element.107.k_ref, bf16[1024,768]{1,0:T(8,128)(2,1)} %get-tuple-element.106.v_ref, bf16[512,768]{1,0:T(8,128)(2,1)} %convolution_convert_fusion.8.do_ref, ...), custom_call_target="tpu_custom_call" | custom-call | tf_op jit(solution)/shard_map/attend_backward/pallas_call | solution.py:264
  270.6 3.4 multiply_reduce_fusion.2
  286.0 11.9 %convert_add_fusion = f32[4,2,2,288,768]{4,3,2,1,0:T(8,128)} fusion(bf16[4,2,2,288,768]{4,3,2,1,0:T(8,128)(2,1)} %collective-permute-done.39, bf16[4,2,2,288,768]{4,3,2,1,0:T(8,128)(2,1)} %get-tuple-element.111), kind=kLoop, calls=%fused_computation | loop fusion | flops 10616832 | bytes 28311552 | tf_op jit(solution)/shard_map/add | solution.py:139
  297.9 7.8 %fusion = bf16[4,2,288,768]{3,2,0,1:T(8,128)(2,1)} fusion(pred[]{:T(512)S(6)} %eq.54, f32[4,2,2,288,768]{4,3,2,1,0:T(8,128)} %convert_add_fusion, s32[]{:T(128)S(6)} %select_n.166, s32[]{:T(128)S(6)} %select_n.173), kind=kLoop, calls=%fused_computation.3 | loop fusion | flops 1769472 | bytes 10616841 | tf_op jit(solution)/shard_map/convert_element_type | solution.py:140
  307.4 4.4 collective-permute-done.33
  316.9 30.6 %collective-permute-done.40 = bf16[4,2,288,768]{3,2,0,1:T(8,128)(2,1)} collective-permute-done((bf16[4,2,288,768]{3,2,0,1:T(8,128)(2,1)}, bf16[4,2,288,768]{3,2,0,1:T(8,128)(2,1)}, u32[]{:S(2)}, u32[]{:S(2)}) %collective-permute-start.40) | collective-permute-done | bytes 3538976 | tf_op jit(solution)/shard_map/ppermute | solution.py:43
  347.5 10.1 %fusion.1 = f32[4,2,288,768]{3,2,0,1:T(8,128)} fusion(bf16[4,2,288,768]{3,2,0,1:T(8,128)(2,1)} %collective-permute-done.40, pred[]{:T(512)S(6)} %eq.54, f32[4,2,2,288,768]{4,3,2,1,0:T(8,128)} %convert_add_fusion, s32[]{:T(128)S(6)} %select_n.165, s32[]{:T(128)S(6)} %select_n.171), kind=kLoop, calls=%fused_computation.5 | loop fusion | flops 5308416 | bytes 24772616 | tf_op jit(solution)/shard_map/add | solution.py:142
  357.6 3.4 fusion.13
  365.7 24.9 %collective-permute-done.35 = bf16[4,104,768]{2,1,0:T(8,128)(2,1)S(1)} collective-permute-done((bf16[4,104,768]{2,1,0:T(8,128)(2,1)S(1)}, bf16[4,104,768]{2,1,0:T(8,128)(2,1)S(1)}, u32[]{:S(2)}, u32[]{:S(2)}) %collective-permute-start.35) | collective-permute-done | bytes 639008 | tf_op jit(solution)/shard_map/ppermute | solution.py:43
  406.5 16.2 %collective-permute-done.37 = bf16[104,768]{1,0:T(8,128)(2,1)S(1)} collective-permute-done((bf16[104,768]{1,0:T(8,128)(2,1)S(1)}, bf16[104,768]{1,0:T(8,128)(2,1)S(1)}, u32[]{:S(2)}, u32[]{:S(2)}) %collective-permute-start.37) | collective-permute-done | bytes 159776 | tf_op jit(solution)/shard_map/ppermute | solution.py:43
  426.0 17.7 %collective-permute-done.43 = bf16[288,768]{1,0:T(8,128)(2,1)S(1)} collective-permute-done((bf16[288,768]{1,0:T(8,128)(2,1)S(1)}, bf16[288,768]{1,0:T(8,128)(2,1)S(1)}, u32[]{:S(2)}, u32[]{:S(2)}) %collective-permute-start.43) | collective-permute-done | bytes 442400 | tf_op jit(solution)/shard_map/ppermute | solution.py:43
  461.5 3.6 collective-permute-done.48
  466.1 3.4 collective-permute-done.49
  (409 shorter events, 178.7 us)
Async XLA Ops:
  8.5 22.4 %collective-permute-start.2 = (bf16[104,768]{1,0:T(8,128)(2,1)S(1)}, bf16[104,768]{1,0:T(8,128)(2,1)S(1)}, u32[]{:S(2)}, u32[]{:S(2)}) collective-permute-start(bf16[104,768]{1,0:T(8,128)(2,1)S(1)} %constant_dynamic-update-slice_fusion), channel_id=1, source_target_pairs={{0,16},{1,17},{2,18},{3,19},{4,20},{5,21},{6,22},{7,23},{8,24},{9,... | collective-permute-start | bytes 479240 | tf_op jit(solution)/shard_map/ppermute | solution.py:43
  8.5 22.4 %collective-permute-start.1 = (bf16[104,768]{1,0:T(8,128)(2,1)S(1)}, bf16[104,768]{1,0:T(8,128)(2,1)S(1)}, u32[]{:S(2)}, u32[]{:S(2)}) collective-permute-start(bf16[104,768]{1,0:T(8,128)(2,1)S(1)} %constant_dynamic-update-slice_fusion), channel_id=1, source_target_pairs={{0,8},{1,9},{2,10},{3,11},{4,12},{5,13},{6,14},{7,15},{8,0},{9,1},... | collective-permute-start | bytes 479240 | tf_op jit(solution)/shard_map/ppermute | solution.py:43
  11.0 24.5 %collective-permute-start.14 = (bf16[120,768]{1,0:T(8,128)(2,1)S(1)}, bf16[120,768]{1,0:T(8,128)(2,1)S(1)}, u32[]{:S(2)}, u32[]{:S(2)}) collective-permute-start(bf16[120,768]{1,0:T(8,128)(2,1)S(1)} %constant_dynamic-update-slice_fusion.5), channel_id=1, source_target_pairs={{0,24},{1,25},{2,26},{3,27},{4,28},{5,29},{6,30},{7,31},{8,16},{9,... | collective-permute-start | bytes 552968 | tf_op jit(solution)/shard_map/ppermute | solution.py:43
  14.8 35.5 %collective-permute-start.13 = (bf16[120,768]{1,0:T(8,128)(2,1)S(1)}, bf16[120,768]{1,0:T(8,128)(2,1)S(1)}, u32[]{:S(2)}, u32[]{:S(2)}) collective-permute-start(bf16[120,768]{1,0:T(8,128)(2,1)S(1)} %constant_dynamic-update-slice_fusion.5), channel_id=1, source_target_pairs={{0,16},{1,17},{2,18},{3,19},{4,20},{5,21},{6,22},{7,23},{8,24},{9,... | collective-permute-start | bytes 552968 | tf_op jit(solution)/shard_map/ppermute | solution.py:43
  15.8 34.6 %collective-permute-start.12 = (bf16[120,768]{1,0:T(8,128)(2,1)S(1)}, bf16[120,768]{1,0:T(8,128)(2,1)S(1)}, u32[]{:S(2)}, u32[]{:S(2)}) collective-permute-start(bf16[120,768]{1,0:T(8,128)(2,1)S(1)} %constant_dynamic-update-slice_fusion.5), channel_id=1, source_target_pairs={{0,8},{1,9},{2,10},{3,11},{4,12},{5,13},{6,14},{7,15},{8,0},{9,1},... | collective-permute-start | bytes 552968 | tf_op jit(solution)/shard_map/ppermute | solution.py:43
  30.9 17.2 %collective-permute-start.4 = (bf16[4,104,768]{2,1,0:T(8,128)(2,1)S(1)}, bf16[4,104,768]{2,1,0:T(8,128)(2,1)S(1)}, u32[]{:S(2)}, u32[]{:S(2)}) collective-permute-start(bf16[4,104,768]{2,1,0:T(8,128)(2,1)S(1)} %pad_maximum_fusion.7.refs_0_), channel_id=1, source_target_pairs={{0,4},{1,3},{2,6},{3,1},{4,0},{5,7},{6,2},{7,5},{8,12},{9,11},{10,... | collective-permute-start | bytes 1916936 | tf_op jit(solution)/shard_map/ppermute | solution.py:43
  32.7 17.8 %collective-permute-start.24 = (bf16[168,768]{1,0:T(8,128)(2,1)S(1)}, bf16[168,768]{1,0:T(8,128)(2,1)S(1)}, u32[]{:S(2)}, u32[]{:S(2)}) collective-permute-start(bf16[168,768]{1,0:T(8,128)(2,1)S(1)} %get-tuple-element.155), channel_id=1, source_target_pairs={{0,24},{1,25},{2,26},{3,27},{4,28},{5,29},{6,30},{7,31},{8,16},{9,... | collective-permute-start | bytes 774152 | tf_op jit(solution)/shard_map/ppermute | solution.py:43
  35.6 32.1 %collective-permute-start.5 = (bf16[4,104,768]{2,1,0:T(8,128)(2,1)S(1)}, bf16[4,104,768]{2,1,0:T(8,128)(2,1)}, u32[]{:S(2)}, u32[]{:S(2)}) collective-permute-start(bf16[4,104,768]{2,1,0:T(8,128)(2,1)S(1)} %pad_maximum_fusion.7.refs_0_), channel_id=1, source_target_pairs={{0,2},{1,5},{2,0},{3,7},{4,6},{5,1},{6,4},{7,3},{8,10},{9,13},{10,... | collective-permute-start | bytes 1916936 | tf_op jit(solution)/shard_map/ppermute | solution.py:43
  48.2 20.0 %collective-permute-start.6 = (bf16[4,104,768]{2,1,0:T(8,128)(2,1)S(1)}, bf16[4,104,768]{2,1,0:T(8,128)(2,1)}, u32[]{:S(2)}, u32[]{:S(2)}) collective-permute-start(bf16[4,104,768]{2,1,0:T(8,128)(2,1)S(1)} %collective-permute-done.4.refs_1_), channel_id=1, source_target_pairs={{0,2},{1,5},{2,0},{3,7},{4,6},{5,1},{6,4},{7,3},{8,10},{9,13},{10,... | collective-permute-start | bytes 1916936 | tf_op jit(solution)/shard_map/ppermute | solution.py:43
  50.3 19.3 %collective-permute-start.7 = (bf16[4,104,768]{2,1,0:T(8,128)(2,1)S(1)}, bf16[4,104,768]{2,1,0:T(8,128)(2,1)}, u32[]{:S(2)}, u32[]{:S(2)}) collective-permute-start(bf16[4,104,768]{2,1,0:T(8,128)(2,1)S(1)} %pad_maximum_fusion.7.refs_0_), channel_id=1, source_target_pairs={{0,1},{1,0},{2,3},{3,2},{4,5},{5,4},{6,7},{7,6},{8,9},{9,8},{10,11... | collective-permute-start | bytes 1916936 | tf_op jit(solution)/shard_map/ppermute | solution.py:43
  50.5 17.2 %collective-permute-start.22 = (bf16[168,768]{1,0:T(8,128)(2,1)S(1)}, bf16[168,768]{1,0:T(8,128)(2,1)}, u32[]{:S(2)}, u32[]{:S(2)}) collective-permute-start(bf16[168,768]{1,0:T(8,128)(2,1)S(1)} %get-tuple-element.155), channel_id=1, source_target_pairs={{0,8},{1,9},{2,10},{3,11},{4,12},{5,13},{6,14},{7,15},{8,0},{9,1},... | collective-permute-start | bytes 774152 | tf_op jit(solution)/shard_map/ppermute | solution.py:43
  69.6 27.8 %collective-permute-start.25 = (bf16[4,168,768]{2,1,0:T(8,128)(2,1)S(1)}, bf16[4,168,768]{2,1,0:T(8,128)(2,1)}, u32[]{:S(2)}, u32[]{:S(2)}) collective-permute-start(bf16[4,168,768]{2,1,0:T(8,128)(2,1)S(1)} %pad_maximum_fusion.4.refs_0_), channel_id=1, source_target_pairs={{0,4},{1,3},{2,6},{3,1},{4,0},{5,7},{6,2},{7,5},{8,12},{9,11},{10,... | collective-permute-start | bytes 3096584 | tf_op jit(solution)/shard_map/ppermute | solution.py:43
  77.6 25.9 %collective-permute-start.16 = (bf16[4,120,768]{2,1,0:T(8,128)(2,1)S(1)}, bf16[4,120,768]{2,1,0:T(8,128)(2,1)}, u32[]{:S(2)}, u32[]{:S(2)}) collective-permute-start(bf16[4,120,768]{2,1,0:T(8,128)(2,1)S(1)} %pad_maximum_fusion.6.refs_0_), channel_id=1, source_target_pairs={{0,2},{1,5},{2,0},{3,7},{4,6},{5,1},{6,4},{7,3},{8,10},{9,13},{10,... | collective-permute-start | bytes 2211848 | tf_op jit(solution)/shard_map/ppermute | solution.py:43
  80.0 26.4 %collective-permute-start.18 = (bf16[4,120,768]{2,1,0:T(8,128)(2,1)S(1)}, bf16[4,120,768]{2,1,0:T(8,128)(2,1)}, u32[]{:S(2)}, u32[]{:S(2)}) collective-permute-start(bf16[4,120,768]{2,1,0:T(8,128)(2,1)S(1)} %pad_maximum_fusion.6.refs_0_), channel_id=1, source_target_pairs={{0,1},{1,0},{2,3},{3,2},{4,5},{5,4},{6,7},{7,6},{8,9},{9,8},{10,11... | collective-permute-start | bytes 2211848 | tf_op jit(solution)/shard_map/ppermute | solution.py:43
  80.0 31.4 %collective-permute-start.17 = (bf16[4,120,768]{2,1,0:T(8,128)(2,1)}, bf16[4,120,768]{2,1,0:T(8,128)(2,1)}, u32[]{:S(2)}, u32[]{:S(2)}) collective-permute-start(bf16[4,120,768]{2,1,0:T(8,128)(2,1)} %collective-permute-done.15.refs_1_), channel_id=1, source_target_pairs={{0,2},{1,5},{2,0},{3,7},{4,6},{5,1},{6,4},{7,3},{8,10},{9,13},{10,... | collective-permute-start | bytes 2211848 | tf_op jit(solution)/shard_map/ppermute | solution.py:43
  89.1 33.3 %collective-permute-start.26 = (bf16[4,168,768]{2,1,0:T(8,128)(2,1)S(1)}, bf16[4,168,768]{2,1,0:T(8,128)(2,1)}, u32[]{:S(2)}, u32[]{:S(2)}) collective-permute-start(bf16[4,168,768]{2,1,0:T(8,128)(2,1)S(1)} %pad_maximum_fusion.4.refs_0_), channel_id=1, source_target_pairs={{0,2},{1,5},{2,0},{3,7},{4,6},{5,1},{6,4},{7,3},{8,10},{9,13},{10,... | collective-permute-start | bytes 3096584 | tf_op jit(solution)/shard_map/ppermute | solution.py:43
  97.4 36.1 %collective-permute-start.27 = (bf16[4,168,768]{2,1,0:T(8,128)(2,1)}, bf16[4,168,768]{2,1,0:T(8,128)(2,1)}, u32[]{:S(2)}, u32[]{:S(2)}) collective-permute-start(bf16[4,168,768]{2,1,0:T(8,128)(2,1)} %collective-permute-done.25.refs_1_), channel_id=1, source_target_pairs={{0,2},{1,5},{2,0},{3,7},{4,6},{5,1},{6,4},{7,3},{8,10},{9,13},{10,... | collective-permute-start | bytes 3096584 | tf_op jit(solution)/shard_map/ppermute | solution.py:43
  103.5 19.1 %collective-permute-start.19 = (bf16[4,120,768]{2,1,0:T(8,128)(2,1)}, bf16[4,120,768]{2,1,0:T(8,128)(2,1)}, u32[]{:S(2)}, u32[]{:S(2)}) collective-permute-start(bf16[4,120,768]{2,1,0:T(8,128)(2,1)} %collective-permute-done.15.refs_1_), channel_id=1, source_target_pairs={{0,1},{1,0},{2,3},{3,2},{4,5},{5,4},{6,7},{7,6},{8,9},{9,8},{10,11... | collective-permute-start | bytes 2211848 | tf_op jit(solution)/shard_map/ppermute | solution.py:43
  111.4 22.1 %collective-permute-start.21 = (bf16[4,120,768]{2,1,0:T(8,128)(2,1)}, bf16[4,120,768]{2,1,0:T(8,128)(2,1)}, u32[]{:S(2)}, u32[]{:S(2)}) collective-permute-start(bf16[4,120,768]{2,1,0:T(8,128)(2,1)} %collective-permute-done.17.refs_3_), channel_id=1, source_target_pairs={{0,1},{1,0},{2,3},{3,2},{4,5},{5,4},{6,7},{7,6},{8,9},{9,8},{10,11... | collective-permute-start | bytes 2211848 | tf_op jit(solution)/shard_map/ppermute | solution.py:43
  122.4 34.1 %collective-permute-start.11 = (bf16[512,1536]{1,0:T(8,128)(2,1)}, bf16[512,1536]{1,0:T(8,128)(2,1)}, u32[]{:S(2)}, u32[]{:S(2)}) collective-permute-start(bf16[512,1536]{1,0:T(8,128)(2,1)} %slice.281), channel_id=1, source_target_pairs={{0,1},{1,0},{2,3},{3,2},{4,5},{5,4},{6,7},{7,6},{8,9},{9,8},{10,11... | collective-permute-start | bytes 4718600 | tf_op jit(solution)/shard_map/ppermute | solution.py:330
  122.6 23.0 %collective-permute-start.28 = (bf16[4,168,768]{2,1,0:T(8,128)(2,1)S(1)}, bf16[4,168,768]{2,1,0:T(8,128)(2,1)}, u32[]{:S(2)}, u32[]{:S(2)}) collective-permute-start(bf16[4,168,768]{2,1,0:T(8,128)(2,1)S(1)} %pad_maximum_fusion.4.refs_0_), channel_id=1, source_target_pairs={{0,1},{1,0},{2,3},{3,2},{4,5},{5,4},{6,7},{7,6},{8,9},{9,8},{10,11... | collective-permute-start | bytes 3096584 | tf_op jit(solution)/shard_map/ppermute | solution.py:43
  123.1 22.4 %collective-permute-start.29 = (bf16[4,168,768]{2,1,0:T(8,128)(2,1)}, bf16[4,168,768]{2,1,0:T(8,128)(2,1)}, u32[]{:S(2)}, u32[]{:S(2)}) collective-permute-start(bf16[4,168,768]{2,1,0:T(8,128)(2,1)} %collective-permute-done.25.refs_1_), channel_id=1, source_target_pairs={{0,1},{1,0},{2,3},{3,2},{4,5},{5,4},{6,7},{7,6},{8,9},{9,8},{10,11... | collective-permute-start | bytes 3096584 | tf_op jit(solution)/shard_map/ppermute | solution.py:43
  230.6 54.0 %collective-permute-start.39 = (bf16[4,2,2,288,768]{4,3,2,1,0:T(8,128)(2,1)}, bf16[4,2,2,288,768]{4,3,2,1,0:T(8,128)(2,1)}, u32[]{:S(2)}, u32[]{:S(2)}) collective-permute-start(bf16[4,2,2,288,768]{4,3,2,1,0:T(8,128)(2,1)} %get-tuple-element.112), channel_id=1, source_target_pairs={{0,1},{1,0},{2,3},{3,2},{4,5},{5,4},{6,7},{7,6},{8,9},{9,8},{10,11... | collective-permute-start | bytes 21233672 | tf_op jit(solution)/shard_map/ppermute | solution.py:43
  305.7 41.8 %collective-permute-start.40 = (bf16[4,2,288,768]{3,2,0,1:T(8,128)(2,1)}, bf16[4,2,288,768]{3,2,0,1:T(8,128)(2,1)}, u32[]{:S(2)}, u32[]{:S(2)}) collective-permute-start(bf16[4,2,288,768]{3,2,0,1:T(8,128)(2,1)} %fusion), channel_id=1, source_target_pairs={{0,2},{1,5},{2,0},{3,7},{4,6},{5,1},{6,4},{7,3},{8,10},{9,13},{10,... | collective-permute-start | bytes 10616840 | tf_op jit(solution)/shard_map/ppermute | solution.py:43
  316.3 46.3 %collective-permute-start.34 = (bf16[4,2,104,768]{3,2,1,0:T(8,128)(2,1)}, bf16[4,2,104,768]{3,2,1,0:T(8,128)(2,1)S(1)}, u32[]{:S(2)}, u32[]{:S(2)}) collective-permute-start(bf16[4,2,104,768]{3,2,1,0:T(8,128)(2,1)} %fusion.9), channel_id=1, source_target_pairs={{0,2},{1,5},{2,0},{3,7},{4,6},{5,1},{6,4},{7,3},{8,10},{9,13},{10,... | collective-permute-start | bytes 3833864 | tf_op jit(solution)/shard_map/ppermute | solution.py:43
  361.0 35.6 %collective-permute-start.41 = (bf16[4,288,768]{2,1,0:T(8,128)(2,1)}, bf16[4,288,768]{2,1,0:T(8,128)(2,1)}, u32[]{:S(2)}, u32[]{:S(2)}) collective-permute-start(bf16[4,288,768]{2,1,0:T(8,128)(2,1)} %fusion.13), channel_id=1, source_target_pairs={{0,4},{1,3},{2,6},{3,1},{4,0},{5,7},{6,2},{7,5},{8,12},{9,11},{10,... | collective-permute-start | bytes 5308424 | tf_op jit(solution)/shard_map/ppermute | solution.py:43
  364.6 26.0 %collective-permute-start.35 = (bf16[4,104,768]{2,1,0:T(8,128)(2,1)S(1)}, bf16[4,104,768]{2,1,0:T(8,128)(2,1)S(1)}, u32[]{:S(2)}, u32[]{:S(2)}) collective-permute-start(bf16[4,104,768]{2,1,0:T(8,128)(2,1)S(1)} %fusion.24), channel_id=1, source_target_pairs={{0,4},{1,3},{2,6},{3,1},{4,0},{5,7},{6,2},{7,5},{8,12},{9,11},{10,... | collective-permute-start | bytes 1916936 | tf_op jit(solution)/shard_map/ppermute | solution.py:43
  393.6 29.2 %collective-permute-start.37 = (bf16[104,768]{1,0:T(8,128)(2,1)S(1)}, bf16[104,768]{1,0:T(8,128)(2,1)S(1)}, u32[]{:S(2)}, u32[]{:S(2)}) collective-permute-start(bf16[104,768]{1,0:T(8,128)(2,1)S(1)} %get-tuple-element.110), channel_id=1, source_target_pairs={{0,16},{1,17},{2,18},{3,19},{4,20},{5,21},{6,22},{7,23},{8,24},{9,... | collective-permute-start | bytes 479240 | tf_op jit(solution)/shard_map/ppermute | solution.py:43
  393.6 29.2 %collective-permute-start.36 = (bf16[104,768]{1,0:T(8,128)(2,1)S(1)}, bf16[104,768]{1,0:T(8,128)(2,1)S(1)}, u32[]{:S(2)}, u32[]{:S(2)}) collective-permute-start(bf16[104,768]{1,0:T(8,128)(2,1)S(1)} %get-tuple-element.108), channel_id=1, source_target_pairs={{0,8},{1,9},{2,10},{3,11},{4,12},{5,13},{6,14},{7,15},{8,0},{9,1},... | collective-permute-start | bytes 479240 | tf_op jit(solution)/shard_map/ppermute | solution.py:43
  402.1 23.8 %collective-permute-start.44 = (bf16[288,768]{1,0:T(8,128)(2,1)}, bf16[288,768]{1,0:T(8,128)(2,1)S(1)}, u32[]{:S(2)}, u32[]{:S(2)}) collective-permute-start(bf16[288,768]{1,0:T(8,128)(2,1)} %get-tuple-element.99), channel_id=1, source_target_pairs={{0,24},{1,25},{2,26},{3,27},{4,28},{5,29},{6,30},{7,31},{8,16},{9,... | collective-permute-start | bytes 1327112 | tf_op jit(solution)/shard_map/ppermute | solution.py:43
  403.5 40.2 %collective-permute-start.43 = (bf16[288,768]{1,0:T(8,128)(2,1)S(1)}, bf16[288,768]{1,0:T(8,128)(2,1)S(1)}, u32[]{:S(2)}, u32[]{:S(2)}) collective-permute-start(bf16[288,768]{1,0:T(8,128)(2,1)S(1)} %get-tuple-element.100), channel_id=1, source_target_pairs={{0,16},{1,17},{2,18},{3,19},{4,20},{5,21},{6,22},{7,23},{8,24},{9,... | collective-permute-start | bytes 1327112 | tf_op jit(solution)/shard_map/ppermute | solution.py:43
  403.6 40.0 %collective-permute-start.42 = (bf16[288,768]{1,0:T(8,128)(2,1)S(1)}, bf16[288,768]{1,0:T(8,128)(2,1)S(1)}, u32[]{:S(2)}, u32[]{:S(2)}) collective-permute-start(bf16[288,768]{1,0:T(8,128)(2,1)S(1)} %get-tuple-element.98), channel_id=1, source_target_pairs={{0,8},{1,9},{2,10},{3,11},{4,12},{5,13},{6,14},{7,15},{8,0},{9,1},... | collective-permute-start | bytes 1327112 | tf_op jit(solution)/shard_map/ppermute | solution.py:43
  (88 other events, 1151.8 us)

commit v2 on v1

v2 whole, which is shorter than its diff:
```python
from functools import partial

import jax
import jax.numpy as jnp
from jax import lax
from jax.experimental import pallas as pl
from jax.experimental.pallas import tpu as pltpu
from jax.sharding import PartitionSpec as P

HEADS = 12
HD = 64
L = 1
IMGS = 3
STEP_COUNT = 7

NORM_EPS = 1e-06
MASKED = -1000000000.0
SCALE = 0.125
BETA_ONE = 0.9
BETA_TWO = 0.999
ADAM_EPS = 1e-08
DECAY = 0.05
BASE_RATE = 0.05
LAYER_RATE = 0.75
CLIP_AT = 0.05
HIGH = lax.Precision.HIGHEST
BF = jnp.bfloat16
F32 = jnp.float32
AXES = ("dp", "seq")
D = 768
HALF = 384
PAIRS = HEADS // 4
RATES = (LAYER_RATE ** (L + 1), LAYER_RATE, LAYER_RATE, LAYER_RATE, LAYER_RATE, 1.0)


def pairs(move):
    dp_size, seq_size = lax.axis_size("dp"), lax.axis_size("seq")
    return [
        (d * seq_size + s, move(d, s)[0] * seq_size + move(d, s)[1])
        for d in range(dp_size)
        for s in range(seq_size)
    ]


def exchange(value, move):
    return lax.ppermute(value, AXES, pairs(move))


def along_z(step):
    return lambda d, s: (d ^ (2 * step), s)


def across_core(d, s):
    return (d, s ^ 1)


def across_first(d, s):
    return (d ^ 1, s) if s % 2 == 0 else (d, s ^ 2)


def across_second(d, s):
    return (d, s ^ 2) if s % 2 == 0 else (d ^ 1, s)


def swap(value):
    return exchange(value, across_core)


def spot():
    dp, seq = lax.axis_index("dp"), lax.axis_index("seq")
    return (dp // 2, dp % 2, seq // 2, seq % 2)


def total_of(value):
    for bit in range((lax.axis_size("seq") - 1).bit_length()):
        value = value + exchange(value, lambda d, s, bit=bit: (d, s ^ (1 << bit)))
    for bit in range((lax.axis_size("dp") - 1).bit_length()):
        value = value + exchange(value, lambda d, s, bit=bit: (d ^ (1 << bit), s))
    return value


def after(value, *others):
    return lax.optimization_barrier((value,) + others)[0]


def at(value, index, axis):
    return lax.dynamic_index_in_dim(value, index, axis, keepdims=False)


def in_core_order(core, mine, other, axis):
    return jnp.where(
        core == 0,
        jnp.concatenate([mine, other], axis),
        jnp.concatenate([other, mine], axis),
    )


def both_tokens(value):
    return jnp.concatenate([value, swap(value)], 0)


def to_columns(core, value):
    halves = value.reshape(value.shape[0], 2, HALF)
    return jnp.concatenate([at(halves, core, 1), swap(at(halves, 1 - core, 1))], 0)


def to_tokens(core, value):
    count = value.shape[0] // 2
    return in_core_order(core, value[:count], swap(value[count:]), 1)


def reduce_tokens(value):
    count = value.shape[0] // 2
    return value[:count] + swap(value[count:])


def cost(flops, byte_count):
    return pl.CostEstimate(flops=int(flops), bytes_accessed=int(byte_count), transcendentals=0)


def half_of(shard, parts, which):
    rows, wide = shard.shape
    return at(shard.reshape(rows, parts, 2, wide // parts // 2), which, 2).reshape(rows, -1)


def join_halves(core, mine, other, parts):
    rows = mine.shape[0]
    shape = (rows, parts, 1, mine.shape[1] // parts)
    return in_core_order(core, mine.reshape(shape), other.reshape(shape), 2).reshape(rows, -1)


def pad_lanes(value, width):
    return jnp.pad(value, ((0, 0), (0, width - value.shape[1])))


def assemble(pieces, places, z, plan, shapes):
    count = len(pieces)

    def body(where, *refs):
        ins, outs = refs[:count], refs[count:]
        for i in range(count):
            x, y = where[2 * i + 1], where[2 * i + 2]
            rows = ins[i].shape[1]
            for j in range(2):
                for o, row, lane in plan:
                    outs[o][(where[0] % 2) ^ j, x, y, row : row + rows, :] = ins[i][
                        j, :, lane : lane + outs[o].shape[-1]
                    ]

    def out_spec(shape):
        return pl.BlockSpec((2,) + shape[1:], lambda j, where: ((where[0] // 2) ^ j, 0, 0, 0, 0))

    slab = (2,) + pieces[0].shape[1:]
    size = 4 * pieces[0].size
    return pl.pallas_call(
        body,
        out_shape=[jax.ShapeDtypeStruct(s, BF) for s in shapes],
        grid_spec=pltpu.PrefetchScalarGridSpec(
            num_scalar_prefetch=1,
            grid=(pieces[0].shape[0] // 2,),
            in_specs=[pl.BlockSpec(slab, lambda j, where: (j, 0, 0))] * count,
            out_specs=[out_spec(s) for s in shapes],
        ),
        cost_estimate=cost(0, 4 * size),
        name="assemble",
    )(jnp.concatenate([jnp.stack([z]), places]).astype(jnp.int32), *pieces)


def gather_column(unit):
    pair = jnp.stack([unit, exchange(unit, along_z(1))])
    return jnp.concatenate([pair, exchange(pair, along_z(2))], 0)


def gather_plane(own, plan, widths):
    z, x, y, c = spot()
    near = exchange(own, across_first)
    side = exchange(own, across_second)
    far = exchange(near, across_second)
    places = jnp.stack([x, y, x ^ (1 - c), y ^ c, x ^ c, y ^ (1 - c), x ^ 1, y ^ 1])
    shapes = [(own.shape[0], 2, 2) + w for w in widths]
    return assemble([own, near, side, far], places, z, plan, shapes), near


def gather_weights(embedder, attend, merger, expand, shrink, readout, vectors):
    _, _, _, c = spot()
    low = [w.astype(BF) for w in (embedder, attend[0], merger[0], expand[0], shrink[0], readout)]
    embedder, attend, merger, expand, shrink, readout = low
    vectors = vectors.astype(BF)
    rows, chips = embedder.shape[0], lax.axis_size("dp") * lax.axis_size("seq") // 2
    tall, thin = vectors.shape
    wide = -(-readout.shape[2] // 128) * 128

    def chip_rows(mine, other):
        return in_core_order(c, mine, other, 0)

    def of_core(k):
        vec = jnp.pad(vectors, ((0, rows - tall), (0, 128 - thin)))
        first = [half_of(embedder, 1, k), vec, half_of(attend, 3, k)]
        second = [half_of(merger, 1, k), half_of(expand, chips, k), pad_lanes(at(readout, k, 0), wide)]
        return jnp.concatenate(first, 1), jnp.concatenate(second, 1)

    mine, give = of_core(c), of_core(1 - c)
    got = swap(give[0])
    front = chip_rows(mine[0], got)
    vec = in_core_order(c, vectors, got[:tall, HALF : HALF + thin], 1)
    vec = jnp.pad(vec, ((0, 2 * rows - tall), (0, 128 - 2 * thin)))
    back = chip_rows(mine[1], swap(give[1]))
    tall_shrink = shrink.shape[0]
    shrink = jnp.concatenate([shrink[: 2 * rows], shrink[2 * rows :]], 1)

    tall_rows = 2 * rows
    unit = jnp.concatenate([front[:, :HALF], vec, front[:, HALF + 128 :]], 1)
    own = gather_column(unit)
    (emb, vec, att), near = gather_plane(
        own,
        [(0, 0, 0), (1, 0, HALF), (2, 0, HALF + 128)],
        [(tall_rows, HALF), (tall_rows, 128), (tall_rows, 3 * HALF)],
    )
    own = gather_column(after(back[:, : 5 * HALF], own))
    (mer, exp), _ = gather_plane(
        own, [(0, 0, 0), (1, 0, HALF)], [(tall_rows, HALF), (tall_rows, 4 * HALF)]
    )
    unit = jnp.concatenate([shrink, back[:, 5 * HALF :]], 1)
    own = gather_column(after(unit, own, near))
    (shr, rea), _ = gather_plane(
        own,
        [(0, 0, 0), (0, tall_rows, D), (1, 0, 2 * D)],
        [(tall_shrink, D), (tall_rows, wide)],
    )
    vec = vec.reshape(chips, 2 * rows, 128)[:, :tall, : 2 * thin].transpose(1, 0, 2)
    return (
        emb.reshape(-1, HALF),
        att.reshape(-1, 3 * HALF),
        mer.reshape(-1, HALF),
        exp.reshape(-1, 4 * HALF),
        shr.reshape(-1, D),
        rea.reshape(-1, wide),
        vec.reshape(tall, -1),
    )


def gather_plain(embedder, attend, merger, expand, shrink, readout, vectors):
    _, _, _, c = spot()
    chips = lax.axis_size("dp") * lax.axis_size("seq") // 2
    wide = -(-readout.shape[2] // 128) * 128

    def whole_of(shard, axis):
        return lax.all_gather(shard.astype(BF), AXES, axis=axis, tiled=True)

    shrink = whole_of(shrink[0], 0).reshape(chips, 2, -1, D)
    return (
        half_of(whole_of(embedder, 0), 1, c),
        half_of(whole_of(attend[0], 0), 3, c),
        half_of(whole_of(merger[0], 0), 1, c),
        half_of(whole_of(expand[0], 0), chips, c),
        at(shrink, c, 1).reshape(-1, D),
        pad_lanes(at(whole_of(readout, 1), c, 0), wide),
        whole_of(vectors, 1),
    )


def blocks(grad):
    chips = lax.axis_size("dp") * lax.axis_size("seq") // 2
    return grad.reshape(chips // 4, 2, 2, grad.shape[0] // chips, grad.shape[1])


def lane_plan(grads, rows):
    plan, lane = [], 0
    for n, g in enumerate(grads):
        for row in range(0, g.shape[3], rows):
            plan.append((n, row, lane))
            lane += g.shape[4]
    return plan, lane


def position():
    return jnp.stack(spot()).astype(jnp.int32)


def chosen(grads, keep):
    def spec(g):
        def index(t, w):
            px = jnp.where(w[3] == 0, t, w[1] if keep else 1 - w[1])
            py = jnp.where(w[3] == 0, w[2] if keep else 1 - w[2], t)
            return (0, px, py, 0, 0)

        return pl.BlockSpec((g.shape[0], 1, 1) + g.shape[3:], index)

    return [spec(g) for g in grads]


def scatter_give(grads, rows):
    depth, count = grads[0].shape[0], len(grads)
    plan, lanes = lane_plan(grads, rows)

    def body(w, *refs):
        for n, row, lane in plan:
            block = refs[n][:, 0, 0, row : row + rows, :]
            refs[count][:, 0, :, lane : lane + block.shape[2]] = block

    give = pl.pallas_call(
        body,
        out_shape=jax.ShapeDtypeStruct((depth, 2, rows, lanes), BF),
        grid_spec=pltpu.PrefetchScalarGridSpec(
            num_scalar_prefetch=1,
            grid=(2,),
            in_specs=chosen(grads, False),
            out_specs=pl.BlockSpec((depth, 1, rows, lanes), lambda t, w: (0, t, 0, 0)),
        ),
        cost_estimate=cost(0, 8 * depth * rows * lanes),
        name="scatter_give",
    )(position(), *grads)
    return grads, rows, exchange(give, across_second)


def scatter_near(state, *others):
    grads, rows, got = state
    depth, count = grads[0].shape[0], len(grads)
    plan, lanes = lane_plan(grads, rows)

    def body(w, *refs):
        ins, got_ref, give_ref, keep_ref = refs[:count], refs[count], refs[count + 1], refs[count + 2]
        here = jnp.where(w[3] == 0, w[1], w[2])
        for n, row, lane in plan:
            block = ins[n][:, 0, 0, row : row + rows, :]
            span = slice(lane, lane + block.shape[2])
            value = block.astype(F32) + got_ref[:, 0, :, span].astype(F32)

            @pl.when(pl.program_id(0) == here)
            def _():
                keep_ref[:, :, span] = value

            @pl.when(pl.program_id(0) != here)
            def _():
                give_ref[:, :, span] = value.astype(BF)

    out = pl.BlockSpec((depth, rows, lanes), lambda t, w: (0, 0, 0))
    slab = pl.BlockSpec((depth, 1, rows, lanes), lambda t, w: (0, t, 0, 0))
    give, keep = pl.pallas_call(
        body,
        out_shape=[jax.ShapeDtypeStruct((depth, rows, lanes), t) for t in (BF, F32)],
        grid_spec=pltpu.PrefetchScalarGridSpec(
            num_scalar_prefetch=1,
            grid=(2,),
            in_specs=chosen(grads, True) + [slab],
            out_specs=[out, out],
        ),
        cost_estimate=cost(0, 14 * depth * rows * lanes),
        name="scatter_near",
    )(position(), *grads, after(got, *others))
    return keep, exchange(give, across_first)


def scatter_column(state, *others):
    keep, got = state
    depth, rows, lanes = keep.shape

    def body(w, keep_in, got_ref, keep_ref, give_ref):
        for j in range(depth):
            value = keep_in[w[0] ^ j] + got_ref[w[0] ^ j].astype(F32)
            if j < 2:
                keep_ref[j] = value
            else:
                give_ref[j - 2] = value.astype(BF)

    block = pl.BlockSpec((depth, rows, lanes), lambda t, w: (0, 0, 0))
    out = pl.BlockSpec((2, rows, lanes), lambda t, w: (0, 0, 0))
    keep, give = pl.pallas_call(
        body,
        out_shape=[jax.ShapeDtypeStruct((2, rows, lanes), t) for t in (F32, BF)],
        grid_spec=pltpu.PrefetchScalarGridSpec(
            num_scalar_prefetch=1, grid=(1,), in_specs=[block, block], out_specs=[out, out]
        ),
        cost_estimate=cost(0, 9 * depth * rows * lanes),
        name="scatter_column",
    )(position(), keep, after(got, *others))
    return keep, exchange(give, along_z(2))


def scatter_pair(state, *others):
    keep, got = state
    total = keep + after(got, *others).astype(F32)
    return total[0], exchange(total[1].astype(BF), along_z(1))


def scatter_end(state):
    return state[0] + state[1].astype(F32)


def own_rows(core, unit):
    halves = unit.reshape(2, unit.shape[0] // 2, unit.shape[1])
    return at(halves, core, 0), swap(at(halves, 1 - core, 0))


def first_done(state, classes):
    core = lax.axis_index("seq") % 2
    unit = scatter_end(state)
    shrink = jnp.concatenate([unit[:, :D], unit[:, D : 2 * D]], 0)
    mine, other = own_rows(core, unit[:, 2 * D :])
    return shrink, in_core_order(core, mine[None], other[None], 0)[:, :, :classes]


def second_done(state, wide):
    core = lax.axis_index("seq") % 2
    chips = lax.axis_size("dp") * lax.axis_size("seq") // 2
    mine, other = own_rows(core, scatter_end(state))
    return (
        join_halves(core, mine[:, :wide], other[:, :wide], chips),
        join_halves(core, mine[:, wide:], other[:, wide:], 1),
    )


def vector_blocks(vectors, like):
    chips = lax.axis_size("dp") * lax.axis_size("seq") // 2
    tall, thin = vectors.shape[0], vectors.shape[1] // chips
    vec = vectors.astype(BF).reshape(tall, chips, thin).transpose(1, 0, 2)
    vec = jnp.pad(vec, ((0, 0), (0, like.shape[3] - tall), (0, 128 - thin)))
    return vec.reshape(like.shape[:4] + (128,))


def last_done(attend, embedder, tall, thin):
    core = lax.axis_index("seq") % 2
    attend, unit = scatter_end(attend), scatter_end(embedder)
    rows = attend.shape[0] // 2
    pieces = unit[:tall, HALF : HALF + 2 * thin].reshape(tall, 2, thin)
    halves = jnp.concatenate([unit[:, :HALF], attend], 1).reshape(2, rows, -1)
    mine = at(halves, core, 0)
    sent = jnp.pad(at(pieces, 1 - core, 1), ((0, rows - tall), (0, 128 - thin)))
    got = swap(jnp.concatenate([at(halves, 1 - core, 0), sent], 1))
    wide = mine.shape[1]
    return (
        join_halves(core, mine[:, :HALF], got[:, :HALF], 1),
        join_halves(core, mine[:, HALF:], got[:, HALF:wide], 3),
        at(pieces, core, 1) + got[:tall, wide : wide + thin],
    )


def scatter_plain(grads, classes):
    embedder, attend, merger, expand, shrink, readout, vectors = grads
    _, _, _, c = spot()
    chips = lax.axis_size("dp") * lax.axis_size("seq") // 2

    def reduced(value, axis):
        value = value.astype(F32)
        return lax.psum_scatter(value, AXES, scatter_dimension=axis, tiled=True)

    def spread(half, parts):
        return reduced(join_halves(c, half, jnp.zeros_like(half), parts), 0)

    tall = shrink.reshape(chips, 1, -1, D)
    tall = in_core_order(c, tall, jnp.zeros_like(tall), 1).reshape(-1, D)
    pair = in_core_order(c, readout[None], jnp.zeros_like(readout)[None], 0)
    return (
        spread(embedder, 1),
        spread(attend, 3),
        spread(merger, 1),
        spread(expand, chips),
        reduced(tall, 0),
        reduced(pair, 1)[:, :, :classes],
        reduced(vectors, 1),
    )


def dot_keys(left, right):
    return lax.dot_general(left, right, (((1,), (1,)), ((), ())), preferred_element_type=F32)


def turned(value):
    return value.astype(F32).T.astype(BF)


def attend_forward(q_ref, k_ref, v_ref, qm_ref, km_ref, out_ref, exact_ref, lse_ref, keys, values):
    lane = lax.broadcasted_iota(jnp.int32, (1, 2 * HD), 1) // HD

    @pl.when(pl.program_id(1) == 0)
    def _():
        for h in range(2):
            keys[h] = jnp.where(lane == h, k_ref[...], km_ref[...])
        values[...] = turned(v_ref[...])

    query = q_ref[...] * jnp.asarray(SCALE, BF)
    parts = []
    for h in range(2):
        raw = dot_keys(keys[h], jnp.where(lane == h, query, qm_ref[...]))
        top = jnp.max(raw, 0, keepdims=True)
        heavy = jnp.exp(raw - top)
        mass = jnp.sum(heavy, 0, keepdims=True)
        shares = (heavy * (1.0 / mass)).astype(BF)
        part = jnp.dot(values[...], shares, preferred_element_type=F32)
        parts.append(part[HD * h : HD * (h + 1)])
        lse_ref[0, h : h + 1, :] = top + jnp.log(mass)
    mixed = jnp.concatenate(parts, 0).T
    exact_ref[...] = mixed
    out_ref[...] = mixed.astype(BF)


def attend_backward(joined, q_ref, k_ref, v_ref, do_ref, exact_ref, lse_ref, qm_ref, km_ref, *refs):
    outs, (keys, turned_keys, grad_keys, grad_values) = refs[:-4], refs[-4:]
    lane = lax.broadcasted_iota(jnp.int32, (1, 2 * HD), 1) // HD
    pair, step = pl.program_id(0), pl.program_id(1)

    @pl.when(step == 0)
    def _():
        for h in range(2):
            keys[h] = jnp.where(lane == h, k_ref[...], km_ref[...])
        turned_keys[...] = turned(k_ref[...])
        grad_keys[...] = jnp.zeros_like(grad_keys)
        grad_values[...] = jnp.zeros_like(grad_values)

    query = q_ref[...] * jnp.asarray(SCALE, BF)
    grad = do_ref[...]
    spreads = (grad.astype(F32) * exact_ref[...]).T
    parts = []
    for h in range(2):
        own = slice(HD * h, HD * (h + 1))
        grad_h = jnp.where(lane == h, grad, jnp.zeros_like(grad))
        query_h = jnp.where(lane == h, query, jnp.zeros_like(query))
        raw = dot_keys(keys[h], jnp.where(lane == h, query, qm_ref[...]))
        shares = jnp.exp(raw - lse_ref[0, h : h + 1, :])
        spread = jnp.sum(spreads[own], 0, keepdims=True)
        grad_raw = (shares * (dot_keys(v_ref[...], grad_h) - spread)).astype(BF)
        parts.append(jnp.dot(turned_keys[...], grad_raw, preferred_element_type=F32)[own])
        grad_keys[...] += jnp.dot(grad_raw, query_h, preferred_element_type=F32)
        grad_values[...] += jnp.dot(shares.astype(BF), grad_h, preferred_element_type=F32)
    grad_query = (jnp.concatenate(parts, 0).T * SCALE).astype(BF)
    if joined:
        rows = grad_query.shape[0]
        down = pl.ds(pl.multiple_of(step * rows, rows), rows)
        outs[0][down, pl.ds(pl.multiple_of(pair * 128, 128), 128)] = grad_query
    else:
        outs[0][...] = grad_query

    @pl.when(step == pl.num_programs(1) - 1)
    def _():
        if joined:
            across = pl.num_programs(0)
            for n, total in enumerate((grad_keys, grad_values)):
                place = (pair + across * (n + 1)) * 128
                outs[0][:, pl.ds(pl.multiple_of(place, 128), 128)] = total[...].astype(BF)
        else:
            outs[1][...] = grad_keys[...]
            outs[2][...] = grad_values[...]


def tile_of(count):
    return 256 if count % 256 == 0 else count


def mix_tokens(projected, around, mask_q, mask_k):
    nq, nk = projected.shape[0], around.shape[0]
    tile = tile_of(nq)
    rows = lambda part: pl.BlockSpec((tile, 128), lambda i, j: (j, part * PAIRS + i))
    tall = lambda part: pl.BlockSpec((nk, 128), lambda i, j: (0, part * PAIRS + i))
    return pl.pallas_call(
        attend_forward,
        grid=(PAIRS, nq // tile),
        in_specs=[
            rows(0),
            tall(1),
            tall(2),
            pl.BlockSpec((tile, 128), lambda i, j: (j, 0)),
            pl.BlockSpec((nk, 128), lambda i, j: (0, 0)),
        ],
        out_specs=[rows(0), rows(0), pl.BlockSpec((1, 2, tile), lambda i, j: (i, 0, j))],
        out_shape=[
            jax.ShapeDtypeStruct((nq, HALF), BF),
            jax.ShapeDtypeStruct((nq, HALF), F32),
            jax.ShapeDtypeStruct((PAIRS, 2, nq), F32),
        ],
        scratch_shapes=[pltpu.VMEM((2, nk, 128), BF), pltpu.VMEM((128, nk), BF)],
        cost_estimate=cost(8 * nq * nk * HALF * 4, 12 * nq * HALF),
        name="attend_forward",
    )(projected, around, around, mask_q, mask_k)


def mix_back(projected, around, grad, exact, lse, mask_q, mask_k):
    nq, nk = projected.shape[0], around.shape[0]
    tile, joined = tile_of(nq), nq == nk
    rows = lambda part: pl.BlockSpec((tile, 128), lambda i, j: (j, part * PAIRS + i))
    tall = lambda part: pl.BlockSpec((nk, 128), lambda i, j: (0, part * PAIRS + i))
    if joined:
        out_specs = [pl.BlockSpec((nq, 3 * HALF), lambda i, j: (0, 0))]
        out_shape = [jax.ShapeDtypeStruct((nq, 3 * HALF), BF)]
    else:
        out_specs = [rows(0), tall(0), tall(0)]
        out_shape = [jax.ShapeDtypeStruct((nq, HALF), BF)]
        out_shape += [jax.ShapeDtypeStruct((nk, HALF), F32)] * 2
    return pl.pallas_call(
        partial(attend_backward, joined),
        grid=(PAIRS, nq // tile),
        in_specs=[
            rows(0),
            tall(1),
            tall(2),
            rows(0),
            rows(0),
            pl.BlockSpec((1, 2, tile), lambda i, j: (i, 0, j)),
            pl.BlockSpec((tile, 128), lambda i, j: (j, 0)),
            pl.BlockSpec((nk, 128), lambda i, j: (0, 0)),
        ],
        out_specs=out_specs,
        out_shape=out_shape,
        scratch_shapes=[
            pltpu.VMEM((2, nk, 128), BF),
            pltpu.VMEM((128, nk), BF),
            pltpu.VMEM((nk, 128), F32),
            pltpu.VMEM((nk, 128), F32),
        ],
        cost_estimate=cost(20 * nq * nk * HALF * 3, 12 * nq * HALF),
        name="attend_backward",
    )(projected, around, around, grad, exact, lse, mask_q, mask_k)


def norm_parts(x):
    centre = x - jnp.mean(x, -1, keepdims=True)
    rate = lax.rsqrt(jnp.mean(centre * centre, -1, keepdims=True) + NORM_EPS)
    return (centre * rate, rate)


def layer_norm(x, gain, shift):
    return norm_parts(x)[0] * gain + shift


def norm_back(x, gain, grad):
    unit, rate = norm_parts(x)
    inner_grad = grad * gain
    back = rate * (
        inner_grad
        - jnp.mean(inner_grad, -1, keepdims=True)
        - unit * jnp.mean(inner_grad * unit, -1, keepdims=True)
    )
    return (back, jnp.sum(grad * unit, 0), jnp.sum(grad, 0))


def matmul(left, right):
    return jnp.dot(left, right, preferred_element_type=F32)


def outer(left, right):
    return lax.dot_general(left, right, (((0,), (0,)), ((), ())), preferred_element_type=F32)


def inner(grad, weight):
    return lax.dot_general(grad, weight, (((1,), (1,)), ((), ())), preferred_element_type=F32)


def chip_bits():
    return [2 << b for b in range((lax.axis_size("seq") // 4 - 1).bit_length())]


def of_bit(value, bit):
    return exchange(value, lambda d, s: (d, s ^ bit))


def row_tokens(value):
    for bit in chip_bits():
        value = jnp.concatenate([value, of_bit(value, bit)], 0)
    return value


def row_return(value):
    for bit in reversed(chip_bits()):
        half = value.shape[0] // 2
        value = value[:half] + of_bit(value[half:].astype(BF), bit).astype(F32)
    return value


def row_sum(value):
    for bit in chip_bits():
        value = value + of_bit(value, bit)
    return value


def segment_lanes(segment, of_query):
    lane = jnp.arange(128, dtype=jnp.int32) % HD
    hit = segment[:, None] == lane[None, :]
    if of_query:
        return jnp.where(hit | (lane > IMGS)[None, :], 0.0, MASKED).astype(BF)
    return hit.astype(BF)


def adamw(weight, mean, square, grad, scale, decay):
    mean_next = BETA_ONE * mean + (1.0 - BETA_ONE) * grad
    square_next = BETA_TWO * square + (1.0 - BETA_TWO) * grad * grad
    mean_hat = mean_next / (1.0 - BETA_ONE**STEP_COUNT)
    square_hat = square_next / (1.0 - BETA_TWO**STEP_COUNT)
    weight_next = weight - BASE_RATE * scale * (
        mean_hat / (jnp.sqrt(square_hat) + ADAM_EPS) + decay * weight
    )
    return (weight_next, mean_next, square_next)


def moments(mean, square, grad):
    return (
        BETA_ONE * mean + (1.0 - BETA_ONE) * grad,
        BETA_TWO * square + (1.0 - BETA_TWO) * grad * grad,
    )


def on_device(
    pixels,
    lengths,
    labels,
    teacher,
    embedder,
    embedder_mean,
    embedder_square,
    attend,
    attend_mean,
    attend_square,
    merger,
    merger_mean,
    merger_square,
    expand,
    expand_mean,
    expand_square,
    shrink,
    shrink_mean,
    shrink_square,
    readout,
    readout_mean,
    readout_square,
    vectors,
    vectors_mean,
    vectors_square,
):
    seq_size, dp_size = lax.axis_size("seq"), lax.axis_size("dp")
    fast = seq_size == 4 and dp_size == 8 and embedder.shape[0] == 24
    seq, core = lax.axis_index("seq"), lax.axis_index("seq") % 2
    local, far = pixels.shape[1], seq_size // 2
    span = seq_size // 4
    classes = readout.shape[2]
    image_count = lengths.shape[0] * dp_size * IMGS

    side = seq // far
    pixels_got = of_bit(at(pixels, 1 - side, 0), far)
    tokens = jnp.concatenate([at(pixels, side, 0), pixels_got], 0)
    all_pixels = both_tokens(tokens)
    row_lengths = at(lengths, side, 0)
    row_labels = at(labels, side, 0)
    row_teacher = at(teacher, side, 0)

    def places_of(where):
        step = jnp.arange(local, dtype=jnp.int32)
        return jnp.concatenate([where * local + step, (where ^ far) * local + step])

    places = places_of(seq)
    ends = jnp.cumsum(row_lengths)
    starts = ends - row_lengths

    def segment_of(spots):
        return jnp.sum((spots[:, None] >= ends[None, :]).astype(jnp.int32), 1)

    seg_q = segment_of(jnp.concatenate([places, places_of(seq ^ 1)]))
    order = [0]
    for bit in chip_bits():
        order = order + [o ^ bit for o in order]
    seg_k = segment_of(jnp.concatenate([places_of(seq ^ o ^ k) for o in order for k in range(2)]))
    mask_q, mask_k = segment_lanes(seg_q, True), segment_lanes(seg_k, False)
    marks = jnp.concatenate([starts, starts + 1])
    hits = (marks[:, None] == places[None, :]).astype(F32)
    token_hits = (places[:, None] == marks[None, :]).astype(F32)
    is_cls, is_dist = jnp.sum(hits[:IMGS], 0), jnp.sum(hits[IMGS:], 0)
    is_patch = (seg_q[: 2 * local] < IMGS).astype(F32) - is_cls - is_dist

    gather = gather_weights if fast else gather_plain
    embed_w, attend_w, merger_half, expand_w, shrink_w, readout_w, vector_w = gather(
        embedder, attend, merger, expand, shrink, readout, vectors
    )
    merger_w = in_core_order(core, merger_half, swap(merger_half), 1)
    vector_f = vector_w.astype(F32)

    patches = to_tokens(core, matmul(all_pixels, embed_w))
    x = (
        is_patch[:, None] * patches
        + is_cls[:, None] * vector_f[4 * L + 2]
        + is_dist[:, None] * vector_f[4 * L + 3]
    )
    a = both_tokens(layer_norm(x, vector_f[0], vector_f[1]).astype(BF))
    projected = matmul(a, attend_w).astype(BF)
    around = row_tokens(projected)
    mixed_half, exact, lse = mix_tokens(projected, around, mask_q, mask_k)
    other = swap(mixed_half)
    count = 2 * local
    other = jnp.concatenate([other[count:], other[:count]], 0)
    mixed = in_core_order(core, mixed_half, other, 1)
    x_mid = x + matmul(mixed[:count], merger_w)
    normed = both_tokens(layer_norm(x_mid, vector_f[2], vector_f[3]).astype(BF))
    hidden_in = matmul(normed, expand_w)
    cdf = 0.5 * (1.0 + lax.erf(hidden_in * (0.5**0.5)))
    hidden = (hidden_in * cdf).astype(BF)
    slope = cdf + hidden_in * jnp.exp(-0.5 * hidden_in * hidden_in) * ((0.5 / jnp.pi) ** 0.5)
    x_last = x_mid + reduce_tokens(matmul(hidden, shrink_w))

    label_hot = (row_labels[:, None] == jnp.arange(classes, dtype=jnp.int32)).astype(F32)
    teach_log = jax.nn.log_softmax(row_teacher, -1)
    target = jnp.where(core == 0, label_hot, jnp.exp(teach_log))
    target_log = jnp.where(core == 0, 0.0, teach_log)
    gain, shift = vector_f[4 * L], vector_f[4 * L + 1]
    rows = row_sum(jnp.dot(hits, x_last, precision=HIGH)).reshape(2, IMGS, D)
    rows = at(rows, core, 0) + swap(at(rows, 1 - core, 0))
    unit, rate = norm_parts(rows)
    head_in = (unit * gain + shift).astype(BF)
    logits = matmul(head_in, readout_w)[:, :classes]
    log_share = jax.nn.log_softmax(logits, -1)
    loss_local = jnp.sum(0.5 * target * (target_log - log_share)) / span
    grad_logits = pad_lanes(
        0.5 * (jnp.exp(log_share) - target) / image_count, readout_w.shape[1]
    )
    grad_readout = lax.dot_general(
        head_in.astype(F32), grad_logits / span, (((0,), (0,)), ((), ())), precision=HIGH
    )
    grad_head = lax.dot_general(
        grad_logits, readout_w.astype(F32), (((1,), (1,)), ((), ())), precision=HIGH
    )
    head_back, gain_out, shift_out = norm_back(rows, gain, grad_head)
    back = in_core_order(core, head_back, swap(head_back), 0)

    grad_out = jnp.dot(token_hits, back, precision=HIGH)
    grad_branch = both_tokens(grad_out.astype(BF))
    grad_shrink = outer(hidden, grad_branch).astype(BF)
    grad_readout = grad_readout.astype(BF)
    if fast:
        parts = [blocks(grad_shrink), blocks(grad_readout)]
        unit_rows = parts[1].shape[3]
        first = scatter_give(parts, unit_rows)
    grad_pre = (inner(grad_branch, shrink_w) * slope).astype(BF)
    grad_expand = outer(normed, grad_pre).astype(BF)
    grad_normed, gain_two, shift_two = norm_back(
        x_mid, vector_f[2], reduce_tokens(inner(grad_pre, expand_w))
    )
    grad_mid = grad_out + grad_normed
    grad_attn = both_tokens(grad_mid.astype(BF))
    attn_half = at(grad_attn.reshape(-1, 2, HALF), core, 1)
    grad_merger = outer(mixed, attn_half).astype(BF)
    if fast:
        second = scatter_give([blocks(grad_expand), blocks(grad_merger)], unit_rows)
    grad_mixed = inner(grad_attn, at(merger_w.reshape(2, HALF, D), core, 0)).astype(BF)
    grads = mix_back(projected, around, grad_mixed, exact, lse, mask_q, mask_k)
    if len(grads) == 1:
        grad_proj = grads[0]
    else:
        grad_proj = jnp.concatenate([grads[0]] + [row_return(g).astype(BF) for g in grads[1:]], 1)
    if fast:
        first = scatter_near(first, grad_proj)
    grad_a = inner(grad_proj, attend_w)
    grad_attend = outer(a, grad_proj).astype(BF)
    if fast:
        third = scatter_give([blocks(grad_attend)], unit_rows)
        second = scatter_near(second, grad_attend)
    grad_input, gain_one, shift_one = norm_back(x, vector_f[0], reduce_tokens(grad_a))
    grad_x = grad_mid + grad_input
    grad_patch = (grad_x * is_patch[:, None]).astype(BF)
    grad_embed = outer(all_pixels, to_columns(core, grad_patch)).astype(BF)
    grad_vectors = jnp.stack(
        [
            gain_one,
            shift_one,
            gain_two,
            shift_two,
            gain_out / span,
            shift_out / span,
            jnp.sum(grad_x * is_cls[:, None], 0),
            jnp.sum(grad_x * is_dist[:, None], 0),
        ]
    )
    if fast:
        first = scatter_column(first, grad_patch)
        parts = [blocks(grad_embed)]
        fourth = scatter_give(parts + [vector_blocks(grad_vectors, parts[0])], unit_rows)
        third = scatter_near(third, grad_embed)
        second = scatter_column(second, grad_embed)
        fourth = scatter_near(fourth)
        first = scatter_pair(first, fourth[0])
        third = scatter_column(third)
        fourth = scatter_column(fourth)
        second = scatter_pair(second, fourth[0])
        third, fourth = scatter_pair(third), scatter_pair(fourth)
        sum_shrink, sum_readout = first_done(first, classes)
        sum_expand, sum_merger = second_done(second, grad_expand.shape[1])
        sum_embed, sum_attend, sum_vectors = last_done(third, fourth, *vectors.shape)
    else:
        sum_embed, sum_attend, sum_merger, sum_expand, sum_shrink, sum_readout, sum_vectors = (
            scatter_plain(
                (grad_embed, grad_attend, grad_merger, grad_expand)
                + (grad_shrink, grad_readout, grad_vectors),
                classes,
            )
        )
    reduced = (sum_embed, sum_attend, sum_merger, sum_expand, sum_shrink, sum_readout)
    square_sum = sum((jnp.sum(g * g) for g in reduced)) + jnp.sum(sum_vectors * sum_vectors)
    both = total_of(jnp.stack([square_sum, loss_local])[None, :])
    grad_norm = jnp.sqrt(both[0, 0])
    factor = jnp.minimum(1.0, CLIP_AT / (grad_norm + 1e-06))

    masters = (embedder, attend, merger, expand, shrink, readout)
    means = (embedder_mean, attend_mean, merger_mean, expand_mean, shrink_mean, readout_mean)
    squares = (
        embedder_square,
        attend_square,
        merger_square,
        expand_square,
        shrink_square,
        readout_square,
    )
    outs = []
    for j in range(6):
        grad = reduced[j].reshape(masters[j].shape) * factor
        outs += adamw(masters[j], means[j], squares[j], grad, RATES[j], DECAY)
    outs += moments(vectors_mean, vectors_square, sum_vectors * factor)
    return tuple(outs) + (both[0, 1] / image_count, grad_norm)


def solution(mesh):
    return jax.shard_map(
        on_device,
        mesh=mesh,
        in_specs=(
            P("dp", "seq", None),
            P("dp", None),
            P("dp", None),
            P("dp", None, None),
            P(("dp", "seq"), None),
            P(("dp", "seq"), None),
            P(("dp", "seq"), None),
            P(None, ("dp", "seq"), None),
            P(None, ("dp", "seq"), None),
            P(None, ("dp", "seq"), None),
            P(None, ("dp", "seq"), None),
            P(None, ("dp", "seq"), None),
            P(None, ("dp", "seq"), None),
            P(None, ("dp", "seq"), None),
            P(None, ("dp", "seq"), None),
            P(None, ("dp", "seq"), None),
            P(None, ("dp", "seq"), None),
            P(None, ("dp", "seq"), None),
            P(None, ("dp", "seq"), None),
            P(None, ("dp", "seq"), None),
            P(None, ("dp", "seq"), None),
            P(None, ("dp", "seq"), None),
            P(None, ("dp", "seq")),
            P(None, ("dp", "seq")),
            P(None, ("dp", "seq")),
        ),
        out_specs=(
            P(("dp", "seq"), None),
            P(("dp", "seq"), None),
            P(("dp", "seq"), None),
            P(None, ("dp", "seq"), None),
            P(None, ("dp", "seq"), None),
            P(None, ("dp", "seq"), None),
            P(None, ("dp", "seq"), None),
            P(None, ("dp", "seq"), None),
            P(None, ("dp", "seq"), None),
            P(None, ("dp", "seq"), None),
            P(None, ("dp", "seq"), None),
            P(None, ("dp", "seq"), None),
            P(None, ("dp", "seq"), None),
            P(None, ("dp", "seq"), None),
            P(None, ("dp", "seq"), None),
            P(None, ("dp", "seq"), None),
            P(None, ("dp", "seq"), None),
            P(None, ("dp", "seq"), None),
            P(None, ("dp", "seq")),
            P(None, ("dp", "seq")),
            P(),
            P(),
        ),
        check_vma=False,
    )
```

time: 492 us -> 418 us (0.85)
  waiting for transfers between devices: 177 us -> 119 us
  Pallas kernels: 61.4 us -> 100 us
  other arithmetic: 79.1 us -> 43.8 us
  local copies, waits for them, and re-layouts: 50.4 us -> 23.4 us
  matrix products: 52.1 us -> 65.9 us
    ppermute x50 -> x56, waiting for transfers between devices: 177 us -> 119 us  [exchange(): return lax.ppermute(value, AXES, pairs(move))]
    pallas_call x2 -> x14, Pallas kernels: 41.4 us -> 88.1 us  [the longest x1 24.9 us: mix_tokens(): pl.pallas_call(attend_forward, grid=(PAIRS, nq // tile), in_specs=[rows(0...]
    add x12 -> x13, other arithmetic: 29.9 us -> 0.38 us  [the longest x4 0.22 us: scatter_pair(): total = keep + after(got, *others).astype(F32)]
    unnamed x159 -> x173, local copies, waits for them, and re-layouts: 27.9 us -> 7.84 us
    dot_general x5, matrix products: 12 us -> 20.9 us  [outer(): lax.dot_general(left, right, (((0,), (0,)), ((), ())), preferred_element_...]
    pallas_call x3, Pallas kernels: 20 us -> 12 us  [assemble(): pl.pallas_call(body, out_shape=[jax.ShapeDtypeStruct(s, BF) for s in shap...]
    convert_element_type x4 -> x8, other arithmetic: 12.1 us -> 5.6 us  [the longest x1 1.97 us: on_device(): grad_attn = both_tokens(grad_mid.astype(BF))]
    slice x20 -> x19, local copies, waits for them, and re-layouts: 10.1 us -> 3.8 us  [the longest x3 1.72 us: reduce_tokens(): return value[:count] + swap(value[count:])]
  transfers between devices with their start and end apart: 50 -> 56, of which waited for: 21 -> 26; matrix products, arithmetic and copies ran while one was open for 15% -> 19% of each run, Pallas kernels for 9% -> 24%
where the time goes in v2:
time: 418 us; the launch traced here: 412 us
  waiting for transfers between devices  119 us (28%)
  Pallas kernels  100 us (24%)
  matrix products  65.9 us (16%)
  starting transfers between devices  48.6 us (12%)
  other arithmetic  43.8 us (10%)
  local copies, waits for them, and re-layouts  23.4 us (6%)
  between operations  11.2 us (3%)
    ppermute x56, waiting for transfers between devices, exchange(): return lax.ppermute(value, AXES, pairs(move))  119 us
    ppermute x56, starting transfers between devices, exchange(): return lax.ppermute(value, AXES, pairs(move))  48.6 us
    pallas_call x1, Pallas kernels, mix_tokens(): pl.pallas_call(attend_forward, grid=(PAIRS, nq // tile), in_specs=[rows(0...  24.9 us
    pallas_call x1, Pallas kernels, mix_back(): pl.pallas_call(partial(attend_backward, joined), grid=(PAIRS, nq // tile)...  23.9 us
    dot_general x5, matrix products, outer(): lax.dot_general(left, right, (((0,), (0,)), ((), ())), preferred_element_...  20.9 us
    dot_general x6, matrix products, matmul(): return jnp.dot(left, right, preferred_element_type=F32)  20.6 us
    dot_general x4, matrix products, inner(): lax.dot_general(grad, weight, (((1,), (1,)), ((), ())), preferred_element...  17.3 us
    pallas_call x4, Pallas kernels, scatter_near(): pl.pallas_call(body, out_shape=[jax.ShapeDtypeStruct((depth, rows, lanes)...  15.5 us
  transfers between devices with their start and end apart: 56, of which 26 were waited for; matrix products, arithmetic and copies ran while one was open for 19% of the time, Pallas kernels for 24%

profile of v2, /device:TPU:0, one launch (start us, length us, event | category | flops | bytes accessed | tf_op | source)
XLA Modules:
  0.0 412.2 jit_solution(13459406795773731724)
XLA Ops:
  12.5 4.2 %collective-permute-done.3 = bf16[48,1664]{1,0:T(8,128)(2,1)S(1)} collective-permute-done((bf16[48,1664]{1,0:T(8,128)(2,1)S(1)}, bf16[48,1664]{1,0:T(8,128)(2,1)S(1)}, u32[]{:S(2)}, u32[]{:S(2)}) %collective-permute-start.3) | collective-permute-done | bytes 159776 | tf_op jit(solution)/shard_map/ppermute | solution.py:46
  20.1 12.8 %collective-permute-done.4 = bf16[2,48,1664]{2,1,0:T(8,128)(2,1)S(1)} collective-permute-done((bf16[2,48,1664]{2,1,0:T(8,128)(2,1)S(1)}, bf16[2,48,1664]{2,1,0:T(8,128)(2,1)S(1)}, u32[]{:S(2)}, u32[]{:S(2)}) %collective-permute-start.4) | collective-permute-done | bytes 319520 | tf_op jit(solution)/shard_map/ppermute | solution.py:46
  36.7 3.6 collective-permute-done.12
  43.1 4.7 %collective-permute-done.5.refs_1_ = bf16[4,48,1664]{2,1,0:T(8,128)(2,1)} collective-permute-done((bf16[4,48,1664]{2,1,0:T(8,128)(2,1)S(1)}, bf16[4,48,1664]{2,1,0:T(8,128)(2,1)}, u32[]{:S(2)}, u32[]{:S(2)}) %collective-permute-start.5) | collective-permute-done | bytes 639008 | tf_op jit(solution)/shard_map/ppermute | solution.py:46
  50.7 7.7 %collective-permute-done.13 = bf16[2,48,1920]{2,1,0:T(8,128)(2,1)} collective-permute-done((bf16[2,48,1920]{2,1,0:T(8,128)(2,1)}, bf16[2,48,1920]{2,1,0:T(8,128)(2,1)}, u32[]{:S(2)}, u32[]{:S(2)}) %collective-permute-start.13) | collective-permute-done | bytes 368672 | tf_op jit(solution)/shard_map/ppermute | solution.py:46
  60.3 4.0 assemble.3
  71.0 3.4 collective-permute-start.20
  83.7 13.1 %collective-permute-done.20 = bf16[2,48,2560]{2,1,0:T(8,128)(2,1)} collective-permute-done((bf16[2,48,2560]{2,1,0:T(8,128)(2,1)}, bf16[2,48,2560]{2,1,0:T(8,128)(2,1)}, u32[]{:S(2)}, u32[]{:S(2)}) %collective-permute-start.20) | collective-permute-done | bytes 491552 | tf_op jit(solution)/shard_map/ppermute | solution.py:46
  100.0 3.7 convolution_convert_fusion.q_ref.k_ref.v_ref
  103.7 24.9 %attend_forward.1 = (bf16[1024,384]{1,0:T(8,128)(2,1)}, f32[1024,384]{1,0:T(8,128)}, f32[3,2,1024]{2,1,0:T(2,128)}) custom-call(bf16[1024,1152]{1,0:T(8,128)(2,1)} %convolution_convert_fusion.q_ref.k_ref.v_ref, bf16[1024,1152]{1,0:T(8,128)(2,1)} %convolution_convert_fusion.q_ref.k_ref.v_ref, bf16[1024,1152]{1,0:T(8,128)(2,1)} %convolution_convert_fusion.q_ref.k_ref.v_ref, ...), custom_call_target="tpu_custom_call" | custom-call | flops 12884901888 | bytes 4718592 | tf_op jit(solution)/shard_map/attend_forward/pallas_call | solution.py:554
  128.6 3.7 assemble.4
  141.8 6.1 %collective-permute-done.22.refs_2_ = bf16[4,48,2560]{2,1,0:T(8,128)(2,1)} collective-permute-done((bf16[4,48,2560]{2,1,0:T(8,128)(2,1)}, bf16[4,48,2560]{2,1,0:T(8,128)(2,1)}, u32[]{:S(2)}, u32[]{:S(2)}) %collective-permute-start.22) | collective-permute-done | bytes 983072 | tf_op jit(solution)/shard_map/ppermute | solution.py:46
  147.9 10.5 %collective-permute-done.23.refs_3_ = bf16[4,48,2560]{2,1,0:T(8,128)(2,1)} collective-permute-done((bf16[4,48,2560]{2,1,0:T(8,128)(2,1)}, bf16[4,48,2560]{2,1,0:T(8,128)(2,1)}, u32[]{:S(2)}, u32[]{:S(2)}) %collective-permute-start.23) | collective-permute-done | bytes 983072 | tf_op jit(solution)/shard_map/ppermute | solution.py:46
  158.5 4.2 %assemble.5 = (bf16[4,2,2,96,768]{4,3,2,1,0:T(8,128)(2,1)}, bf16[4,2,2,48,1024]{4,3,2,1,0:T(8,128)(2,1)}) custom-call(s32[9]{0:T(128)} %concatenate.226.where, bf16[4,48,2560]{2,1,0:T(8,128)(2,1)} %pad_maximum_fusion.11.refs_0_, bf16[4,48,2560]{2,1,0:T(8,128)(2,1)} %collective-permute-done.21.refs_1_, bf16[4,48,2560]{2,1,0:T(8,128)(2,1)} %collective-permute-done.22.refs_2_, ...), custom_call_target="tpu_custom_call" | custom-call | bytes 7864320 | tf_op jit(solution)/shard_map/assemble/pallas_call | solution.py:155
  162.7 7.4 %multiply_convert_fusion = (bf16[1024,1536]{1,0:T(8,128)(2,1)S(1)}, f32[1024,1536]{1,0:T(8,128)}) fusion(bf16[768,1536]{1,0:T(8,128)(2,1)} %bitcast.234, bf16[512,768]{0,1:T(8,128)(2,1)} %collective-permute-done.18, bf16[512,768]{0,1:T(8,128)(2,1)} %add_convert_fusion), kind=kOutput, calls=%fused_computation.7 | convolution fusion | flops 2426929152 | bytes 13369344 | tf_op jit(solution)/shard_map/dot_general | solution.py:636
  189.0 6.8 %fusion.5 = bf16[1024,1536]{1,0:T(8,128)(2,1)S(1)} fusion(f32[1024,1536]{1,0:T(8,128)} %get-tuple-element.187, bf16[1536,768]{1,0:T(8,128)(2,1)S(1)} %bitcast.237, bf16[512,768]{1,0:T(8,128)(2,1)S(1)} %collective-permute-done.27, bf16[512,768]{1,0:T(8,128)(2,1)S(1)} %get-tuple-element.191), kind=kOutput, calls=%fused_computation.6 | convolution fusion | flops 2434793472 | bytes 13369344 | tf_op jit(solution)/shard_map/dot_general | solution.py:644
  213.2 4.2 %convolution_convert_fusion.1 = bf16[1536,768]{1,0:T(8,128)(2,1)} fusion(bf16[1024,1536]{1,0:T(8,128)(2,1)S(1)} %copy-done.77, bf16[512,768]{1,0:T(8,128)(2,1)S(1)} %copy-done.72, bf16[512,768]{1,0:T(8,128)(2,1)S(1)} %copy-done.22), kind=kOutput, calls=%fused_computation.10 | convolution fusion | flops 2420244480 | bytes 7077888 | tf_op jit(solution)/shard_map/dot_general | solution.py:640
  222.7 6.4 %convolution_convert_fusion.2 = bf16[768,1536]{1,0:T(8,128)(2,1)} fusion(bf16[1024,1536]{1,0:T(8,128)(2,1)} %copy-done.78, bf16[512,768]{0,1:T(8,128)(2,1)} %collective-permute-done.18, bf16[512,768]{0,1:T(8,128)(2,1)} %add_convert_fusion), kind=kOutput, calls=%fused_computation.11 | convolution fusion | flops 2420244480 | bytes 7077888 | tf_op jit(solution)/shard_map/dot_general | solution.py:640
  229.0 3.5 convolution_convert_fusion.5.do_ref
  232.5 23.9 %attend_backward.1 = bf16[1024,1152]{1,0:T(8,128)(2,1)} custom-call(bf16[1024,1152]{1,0:T(8,128)(2,1)} %convolution_convert_fusion.q_ref.k_ref.v_ref, bf16[1024,1152]{1,0:T(8,128)(2,1)} %convolution_convert_fusion.q_ref.k_ref.v_ref, bf16[1024,1152]{1,0:T(8,128)(2,1)} %convolution_convert_fusion.q_ref.k_ref.v_ref, ...), custom_call_target="tpu_custom_call" | custom-call | flops 24159191040 | bytes 4718592 | tf_op jit(solution)/shard_map/attend_backward/pallas_call | solution.py:588
  256.4 4.4 %fusion.114 = f32[1024,768]{0,1:T(8,128)S(1)} fusion(bf16[1024,1152]{1,0:T(8,128)(2,1)} %attend_backward.1, bf16[768,1152]{1,0:T(8,128)(2,1)} %bitcast.238), kind=kOutput, calls=%fused_computation.319 | convolution fusion | flops 1811939328 | bytes 7274496 | tf_op jit(solution)/shard_map/dot_general | solution.py:644
  269.6 5.6 %convolution_convert_fusion.3 = bf16[768,1152]{1,0:T(8,128)(2,1)} fusion(bf16[1024,1152]{1,0:T(8,128)(2,1)} %attend_backward.1, bf16[512,768]{0,1:T(8,128)(2,1)} %copy-done.70, bf16[512,768]{0,1:T(8,128)(2,1)} %copy-done.25), kind=kOutput, calls=%fused_computation.12 | convolution fusion | flops 1815969792 | bytes 5701632 | tf_op jit(solution)/shard_map/dot_general | solution.py:640
  279.6 4.9 %scatter_near.7 = (bf16[4,48,2560]{2,1,0:T(8,128)(2,1)}, f32[4,48,2560]{2,1,0:T(8,128)}) custom-call(s32[4]{0:T(128)} %pad_add_fusion.2.w, bf16[4,2,2,96,768]{4,3,2,1,0:T(8,128)(2,1)} %bitcast.188, bf16[4,2,2,48,1024]{4,3,2,1,0:T(8,128)(2,1)} %bitcast.186, bf16[4,2,48,2560]{3,2,1,0:T(8,128)(2,1)} %collective-permute-done.46.refs_2_), custom_call_target="tpu_custom_call" | custom-call | bytes 6881280 | tf_op jit(solution)/shard_map/scatter_near/pallas_call | solution.py:339
  284.5 5.7 %collective-permute-done.41.refs_2_ = bf16[4,2,48,1920]{3,2,1,0:T(8,128)(2,1)} collective-permute-done((bf16[4,2,48,1920]{3,2,1,0:T(8,128)(2,1)}, bf16[4,2,48,1920]{3,2,1,0:T(8,128)(2,1)}, u32[]{:S(2)}, u32[]{:S(2)}) %collective-permute-start.41) | collective-permute-done | bytes 1474592 | tf_op jit(solution)/shard_map/ppermute | solution.py:46
  290.2 4.5 %scatter_near.6 = (bf16[4,48,1920]{2,1,0:T(8,128)(2,1)}, f32[4,48,1920]{2,1,0:T(8,128)}) custom-call(s32[4]{0:T(128)} %pad_add_fusion.2.w, bf16[4,2,2,48,1536]{4,3,2,1,0:T(8,128)(2,1)} %bitcast.190, bf16[4,2,2,48,384]{4,3,2,1,0:T(8,128)(2,1)} %bitcast.197, bf16[4,2,48,1920]{3,2,1,0:T(8,128)(2,1)} %collective-permute-done.41.refs_2_), custom_call_target="tpu_custom_call" | custom-call | bytes 5160960 | tf_op jit(solution)/shard_map/scatter_near/pallas_call | solution.py:339
  300.0 8.0 %collective-permute-done.47.got_ref = bf16[4,48,2560]{2,1,0:T(8,128)(2,1)} collective-permute-done((bf16[4,48,2560]{2,1,0:T(8,128)(2,1)}, bf16[4,48,2560]{2,1,0:T(8,128)(2,1)}, u32[]{:S(2)}, u32[]{:S(2)}) %collective-permute-start.47) | collective-permute-done | bytes 983072 | tf_op jit(solution)/shard_map/ppermute | solution.py:46
  307.9 3.7 scatter_column.7
  317.3 3.4 scatter_near.5
  322.4 3.5 scatter_column.6
  332.6 11.6 %collective-permute-done.48 = bf16[2,48,2560]{2,1,0:T(8,128)(2,1)S(1)} collective-permute-done((bf16[2,48,2560]{2,1,0:T(8,128)(2,1)}, bf16[2,48,2560]{2,1,0:T(8,128)(2,1)S(1)}, u32[]{:S(2)}, u32[]{:S(2)}) %collective-permute-start.48) | collective-permute-done | bytes 491552 | tf_op jit(solution)/shard_map/ppermute | solution.py:46
  359.7 5.4 %collective-permute-done.38 = bf16[2,48,1152]{2,1,0:T(8,128)(2,1)S(1)} collective-permute-done((bf16[2,48,1152]{2,1,0:T(8,128)(2,1)}, bf16[2,48,1152]{2,1,0:T(8,128)(2,1)S(1)}, u32[]{:S(2)}, u32[]{:S(2)}) %collective-permute-start.38) | collective-permute-done | bytes 221216 | tf_op jit(solution)/shard_map/ppermute | solution.py:46
  388.3 3.3 collective-permute-done.53
  (483 shorter events, 178.3 us)
Async XLA Ops:
  4.6 30.0 %collective-permute-start.11 = (bf16[24,2944]{1,0:T(8,128)(2,1)S(1)}, bf16[24,2944]{1,0:T(8,128)(2,1)S(1)}, u32[]{:S(2)}, u32[]{:S(2)}) collective-permute-start(bf16[24,2944]{1,0:T(8,128)(2,1)S(1)} %fusion.54), channel_id=1, source_target_pairs={{0,1},{1,0},{2,3},{3,2},{4,5},{5,4},{6,7},{7,6},{8,9},{9,8},{10,11... | collective-permute-start | bytes 423944 | tf_op jit(solution)/shard_map/ppermute | solution.py:46
  6.4 29.6 %collective-permute-start = (bf16[256,768]{1,0:T(8,128)(2,1)S(1)}, bf16[256,768]{1,0:T(8,128)(2,1)S(1)}, u32[]{:S(2)}, u32[]{:S(2)}) collective-permute-start(bf16[256,768]{1,0:T(8,128)(2,1)S(1)} %get-tuple-element.157), channel_id=1, source_target_pairs={{0,2},{1,3},{2,0},{3,1},{4,6},{5,7},{6,4},{7,5},{8,10},{9,11},{10,... | collective-permute-start | bytes 1179656 | tf_op jit(solution)/shard_map/ppermute | solution.py:46
  16.8 16.2 %collective-permute-start.4 = (bf16[2,48,1664]{2,1,0:T(8,128)(2,1)S(1)}, bf16[2,48,1664]{2,1,0:T(8,128)(2,1)S(1)}, u32[]{:S(2)}, u32[]{:S(2)}) collective-permute-start(bf16[2,48,1664]{2,1,0:T(8,128)(2,1)S(1)} %pad_maximum_fusion.19), channel_id=1, source_target_pairs={{0,16},{1,17},{2,18},{3,19},{4,20},{5,21},{6,22},{7,23},{8,24},{9,... | collective-permute-start | bytes 958472 | tf_op jit(solution)/shard_map/ppermute | solution.py:46
  33.0 14.8 %collective-permute-start.5 = (bf16[4,48,1664]{2,1,0:T(8,128)(2,1)S(1)}, bf16[4,48,1664]{2,1,0:T(8,128)(2,1)}, u32[]{:S(2)}, u32[]{:S(2)}) collective-permute-start(bf16[4,48,1664]{2,1,0:T(8,128)(2,1)S(1)} %pad_maximum_fusion.16.refs_0_), channel_id=1, source_target_pairs={{0,4},{1,3},{2,6},{3,1},{4,0},{5,7},{6,2},{7,5},{8,12},{9,11},{10,... | collective-permute-start | bytes 1916936 | tf_op jit(solution)/shard_map/ppermute | solution.py:46
  36.1 28.2 %collective-permute-start.1 = (bf16[512,768]{1,0:T(8,128)(2,1)S(1)}, bf16[512,768]{1,0:T(8,128)(2,1)}, u32[]{:S(2)}, u32[]{:S(2)}) collective-permute-start(bf16[512,768]{1,0:T(8,128)(2,1)S(1)} %pad_maximum_fusion.12), channel_id=1, source_target_pairs={{0,1},{1,0},{2,3},{3,2},{4,5},{5,4},{6,7},{7,6},{8,9},{9,8},{10,11... | collective-permute-start | bytes 2359304 | tf_op jit(solution)/shard_map/ppermute | solution.py:46
  36.2 24.1 %collective-permute-start.6 = (bf16[4,48,1664]{2,1,0:T(8,128)(2,1)S(1)}, bf16[4,48,1664]{2,1,0:T(8,128)(2,1)}, u32[]{:S(2)}, u32[]{:S(2)}) collective-permute-start(bf16[4,48,1664]{2,1,0:T(8,128)(2,1)S(1)} %pad_maximum_fusion.16.refs_0_), channel_id=1, source_target_pairs={{0,2},{1,5},{2,0},{3,7},{4,6},{5,1},{6,4},{7,3},{8,10},{9,13},{10,... | collective-permute-start | bytes 1916936 | tf_op jit(solution)/shard_map/ppermute | solution.py:46
  41.1 17.3 %collective-permute-start.13 = (bf16[2,48,1920]{2,1,0:T(8,128)(2,1)}, bf16[2,48,1920]{2,1,0:T(8,128)(2,1)}, u32[]{:S(2)}, u32[]{:S(2)}) collective-permute-start(bf16[2,48,1920]{2,1,0:T(8,128)(2,1)} %pad_maximum_fusion.18), channel_id=1, source_target_pairs={{0,16},{1,17},{2,18},{3,19},{4,20},{5,21},{6,22},{7,23},{8,24},{9,... | collective-permute-start | bytes 1105928 | tf_op jit(solution)/shard_map/ppermute | solution.py:46
  67.6 16.0 %collective-permute-start.14 = (bf16[4,48,1920]{2,1,0:T(8,128)(2,1)S(1)}, bf16[4,48,1920]{2,1,0:T(8,128)(2,1)}, u32[]{:S(2)}, u32[]{:S(2)}) collective-permute-start(bf16[4,48,1920]{2,1,0:T(8,128)(2,1)S(1)} %pad_maximum_fusion.13.refs_0_), channel_id=1, source_target_pairs={{0,4},{1,3},{2,6},{3,1},{4,0},{5,7},{6,2},{7,5},{8,12},{9,11},{10,... | collective-permute-start | bytes 2211848 | tf_op jit(solution)/shard_map/ppermute | solution.py:46
  71.0 25.9 %collective-permute-start.20 = (bf16[2,48,2560]{2,1,0:T(8,128)(2,1)}, bf16[2,48,2560]{2,1,0:T(8,128)(2,1)}, u32[]{:S(2)}, u32[]{:S(2)}) collective-permute-start(bf16[2,48,2560]{2,1,0:T(8,128)(2,1)} %pad_maximum_fusion.17), channel_id=1, source_target_pairs={{0,16},{1,17},{2,18},{3,19},{4,20},{5,21},{6,22},{7,23},{8,24},{9,... | collective-permute-start | bytes 1474568 | tf_op jit(solution)/shard_map/ppermute | solution.py:46
  79.1 20.0 %collective-permute-start.9 = (bf16[512,768]{0,1:T(8,128)(2,1)S(1)}, bf16[512,768]{0,1:T(8,128)(2,1)S(1)}, u32[]{:S(2)}, u32[]{:S(2)}) collective-permute-start(bf16[512,768]{0,1:T(8,128)(2,1)S(1)} %add_convert_fusion.1), channel_id=1, source_target_pairs={{0,1},{1,0},{2,3},{3,2},{4,5},{5,4},{6,7},{7,6},{8,9},{9,8},{10,11... | collective-permute-start | bytes 2359304 | tf_op jit(solution)/shard_map/ppermute | solution.py:46
  81.2 47.4 %collective-permute-start.15 = (bf16[4,48,1920]{2,1,0:T(8,128)(2,1)S(1)}, bf16[4,48,1920]{2,1,0:T(8,128)(2,1)}, u32[]{:S(2)}, u32[]{:S(2)}) collective-permute-start(bf16[4,48,1920]{2,1,0:T(8,128)(2,1)S(1)} %pad_maximum_fusion.13.refs_0_), channel_id=1, source_target_pairs={{0,2},{1,5},{2,0},{3,7},{4,6},{5,1},{6,4},{7,3},{8,10},{9,13},{10,... | collective-permute-start | bytes 2211848 | tf_op jit(solution)/shard_map/ppermute | solution.py:46
  83.6 45.0 %collective-permute-start.16 = (bf16[4,48,1920]{2,1,0:T(8,128)(2,1)}, bf16[4,48,1920]{2,1,0:T(8,128)(2,1)}, u32[]{:S(2)}, u32[]{:S(2)}) collective-permute-start(bf16[4,48,1920]{2,1,0:T(8,128)(2,1)} %collective-permute-done.14.refs_1_), channel_id=1, source_target_pairs={{0,2},{1,5},{2,0},{3,7},{4,6},{5,1},{6,4},{7,3},{8,10},{9,13},{10,... | collective-permute-start | bytes 2211848 | tf_op jit(solution)/shard_map/ppermute | solution.py:46
  99.0 36.6 %collective-permute-start.21 = (bf16[4,48,2560]{2,1,0:T(8,128)(2,1)}, bf16[4,48,2560]{2,1,0:T(8,128)(2,1)}, u32[]{:S(2)}, u32[]{:S(2)}) collective-permute-start(bf16[4,48,2560]{2,1,0:T(8,128)(2,1)} %pad_maximum_fusion.11.refs_0_), channel_id=1, source_target_pairs={{0,4},{1,3},{2,6},{3,1},{4,0},{5,7},{6,2},{7,5},{8,12},{9,11},{10,... | collective-permute-start | bytes 2949128 | tf_op jit(solution)/shard_map/ppermute | solution.py:46
  133.0 15.0 %collective-permute-start.22 = (bf16[4,48,2560]{2,1,0:T(8,128)(2,1)}, bf16[4,48,2560]{2,1,0:T(8,128)(2,1)}, u32[]{:S(2)}, u32[]{:S(2)}) collective-permute-start(bf16[4,48,2560]{2,1,0:T(8,128)(2,1)} %pad_maximum_fusion.11.refs_0_), channel_id=1, source_target_pairs={{0,2},{1,5},{2,0},{3,7},{4,6},{5,1},{6,4},{7,3},{8,10},{9,13},{10,... | collective-permute-start | bytes 2949128 | tf_op jit(solution)/shard_map/ppermute | solution.py:46
  135.5 22.9 %collective-permute-start.23 = (bf16[4,48,2560]{2,1,0:T(8,128)(2,1)}, bf16[4,48,2560]{2,1,0:T(8,128)(2,1)}, u32[]{:S(2)}, u32[]{:S(2)}) collective-permute-start(bf16[4,48,2560]{2,1,0:T(8,128)(2,1)} %collective-permute-done.21.refs_1_), channel_id=1, source_target_pairs={{0,2},{1,5},{2,0},{3,7},{4,6},{5,1},{6,4},{7,3},{8,10},{9,13},{10,... | collective-permute-start | bytes 2949128 | tf_op jit(solution)/shard_map/ppermute | solution.py:46
  141.8 20.9 %collective-permute-start.18 = (bf16[512,768]{0,1:T(8,128)(2,1)}, bf16[512,768]{0,1:T(8,128)(2,1)}, u32[]{:S(2)}, u32[]{:S(2)}) collective-permute-start(bf16[512,768]{0,1:T(8,128)(2,1)} %add_convert_fusion), channel_id=1, source_target_pairs={{0,1},{1,0},{2,3},{3,2},{4,5},{5,4},{6,7},{7,6},{8,9},{9,8},{10,11... | collective-permute-start | bytes 2359304 | tf_op jit(solution)/shard_map/ppermute | solution.py:46
  212.0 17.0 %collective-permute-start.29 = (bf16[512,768]{0,1:T(8,128)(2,1)}, bf16[512,768]{0,1:T(8,128)(2,1)S(1)}, u32[]{:S(2)}, u32[]{:S(2)}) collective-permute-start(bf16[512,768]{0,1:T(8,128)(2,1)} %get-tuple-element.141), channel_id=1, source_target_pairs={{0,1},{1,0},{2,3},{3,2},{4,5},{5,4},{6,7},{7,6},{8,9},{9,8},{10,11... | collective-permute-start | bytes 2359304 | tf_op jit(solution)/shard_map/ppermute | solution.py:46
  220.7 58.9 %collective-permute-start.46 = (bf16[4,2,48,2560]{3,2,1,0:T(8,128)(2,1)}, bf16[4,2,48,2560]{3,2,1,0:T(8,128)(2,1)}, u32[]{:S(2)}, u32[]{:S(2)}) collective-permute-start(bf16[4,2,48,2560]{3,2,1,0:T(8,128)(2,1)} %scatter_give.7), channel_id=1, source_target_pairs={{0,2},{1,5},{2,0},{3,7},{4,6},{5,1},{6,4},{7,3},{8,10},{9,13},{10,... | collective-permute-start | bytes 5898248 | tf_op jit(solution)/shard_map/ppermute | solution.py:46
  262.5 32.1 %collective-permute-start.30 = (f32[512,768]{0,1:T(8,128)S(1)}, f32[512,768]{0,1:T(8,128)}, u32[]{:S(2)}, u32[]{:S(2)}) collective-permute-start(f32[512,768]{0,1:T(8,128)S(1)} %slice.276), channel_id=1, source_target_pairs={{0,1},{1,0},{2,3},{3,2},{4,5},{5,4},{6,7},{7,6},{8,9},{9,8},{10,11... | collective-permute-start | bytes 4718600 | tf_op jit(solution)/shard_map/ppermute | solution.py:46
  269.0 21.2 %collective-permute-start.41 = (bf16[4,2,48,1920]{3,2,1,0:T(8,128)(2,1)}, bf16[4,2,48,1920]{3,2,1,0:T(8,128)(2,1)}, u32[]{:S(2)}, u32[]{:S(2)}) collective-permute-start(bf16[4,2,48,1920]{3,2,1,0:T(8,128)(2,1)} %scatter_give.6), channel_id=1, source_target_pairs={{0,2},{1,5},{2,0},{3,7},{4,6},{5,1},{6,4},{7,3},{8,10},{9,13},{10,... | collective-permute-start | bytes 4423688 | tf_op jit(solution)/shard_map/ppermute | solution.py:46
  277.8 39.5 %collective-permute-start.36 = (bf16[4,2,48,1152]{3,2,1,0:T(8,128)(2,1)}, bf16[4,2,48,1152]{3,2,1,0:T(8,128)(2,1)}, u32[]{:S(2)}, u32[]{:S(2)}) collective-permute-start(bf16[4,2,48,1152]{3,2,1,0:T(8,128)(2,1)} %scatter_give.5), channel_id=1, source_target_pairs={{0,2},{1,5},{2,0},{3,7},{4,6},{5,1},{6,4},{7,3},{8,10},{9,13},{10,... | collective-permute-start | bytes 2654216 | tf_op jit(solution)/shard_map/ppermute | solution.py:46
  284.5 23.5 %collective-permute-start.47 = (bf16[4,48,2560]{2,1,0:T(8,128)(2,1)}, bf16[4,48,2560]{2,1,0:T(8,128)(2,1)}, u32[]{:S(2)}, u32[]{:S(2)}) collective-permute-start(bf16[4,48,2560]{2,1,0:T(8,128)(2,1)} %get-tuple-element.88), channel_id=1, source_target_pairs={{0,4},{1,3},{2,6},{3,1},{4,0},{5,7},{6,2},{7,5},{8,12},{9,11},{10,... | collective-permute-start | bytes 2949128 | tf_op jit(solution)/shard_map/ppermute | solution.py:46
  294.6 27.7 %collective-permute-start.42 = (bf16[4,48,1920]{2,1,0:T(8,128)(2,1)}, bf16[4,48,1920]{2,1,0:T(8,128)(2,1)}, u32[]{:S(2)}, u32[]{:S(2)}) collective-permute-start(bf16[4,48,1920]{2,1,0:T(8,128)(2,1)} %get-tuple-element.81), channel_id=1, source_target_pairs={{0,4},{1,3},{2,6},{3,1},{4,0},{5,7},{6,2},{7,5},{8,12},{9,11},{10,... | collective-permute-start | bytes 2211848 | tf_op jit(solution)/shard_map/ppermute | solution.py:46
  298.7 13.0 %collective-permute-start.31 = (bf16[512,384]{0,1:T(8,128)(2,1)S(1)}, bf16[512,384]{0,1:T(8,128)(2,1)S(1)}, u32[]{:S(2)}, u32[]{:S(2)}) collective-permute-start(bf16[512,384]{0,1:T(8,128)(2,1)S(1)} %get-tuple-element.153), channel_id=1, source_target_pairs={{0,1},{1,0},{2,3},{3,2},{4,5},{5,4},{6,7},{7,6},{8,9},{9,8},{10,11... | collective-permute-start | bytes 1179656 | tf_op jit(solution)/shard_map/ppermute | solution.py:46
  311.7 32.6 %collective-permute-start.48 = (bf16[2,48,2560]{2,1,0:T(8,128)(2,1)}, bf16[2,48,2560]{2,1,0:T(8,128)(2,1)S(1)}, u32[]{:S(2)}, u32[]{:S(2)}) collective-permute-start(bf16[2,48,2560]{2,1,0:T(8,128)(2,1)} %get-tuple-element.91), channel_id=1, source_target_pairs={{0,16},{1,17},{2,18},{3,19},{4,20},{5,21},{6,22},{7,23},{8,24},{9,... | collective-permute-start | bytes 1474568 | tf_op jit(solution)/shard_map/ppermute | solution.py:46
  320.7 24.4 %collective-permute-start.37 = (bf16[4,48,1152]{2,1,0:T(8,128)(2,1)}, bf16[4,48,1152]{2,1,0:T(8,128)(2,1)S(1)}, u32[]{:S(2)}, u32[]{:S(2)}) collective-permute-start(bf16[4,48,1152]{2,1,0:T(8,128)(2,1)} %get-tuple-element.76), channel_id=1, source_target_pairs={{0,4},{1,3},{2,6},{3,1},{4,0},{5,7},{6,2},{7,5},{8,12},{9,11},{10,... | collective-permute-start | bytes 1327112 | tf_op jit(solution)/shard_map/ppermute | solution.py:46
  325.8 28.3 %collective-permute-start.43 = (bf16[2,48,1920]{2,1,0:T(8,128)(2,1)}, bf16[2,48,1920]{2,1,0:T(8,128)(2,1)S(1)}, u32[]{:S(2)}, u32[]{:S(2)}) collective-permute-start(bf16[2,48,1920]{2,1,0:T(8,128)(2,1)} %get-tuple-element.84), channel_id=1, source_target_pairs={{0,16},{1,17},{2,18},{3,19},{4,20},{5,21},{6,22},{7,23},{8,24},{9,... | collective-permute-start | bytes 1105928 | tf_op jit(solution)/shard_map/ppermute | solution.py:46
  332.3 18.7 %collective-permute-start.33 = (bf16[4,48,512]{2,1,0:T(8,128)(2,1)}, bf16[4,48,512]{2,1,0:T(8,128)(2,1)}, u32[]{:S(2)}, u32[]{:S(2)}) collective-permute-start(bf16[4,48,512]{2,1,0:T(8,128)(2,1)} %get-tuple-element.71), channel_id=1, source_target_pairs={{0,4},{1,3},{2,6},{3,1},{4,0},{5,7},{6,2},{7,5},{8,12},{9,11},{10,... | collective-permute-start | bytes 589832 | tf_op jit(solution)/shard_map/ppermute | solution.py:46
  345.1 13.6 %collective-permute-start.49 = (bf16[48,2560]{1,0:T(8,128)(2,1)}, bf16[48,2560]{1,0:T(8,128)(2,1)S(1)}, u32[]{:S(2)}, u32[]{:S(2)}) collective-permute-start(bf16[48,2560]{1,0:T(8,128)(2,1)} %fusion.45), channel_id=1, source_target_pairs={{0,8},{1,9},{2,10},{3,11},{4,12},{5,13},{6,14},{7,15},{8,0},{9,1},... | collective-permute-start | bytes 737288 | tf_op jit(solution)/shard_map/ppermute | solution.py:46
  348.7 16.4 %collective-permute-start.38 = (bf16[2,48,1152]{2,1,0:T(8,128)(2,1)}, bf16[2,48,1152]{2,1,0:T(8,128)(2,1)S(1)}, u32[]{:S(2)}, u32[]{:S(2)}) collective-permute-start(bf16[2,48,1152]{2,1,0:T(8,128)(2,1)} %get-tuple-element.78), channel_id=1, source_target_pairs={{0,16},{1,17},{2,18},{3,19},{4,20},{5,21},{6,22},{7,23},{8,24},{9,... | collective-permute-start | bytes 663560 | tf_op jit(solution)/shard_map/ppermute | solution.py:46
  353.4 12.8 %collective-permute-start.34 = (bf16[2,48,512]{2,1,0:T(8,128)(2,1)}, bf16[2,48,512]{2,1,0:T(8,128)(2,1)S(1)}, u32[]{:S(2)}, u32[]{:S(2)}) collective-permute-start(bf16[2,48,512]{2,1,0:T(8,128)(2,1)} %get-tuple-element.73), channel_id=1, source_target_pairs={{0,16},{1,17},{2,18},{3,19},{4,20},{5,21},{6,22},{7,23},{8,24},{9,... | collective-permute-start | bytes 294920 | tf_op jit(solution)/shard_map/ppermute | solution.py:46
  354.2 17.7 %collective-permute-start.44 = (bf16[48,1920]{1,0:T(8,128)(2,1)S(1)}, bf16[48,1920]{1,0:T(8,128)(2,1)S(1)}, u32[]{:S(2)}, u32[]{:S(2)}) collective-permute-start(bf16[48,1920]{1,0:T(8,128)(2,1)S(1)} %fusion.51), channel_id=1, source_target_pairs={{0,8},{1,9},{2,10},{3,11},{4,12},{5,13},{6,14},{7,15},{8,0},{9,1},... | collective-permute-start | bytes 552968 | tf_op jit(solution)/shard_map/ppermute | solution.py:46
  (103 other events, 809.9 us)

commit v3 on v2

--- a/solution.py
+++ b/solution.py
@@ -166,19 +166,35 @@
     )(jnp.concatenate([jnp.stack([z]), places]).astype(jnp.int32), *pieces)
 
 
-def gather_column(unit):
-    pair = jnp.stack([unit, exchange(unit, along_z(1))])
-    return jnp.concatenate([pair, exchange(pair, along_z(2))], 0)
-
-
-def gather_plane(own, plan, widths):
+def gather_planes(units, plans):
     z, x, y, c = spot()
-    near = exchange(own, across_first)
-    side = exchange(own, across_second)
-    far = exchange(near, across_second)
     places = jnp.stack([x, y, x ^ (1 - c), y ^ c, x ^ c, y ^ (1 - c), x ^ 1, y ^ 1])
-    shapes = [(own.shape[0], 2, 2) + w for w in widths]
-    return assemble([own, near, side, far], places, z, plan, shapes), near
+    others = [exchange(units[0], along_z(1))]
+    others += [exchange(after(u, others[0]), along_z(1)) for u in units[1:]]
+    columns = [jnp.stack([u, o]) for u, o in zip(units, others)]
+
+    def finish(n, own, near, *waits):
+        side = exchange(own, across_second)
+        far = exchange(after(near, *waits), across_second)
+        plan, widths = plans[n]
+        shapes = [(own.shape[0], 2, 2) + w for w in widths]
+        return assemble([own, near, side, far], places, z, plan, shapes)
+
+    owns, nears, last = [], [], ()
+    for n in range(2):
+        other = exchange(after(columns[n], *last), along_z(2))
+        owns.append(jnp.concatenate([columns[n], after(other, *others)], 0))
+        nears.append(exchange(owns[n], across_first))
+        last = (owns[n],)
+    weights = finish(0, owns[0], nears[0], owns[1]) + finish(1, owns[1], nears[1])
+    third = exchange(after(columns[2], *last), along_z(2))
+
+    def later(value):
+        own = jnp.concatenate([columns[2], after(third, value)], 0)
+        near = exchange(own, across_first)
+        return finish(2, own, near), near
+
+    return weights, others[0], (nears[1], third), later
 
 
 def gather_weights(embedder, attend, merger, expand, shrink, readout, vectors):
@@ -209,33 +225,35 @@
     shrink = jnp.concatenate([shrink[: 2 * rows], shrink[2 * rows :]], 1)
 
     tall_rows = 2 * rows
-    unit = jnp.concatenate([front[:, :HALF], vec, front[:, HALF + 128 :]], 1)
-    own = gather_column(unit)
-    (emb, vec, att), near = gather_plane(
-        own,
-        [(0, 0, 0), (1, 0, HALF), (2, 0, HALF + 128)],
-        [(tall_rows, HALF), (tall_rows, 128), (tall_rows, 3 * HALF)],
-    )
-    own = gather_column(after(back[:, : 5 * HALF], own))
-    (mer, exp), _ = gather_plane(
-        own, [(0, 0, 0), (1, 0, HALF)], [(tall_rows, HALF), (tall_rows, 4 * HALF)]
-    )
-    unit = jnp.concatenate([shrink, back[:, 5 * HALF :]], 1)
-    own = gather_column(after(unit, own, near))
-    (shr, rea), _ = gather_plane(
-        own,
-        [(0, 0, 0), (0, tall_rows, D), (1, 0, 2 * D)],
-        [(tall_shrink, D), (tall_rows, wide)],
-    )
-    vec = vec.reshape(chips, 2 * rows, 128)[:, :tall, : 2 * thin].transpose(1, 0, 2)
+    units = [
+        jnp.concatenate([front[:, :HALF], vec, front[:, HALF + 128 :]], 1),
+        back[:, : 5 * HALF],
+        jnp.concatenate([shrink, back[:, 5 * HALF :]], 1),
+    ]
+    plans = [
+        (
+            [(0, 0, 0), (1, 0, HALF), (2, 0, HALF + 128)],
+            [(tall_rows, HALF), (tall_rows, 128), (tall_rows, 3 * HALF)],
+        ),
+        ([(0, 0, 0), (1, 0, HALF)], [(tall_rows, HALF), (tall_rows, 4 * HALF)]),
+        ([(0, 0, 0), (0, tall_rows, D), (1, 0, 2 * D)], [(tall_shrink, D), (tall_rows, wide)]),
+    ]
+    (emb, vec, att, mer, exp), first, cover, later = gather_planes(units, plans)
+
+    def later_weights(value):
+        (shr, rea), near = later(value)
+        return shr.reshape(-1, D), rea.reshape(-1, wide), near
+
+    vec = vec.reshape(chips, tall_rows, 128)[:, :tall, : 2 * thin].transpose(1, 0, 2)
     return (
         emb.reshape(-1, HALF),
         att.reshape(-1, 3 * HALF),
         mer.reshape(-1, HALF),
         exp.reshape(-1, 4 * HALF),
-        shr.reshape(-1, D),
-        rea.reshape(-1, wide),
         vec.reshape(tall, -1),
+        first,
+        cover,
+        later_weights,
     )
 
 
@@ -253,9 +271,14 @@
         half_of(whole_of(attend[0], 0), 3, c),
         half_of(whole_of(merger[0], 0), 1, c),
         half_of(whole_of(expand[0], 0), chips, c),
-        at(shrink, c, 1).reshape(-1, D),
-        pad_lanes(at(whole_of(readout, 1), c, 0), wide),
         whole_of(vectors, 1),
+        c,
+        (c,),
+        lambda value: (
+            at(shrink, c, 1).reshape(-1, D),
+            pad_lanes(at(whole_of(readout, 1), c, 0), wide),
+            c,
+        ),
     )
 
 
@@ -310,11 +333,11 @@
         cost_estimate=cost(0, 8 * depth * rows * lanes),
         name="scatter_give",
     )(position(), *grads)
-    return grads, rows, exchange(give, across_second)
+    return grads, rows, exchange(give, across_second), give
 
 
 def scatter_near(state, *others):
-    grads, rows, got = state
+    grads, rows, got, _ = state
     depth, count = grads[0].shape[0], len(grads)
     plan, lanes = lane_plan(grads, rows)
 
@@ -469,8 +492,14 @@
     return value.astype(F32).T.astype(BF)
 
 
-def attend_forward(q_ref, k_ref, v_ref, qm_ref, km_ref, out_ref, exact_ref, lse_ref, keys, values):
+def chunks_of(count):
+    size = 256 if count % 256 == 0 else count
+    return [slice(start, start + size) for start in range(0, count, size)]
+
+
+def attend_forward(q_ref, k_ref, v_ref, qm_ref, km_ref, out_ref, exact_ref, lse_ref, keys, values, raws):
     lane = lax.broadcasted_iota(jnp.int32, (1, 2 * HD), 1) // HD
+    chunks = chunks_of(k_ref.shape[0])
 
     @pl.when(pl.program_id(1) == 0)
     def _():
@@ -479,16 +508,25 @@
         values[...] = turned(v_ref[...])
 
     query = q_ref[...] * jnp.asarray(SCALE, BF)
-    parts = []
+    tops, parts = [], []
     for h in range(2):
-        raw = dot_keys(keys[h], jnp.where(lane == h, query, qm_ref[...]))
-        top = jnp.max(raw, 0, keepdims=True)
-        heavy = jnp.exp(raw - top)
-        mass = jnp.sum(heavy, 0, keepdims=True)
-        shares = (heavy * (1.0 / mass)).astype(BF)
-        part = jnp.dot(values[...], shares, preferred_element_type=F32)
-        parts.append(part[HD * h : HD * (h + 1)])
-        lse_ref[0, h : h + 1, :] = top + jnp.log(mass)
+        query_h = jnp.where(lane == h, query, qm_ref[...])
+        top = None
+        for chunk in chunks:
+            raw = dot_keys(keys[h, chunk, :], query_h)
+            raws[h, chunk, :] = raw
+            high = jnp.max(raw, 0, keepdims=True)
+            top = high if top is None else jnp.maximum(top, high)
+        tops.append(top)
+    for h in range(2):
+        mass, part = 0.0, 0.0
+        for chunk in chunks:
+            heavy = jnp.exp(raws[h, chunk, :] - tops[h])
+            mass = mass + jnp.sum(heavy, 0, keepdims=True)
+            side = values[HD * h : HD * (h + 1), chunk]
+            part = part + jnp.dot(side, heavy.astype(BF), preferred_element_type=F32)
+        parts.append(part * (1.0 / mass))
+        lse_ref[0, h : h + 1, :] = tops[h] + jnp.log(mass)
     mixed = jnp.concatenate(parts, 0).T
     exact_ref[...] = mixed
     out_ref[...] = mixed.astype(BF)
@@ -510,16 +548,24 @@
     query = q_ref[...] * jnp.asarray(SCALE, BF)
     grad = do_ref[...]
     spreads = (grad.astype(F32) * exact_ref[...]).T
+    of_head = []
+    for h in range(2):
+        zero = jnp.zeros_like(query)
+        of_head.append(
+            (
+                jnp.where(lane == h, query, qm_ref[...]),
+                jnp.where(lane == h, query, zero),
+                jnp.where(lane == h, grad, zero),
+                jnp.sum(spreads[HD * h : HD * (h + 1)], 0, keepdims=True),
+                lse_ref[0, h : h + 1, :],
+            )
+        )
     parts = []
-    for h in range(2):
-        own = slice(HD * h, HD * (h + 1))
-        grad_h = jnp.where(lane == h, grad, jnp.zeros_like(grad))
-        query_h = jnp.where(lane == h, query, jnp.zeros_like(query))
-        raw = dot_keys(keys[h], jnp.where(lane == h, query, qm_ref[...]))
-        shares = jnp.exp(raw - lse_ref[0, h : h + 1, :])
-        spread = jnp.sum(spreads[own], 0, keepdims=True)
+    for h, (query_m, query_h, grad_h, spread, lse) in enumerate(of_head):
+        shares = jnp.exp(dot_keys(keys[h], query_m) - lse)
         grad_raw = (shares * (dot_keys(v_ref[...], grad_h) - spread)).astype(BF)
-        parts.append(jnp.dot(turned_keys[...], grad_raw, preferred_element_type=F32)[own])
+        side = turned_keys[HD * h : HD * (h + 1), :]
+        parts.append(jnp.dot(side, grad_raw, preferred_element_type=F32))
         grad_keys[...] += jnp.dot(grad_raw, query_h, preferred_element_type=F32)
         grad_values[...] += jnp.dot(shares.astype(BF), grad_h, preferred_element_type=F32)
     grad_query = (jnp.concatenate(parts, 0).T * SCALE).astype(BF)
@@ -567,8 +613,12 @@
             jax.ShapeDtypeStruct((nq, HALF), F32),
             jax.ShapeDtypeStruct((PAIRS, 2, nq), F32),
         ],
-        scratch_shapes=[pltpu.VMEM((2, nk, 128), BF), pltpu.VMEM((128, nk), BF)],
-        cost_estimate=cost(8 * nq * nk * HALF * 4, 12 * nq * HALF),
+        scratch_shapes=[
+            pltpu.VMEM((2, nk, 128), BF),
+            pltpu.VMEM((128, nk), BF),
+            pltpu.VMEM((2, nk, tile), F32),
+        ],
+        cost_estimate=cost(nq * nk * HALF, nq * HALF),
         name="attend_forward",
     )(projected, around, around, mask_q, mask_k)
 
@@ -606,7 +656,7 @@
             pltpu.VMEM((nk, 128), F32),
             pltpu.VMEM((nk, 128), F32),
         ],
-        cost_estimate=cost(20 * nq * nk * HALF * 3, 12 * nq * HALF),
+        cost_estimate=cost(nq * nk * HALF, nq * HALF),
         name="attend_backward",
     )(projected, around, around, grad, exact, lse, mask_q, mask_k)
 
@@ -732,7 +782,13 @@
     classes = readout.shape[2]
     image_count = lengths.shape[0] * dp_size * IMGS
 
+    gather = gather_weights if fast else gather_plain
+    embed_w, attend_w, merger_half, expand_w, vector_w, first, cover, later_weights = gather(
+        embedder, attend, merger, expand, shrink, readout, vectors
+    )
+
     side = seq // far
+    pixels = after(pixels, first)
     pixels_got = of_bit(at(pixels, 1 - side, 0), far)
     tokens = jnp.concatenate([at(pixels, side, 0), pixels_got], 0)
     all_pixels = both_tokens(tokens)
@@ -763,10 +819,6 @@
     is_cls, is_dist = jnp.sum(hits[:IMGS], 0), jnp.sum(hits[IMGS:], 0)
     is_patch = (seg_q[: 2 * local] < IMGS).astype(F32) - is_cls - is_dist
 
-    gather = gather_weights if fast else gather_plain
-    embed_w, attend_w, merger_half, expand_w, shrink_w, readout_w, vector_w = gather(
-        embedder, attend, merger, expand, shrink, readout, vectors
-    )
     merger_w = in_core_order(core, merger_half, swap(merger_half), 1)
     vector_f = vector_w.astype(F32)
 
@@ -780,13 +832,15 @@
     projected = matmul(a, attend_w).astype(BF)
     around = row_tokens(projected)
     mixed_half, exact, lse = mix_tokens(projected, around, mask_q, mask_k)
+    mixed_half = after(mixed_half, *cover)
+    shrink_w, readout_w, near = later_weights(mixed_half)
     other = swap(mixed_half)
     count = 2 * local
     other = jnp.concatenate([other[count:], other[:count]], 0)
     mixed = in_core_order(core, mixed_half, other, 1)
     x_mid = x + matmul(mixed[:count], merger_w)
     normed = both_tokens(layer_norm(x_mid, vector_f[2], vector_f[3]).astype(BF))
-    hidden_in = matmul(normed, expand_w)
+    hidden_in = matmul(after(normed, near), expand_w)
     cdf = 0.5 * (1.0 + lax.erf(hidden_in * (0.5**0.5)))
     hidden = (hidden_in * cdf).astype(BF)
     slope = cdf + hidden_in * jnp.exp(-0.5 * hidden_in * hidden_in) * ((0.5 / jnp.pi) ** 0.5)
@@ -836,6 +890,8 @@
     if fast:
         second = scatter_give([blocks(grad_expand), blocks(grad_merger)], unit_rows)
     grad_mixed = inner(grad_attn, at(merger_w.reshape(2, HALF, D), core, 0)).astype(BF)
+    if fast:
+        grad_mixed = after(grad_mixed, second[3])
     grads = mix_back(projected, around, grad_mixed, exact, lse, mask_q, mask_k)
     if len(grads) == 1:
         grad_proj = grads[0]
@@ -843,11 +899,13 @@
         grad_proj = jnp.concatenate([grads[0]] + [row_return(g).astype(BF) for g in grads[1:]], 1)
     if fast:
         first = scatter_near(first, grad_proj)
+        grad_proj = after(grad_proj, first[0], second[2])
     grad_a = inner(grad_proj, attend_w)
     grad_attend = outer(a, grad_proj).astype(BF)
     if fast:
         third = scatter_give([blocks(grad_attend)], unit_rows)
-        second = scatter_near(second, grad_attend)
+        first = scatter_column(first, third[3])
+        second = scatter_near(second, first[0])
     grad_input, gain_one, shift_one = norm_back(x, vector_f[0], reduce_tokens(grad_a))
     grad_x = grad_mid + grad_input
     grad_patch = (grad_x * is_patch[:, None]).astype(BF)
@@ -865,7 +923,6 @@
         ]
     )
     if fast:
-        first = scatter_column(first, grad_patch)
         parts = [blocks(grad_embed)]
         fourth = scatter_give(parts + [vector_blocks(grad_vectors, parts[0])], unit_rows)
         third = scatter_near(third, grad_embed)

time: 418 us -> 392 us (0.938)
  waiting for transfers between devices: 119 us -> 86.4 us
  starting transfers between devices: 48.6 us -> 61.9 us
  Pallas kernels: 100 us -> 91.6 us
  local copies, waits for them, and re-layouts: 23.4 us -> 28.1 us
    ppermute x56, waiting for transfers between devices: 119 us -> 86.4 us  [exchange(): return lax.ppermute(value, AXES, pairs(move))]
    ppermute x56, starting transfers between devices: 48.6 us -> 61.9 us  [exchange(): return lax.ppermute(value, AXES, pairs(move))]
    pallas_call x1, Pallas kernels: 24.9 us -> 16 us  [mix_tokens(): pl.pallas_call(attend_forward, grid=(PAIRS, nq // tile), in_specs=[rows(0...]
    unnamed x173 -> x183, local copies, waits for them, and re-layouts: 7.84 us -> 12.3 us
  transfers between devices with their start and end apart: 56 -> 56, of which waited for: 26 -> 26; matrix products, arithmetic and copies ran while one was open for 19% -> 19% of each run, Pallas kernels for 24% -> 23%
where the time goes in v3:
time: 392 us; the launch traced here: 386 us
  Pallas kernels  91.6 us (23%)
  waiting for transfers between devices  86.4 us (22%)
  matrix products  64.5 us (16%)
  starting transfers between devices  61.9 us (16%)
  other arithmetic  42.6 us (11%)
  local copies, waits for them, and re-layouts  28.1 us (7%)
  between operations  11.2 us (3%)
    ppermute x56, waiting for transfers between devices, exchange(): return lax.ppermute(value, AXES, pairs(move))  86.4 us
    ppermute x56, starting transfers between devices, exchange(): return lax.ppermute(value, AXES, pairs(move))  61.9 us
    pallas_call x1, Pallas kernels, mix_back(): pl.pallas_call(partial(attend_backward, joined), grid=(PAIRS, nq // tile)...  24.1 us
    dot_general x5, matrix products, outer(): lax.dot_general(left, right, (((0,), (0,)), ((), ())), preferred_element_...  20.3 us
    dot_general x6, matrix products, matmul(): return jnp.dot(left, right, preferred_element_type=F32)  19.6 us
    dot_general x4, matrix products, inner(): lax.dot_general(grad, weight, (((1,), (1,)), ((), ())), preferred_element...  17.5 us
    pallas_call x1, Pallas kernels, mix_tokens(): pl.pallas_call(attend_forward, grid=(PAIRS, nq // tile), in_specs=[rows(0...  16 us
    pallas_call x4, Pallas kernels, scatter_near(): pl.pallas_call(body, out_shape=[jax.ShapeDtypeStruct((depth, rows, lanes)...  15.5 us
  transfers between devices with their start and end apart: 56, of which 26 were waited for; matrix products, arithmetic and copies ran while one was open for 19% of the time, Pallas kernels for 23%

profile of v3, /device:TPU:0, one launch (start us, length us, event | category | flops | bytes accessed | tf_op | source)
XLA Modules:
  0.0 386.3 jit_solution(2386938166888807995)
XLA Ops:
  12.8 4.1 %collective-permute-done.1 = bf16[48,1664]{1,0:T(8,128)(2,1)S(1)} collective-permute-done((bf16[48,1664]{1,0:T(8,128)(2,1)S(1)}, bf16[48,1664]{1,0:T(8,128)(2,1)S(1)}, u32[]{:S(2)}, u32[]{:S(2)}) %collective-permute-start.1) | collective-permute-done | bytes 159776 | tf_op jit(solution)/shard_map/ppermute | solution.py:46
  24.2 4.0 %collective-permute-done.6 = bf16[48,1920]{1,0:T(8,128)(2,1)S(1)} collective-permute-done((bf16[48,1920]{1,0:T(8,128)(2,1)S(1)}, bf16[48,1920]{1,0:T(8,128)(2,1)S(1)}, u32[]{:S(2)}, u32[]{:S(2)}) %collective-permute-start.6) | collective-permute-done | bytes 184352 | tf_op jit(solution)/shard_map/ppermute | solution.py:46
  29.0 6.1 %collective-permute-done.7 = bf16[48,2560]{1,0:T(8,128)(2,1)S(1)} collective-permute-done((bf16[48,2560]{1,0:T(8,128)(2,1)S(1)}, bf16[48,2560]{1,0:T(8,128)(2,1)S(1)}, u32[]{:S(2)}, u32[]{:S(2)}) %collective-permute-start.7) | collective-permute-done | bytes 245792 | tf_op jit(solution)/shard_map/ppermute | solution.py:46
  42.6 11.7 %collective-permute-done.10 = bf16[2,48,1920]{2,1,0:T(8,128)(2,1)} collective-permute-done((bf16[2,48,1920]{2,1,0:T(8,128)(2,1)}, bf16[2,48,1920]{2,1,0:T(8,128)(2,1)}, u32[]{:S(2)}, u32[]{:S(2)}) %collective-permute-start.10) | collective-permute-done | bytes 368672 | tf_op jit(solution)/shard_map/ppermute | solution.py:46
  57.1 8.9 %collective-permute-done.11.refs_3_ = bf16[4,48,1664]{2,1,0:T(8,128)(2,1)} collective-permute-done((bf16[4,48,1664]{2,1,0:T(8,128)(2,1)S(1)}, bf16[4,48,1664]{2,1,0:T(8,128)(2,1)}, u32[]{:S(2)}, u32[]{:S(2)}) %collective-permute-start.11) | collective-permute-done | bytes 639008 | tf_op jit(solution)/shard_map/ppermute | solution.py:46
  66.0 4.0 %assemble.3 = (bf16[4,2,2,48,384]{4,3,2,1,0:T(8,128)(2,1)}, bf16[4,2,2,48,128]{4,3,2,1,0:T(8,128)(2,1)}, bf16[4,2,2,48,1152]{4,3,2,1,0:T(8,128)(2,1)}) custom-call(s32[9]{0:T(128)} %concatenate.236.where, bf16[4,48,1664]{2,1,0:T(8,128)(2,1)} %copy-done.11, bf16[4,48,1664]{2,1,0:T(8,128)(2,1)} %copy-done.38, bf16[4,48,1664]{2,1,0:T(8,128)(2,1)} %copy-done.39, ...), custom_call_target="tpu_custom_call" | custom-call | bytes 5111808 | tf_op jit(solution)/shard_map/assemble/pallas_call | solution.py:155
  86.2 3.7 convolution_convert_fusion.q_ref.k_ref.v_ref
  89.9 16.0 %attend_forward.1 = (bf16[1024,384]{1,0:T(8,128)(2,1)}, f32[1024,384]{1,0:T(8,128)}, f32[3,2,1024]{2,1,0:T(2,128)}) custom-call(bf16[1024,1152]{1,0:T(8,128)(2,1)} %convolution_convert_fusion.q_ref.k_ref.v_ref, bf16[1024,1152]{1,0:T(8,128)(2,1)} %convolution_convert_fusion.q_ref.k_ref.v_ref, bf16[1024,1152]{1,0:T(8,128)(2,1)} %convolution_convert_fusion.q_ref.k_ref.v_ref, ...), custom_call_target="tpu_custom_call" | custom-call | flops 402653184 | bytes 393216 | tf_op jit(solution)/shard_map/attend_forward/pallas_call | solution.py:600
  106.2 3.7 assemble.4
  119.4 11.5 %collective-permute-done.21.refs_1_ = bf16[4,48,2560]{2,1,0:T(8,128)(2,1)S(1)} collective-permute-done((bf16[4,48,2560]{2,1,0:T(8,128)(2,1)S(1)}, bf16[4,48,2560]{2,1,0:T(8,128)(2,1)S(1)}, u32[]{:S(2)}, u32[]{:S(2)}) %collective-permute-start.21) | collective-permute-done | bytes 983072 | tf_op jit(solution)/shard_map/ppermute | solution.py:46
  130.9 3.1 collective-permute-start.23
  134.9 5.7 %multiply_convert_fusion = (bf16[1024,1536]{1,0:T(8,128)(2,1)}, f32[1024,1536]{1,0:T(8,128)}) fusion(bf16[1024,768]{0,1:T(8,128)(2,1)S(1)} %pad_maximum_fusion.2, bf16[768,1536]{1,0:T(8,128)(2,1)S(1)} %bitcast.233), kind=kOutput, calls=%fused_computation.7 | convolution fusion | flops 2423783424 | bytes 13369344 | tf_op jit(solution)/shard_map/dot_general | solution.py:686
  141.6 4.6 %collective-permute-done.23.refs_3_ = bf16[4,48,2560]{2,1,0:T(8,128)(2,1)} collective-permute-done((bf16[4,48,2560]{2,1,0:T(8,128)(2,1)S(1)}, bf16[4,48,2560]{2,1,0:T(8,128)(2,1)}, u32[]{:S(2)}, u32[]{:S(2)}) %collective-permute-start.23) | collective-permute-done | bytes 983072 | tf_op jit(solution)/shard_map/ppermute | solution.py:46
  146.2 4.4 %assemble.5 = (bf16[4,2,2,96,768]{4,3,2,1,0:T(8,128)(2,1)}, bf16[4,2,2,48,1024]{4,3,2,1,0:T(8,128)(2,1)}) custom-call(s32[9]{0:T(128)} %concatenate.236.where, bf16[4,48,2560]{2,1,0:T(8,128)(2,1)} %copy-done.5, bf16[4,48,2560]{2,1,0:T(8,128)(2,1)} %copy-done.24, bf16[4,48,2560]{2,1,0:T(8,128)(2,1)} %copy-done.25, ...), custom_call_target="tpu_custom_call" | custom-call | bytes 7864320 | tf_op jit(solution)/shard_map/assemble/pallas_call | solution.py:155
  150.6 5.3 %fusion.110 = f32[1024,768]{0,1:T(8,128)S(1)} fusion(bf16[1024,1536]{1,0:T(8,128)(2,1)} %get-tuple-element.212, bf16[1536,768]{1,0:T(8,128)(2,1)} %bitcast.235), kind=kOutput, calls=%fused_computation.316 | convolution fusion | flops 2415919104 | bytes 8650752 | tf_op jit(solution)/shard_map/dot_general | solution.py:686
  172.1 6.8 %fusion.5 = bf16[1024,1536]{1,0:T(8,128)(2,1)S(1)} fusion(f32[1024,1536]{1,0:T(8,128)} %get-tuple-element.213, bf16[1536,768]{1,0:T(8,128)(2,1)S(1)} %bitcast.236, bf16[512,768]{1,0:T(8,128)(2,1)S(1)} %collective-permute-done.27, bf16[512,768]{1,0:T(8,128)(2,1)S(1)} %get-tuple-element.217), kind=kOutput, calls=%fused_computation.6 | convolution fusion | flops 2434793472 | bytes 13369344 | tf_op jit(solution)/shard_map/dot_general | solution.py:694
  196.5 4.2 %convolution_convert_fusion.1 = bf16[1536,768]{1,0:T(8,128)(2,1)} fusion(bf16[1024,1536]{1,0:T(8,128)(2,1)S(1)} %copy-done.82, bf16[512,768]{1,0:T(8,128)(2,1)S(1)} %copy-done.77, bf16[512,768]{1,0:T(8,128)(2,1)S(1)} %copy-done.28), kind=kOutput, calls=%fused_computation.10 | convolution fusion | flops 2420244480 | bytes 7077888 | tf_op jit(solution)/shard_map/dot_general | solution.py:690
  200.7 3.3 scatter_give.5
  205.9 5.7 %convolution_convert_fusion.2 = bf16[768,1536]{1,0:T(8,128)(2,1)} fusion(bf16[1024,1536]{1,0:T(8,128)(2,1)} %copy-done.83, bf16[512,768]{0,1:T(8,128)(2,1)S(1)} %copy-done.34, bf16[512,768]{0,1:T(8,128)(2,1)S(1)} %copy-done.9), kind=kOutput, calls=%fused_computation.11 | convolution fusion | flops 2420244480 | bytes 7077888 | tf_op jit(solution)/shard_map/dot_general | solution.py:690
  218.5 3.7 convolution_convert_fusion.5.do_ref
  222.2 24.1 %attend_backward.1 = bf16[1024,1152]{1,0:T(8,128)(2,1)} custom-call(bf16[1024,1152]{1,0:T(8,128)(2,1)} %convolution_convert_fusion.q_ref.k_ref.v_ref, bf16[1024,1152]{1,0:T(8,128)(2,1)} %convolution_convert_fusion.q_ref.k_ref.v_ref, bf16[1024,1152]{1,0:T(8,128)(2,1)} %convolution_convert_fusion.q_ref.k_ref.v_ref, ...), custom_call_target="tpu_custom_call" | custom-call | flops 402653184 | bytes 393216 | tf_op jit(solution)/shard_map/attend_backward/pallas_call | solution.py:638
  246.3 4.9 %scatter_near.4 = (bf16[4,48,2560]{2,1,0:T(8,128)(2,1)}, f32[4,48,2560]{2,1,0:T(8,128)}) custom-call(s32[4]{0:T(128)} %pad_add_fusion.2.w, bf16[4,2,2,96,768]{4,3,2,1,0:T(8,128)(2,1)} %bitcast.191, bf16[4,2,2,48,1024]{4,3,2,1,0:T(8,128)(2,1)} %bitcast.189, bf16[4,2,48,2560]{3,2,1,0:T(8,128)(2,1)} %collective-permute-done.30.refs_2_), custom_call_target="tpu_custom_call" | custom-call | bytes 6881280 | tf_op jit(solution)/shard_map/scatter_near/pallas_call | solution.py:362
  252.3 4.4 %fusion.112 = f32[1024,768]{0,1:T(8,128)S(1)} fusion(bf16[1024,1152]{1,0:T(8,128)(2,1)} %attend_backward.1, bf16[768,1152]{1,0:T(8,128)(2,1)} %bitcast.237), kind=kOutput, calls=%fused_computation.318 | convolution fusion | flops 1811939328 | bytes 7274496 | tf_op jit(solution)/shard_map/dot_general | solution.py:694
  261.1 5.6 %convolution_convert_fusion.3 = bf16[768,1152]{1,0:T(8,128)(2,1)} fusion(bf16[1024,1152]{1,0:T(8,128)(2,1)} %attend_backward.1, bf16[512,768]{0,1:T(8,128)(2,1)} %copy-done.75, bf16[512,768]{0,1:T(8,128)(2,1)} %copy-done.32), kind=kOutput, calls=%fused_computation.12 | convolution fusion | flops 1815969792 | bytes 5701632 | tf_op jit(solution)/shard_map/dot_general | solution.py:690
  273.5 3.8 scatter_column.6
  277.3 4.4 %scatter_near.7 = (bf16[4,48,1920]{2,1,0:T(8,128)(2,1)}, f32[4,48,1920]{2,1,0:T(8,128)}) custom-call(s32[4]{0:T(128)} %pad_add_fusion.2.w, bf16[4,2,2,48,1536]{4,3,2,1,0:T(8,128)(2,1)} %bitcast.193, bf16[4,2,2,48,384]{4,3,2,1,0:T(8,128)(2,1)} %bitcast.200, bf16[4,2,48,1920]{3,2,1,0:T(8,128)(2,1)} %copy-done.16), custom_call_target="tpu_custom_call" | custom-call | bytes 5160960 | tf_op jit(solution)/shard_map/scatter_near/pallas_call | solution.py:362
  295.8 3.4 collective-permute-start.34
  299.1 3.4 scatter_column.7
  305.3 3.4 scatter_near.6
  331.8 5.3 %collective-permute-done.40 = bf16[2,48,1152]{2,1,0:T(8,128)(2,1)S(1)} collective-permute-done((bf16[2,48,1152]{2,1,0:T(8,128)(2,1)}, bf16[2,48,1152]{2,1,0:T(8,128)(2,1)S(1)}, u32[]{:S(2)}, u32[]{:S(2)}) %collective-permute-start.40) | collective-permute-done | bytes 221216 | tf_op jit(solution)/shard_map/ppermute | solution.py:46
  360.0 4.2 %collective-permute-start.53 = (f32[1,2]{1,0:T(1,128)S(1)}, f32[1,2]{1,0:T(1,128)S(1)}, u32[]{:S(2)}, u32[]{:S(2)}) collective-permute-start(f32[1,2]{1,0:T(1,128)S(1)} %fusion.131), channel_id=1, source_target_pairs={{0,4},{1,5},{2,6},{3,7},{4,0},{5,1},{6,2},{7,3},{8,12},{9,13},{10,... | collective-permute-start | bytes 32 | tf_op jit(solution)/shard_map/ppermute | solution.py:46
  370.7 3.1 collective-permute-done.55
  (494 shorter events, 184.6 us)
Async XLA Ops:
  16.9 11.2 %collective-permute-start.6 = (bf16[48,1920]{1,0:T(8,128)(2,1)S(1)}, bf16[48,1920]{1,0:T(8,128)(2,1)S(1)}, u32[]{:S(2)}, u32[]{:S(2)}) collective-permute-start(bf16[48,1920]{1,0:T(8,128)(2,1)S(1)} %get-tuple-element.70), channel_id=1, source_target_pairs={{0,8},{1,9},{2,10},{3,11},{4,12},{5,13},{6,14},{7,15},{8,0},{9,1},... | collective-permute-start | bytes 552968 | tf_op jit(solution)/shard_map/ppermute | solution.py:46
  18.7 16.4 %collective-permute-start.4 = (bf16[2,48,1664]{2,1,0:T(8,128)(2,1)S(1)}, bf16[2,48,1664]{2,1,0:T(8,128)(2,1)S(1)}, u32[]{:S(2)}, u32[]{:S(2)}) collective-permute-start(bf16[2,48,1664]{2,1,0:T(8,128)(2,1)S(1)} %pad_maximum_fusion.17), channel_id=1, source_target_pairs={{0,16},{1,17},{2,18},{3,19},{4,20},{5,21},{6,22},{7,23},{8,24},{9,... | collective-permute-start | bytes 958472 | tf_op jit(solution)/shard_map/ppermute | solution.py:46
  21.4 13.7 %collective-permute-start.7 = (bf16[48,2560]{1,0:T(8,128)(2,1)S(1)}, bf16[48,2560]{1,0:T(8,128)(2,1)S(1)}, u32[]{:S(2)}, u32[]{:S(2)}) collective-permute-start(bf16[48,2560]{1,0:T(8,128)(2,1)S(1)} %get-tuple-element.71), channel_id=1, source_target_pairs={{0,8},{1,9},{2,10},{3,11},{4,12},{5,13},{6,14},{7,15},{8,0},{9,1},... | collective-permute-start | bytes 737288 | tf_op jit(solution)/shard_map/ppermute | solution.py:46
  22.6 19.0 %collective-permute-start.2 = (bf16[256,768]{1,0:T(8,128)(2,1)}, bf16[256,768]{1,0:T(8,128)(2,1)S(1)}, u32[]{:S(2)}, u32[]{:S(2)}) collective-permute-start(bf16[256,768]{1,0:T(8,128)(2,1)} %get-tuple-element.179), channel_id=1, source_target_pairs={{0,2},{1,3},{2,0},{3,1},{4,6},{5,7},{6,4},{7,5},{8,10},{9,11},{10,... | collective-permute-start | bytes 1179656 | tf_op jit(solution)/shard_map/ppermute | solution.py:46
  35.2 20.2 %collective-permute-start.8 = (bf16[4,48,1664]{2,1,0:T(8,128)(2,1)S(1)}, bf16[4,48,1664]{2,1,0:T(8,128)(2,1)S(1)}, u32[]{:S(2)}, u32[]{:S(2)}) collective-permute-start(bf16[4,48,1664]{2,1,0:T(8,128)(2,1)S(1)} %pad_maximum_fusion.14.refs_0_), channel_id=1, source_target_pairs={{0,4},{1,3},{2,6},{3,1},{4,0},{5,7},{6,2},{7,5},{8,12},{9,11},{10,... | collective-permute-start | bytes 1916936 | tf_op jit(solution)/shard_map/ppermute | solution.py:46
  36.6 17.7 %collective-permute-start.10 = (bf16[2,48,1920]{2,1,0:T(8,128)(2,1)}, bf16[2,48,1920]{2,1,0:T(8,128)(2,1)}, u32[]{:S(2)}, u32[]{:S(2)}) collective-permute-start(bf16[2,48,1920]{2,1,0:T(8,128)(2,1)} %pad_maximum_fusion.16), channel_id=1, source_target_pairs={{0,16},{1,17},{2,18},{3,19},{4,20},{5,21},{6,22},{7,23},{8,24},{9,... | collective-permute-start | bytes 1105928 | tf_op jit(solution)/shard_map/ppermute | solution.py:46
  40.1 16.2 %collective-permute-start.9 = (bf16[4,48,1664]{2,1,0:T(8,128)(2,1)S(1)}, bf16[4,48,1664]{2,1,0:T(8,128)(2,1)S(1)}, u32[]{:S(2)}, u32[]{:S(2)}) collective-permute-start(bf16[4,48,1664]{2,1,0:T(8,128)(2,1)S(1)} %pad_maximum_fusion.14.refs_0_), channel_id=1, source_target_pairs={{0,2},{1,5},{2,0},{3,7},{4,6},{5,1},{6,4},{7,3},{8,10},{9,13},{10,... | collective-permute-start | bytes 1916936 | tf_op jit(solution)/shard_map/ppermute | solution.py:46
  42.6 27.5 %collective-permute-start.3 = (bf16[512,768]{1,0:T(8,128)(2,1)}, bf16[512,768]{1,0:T(8,128)(2,1)}, u32[]{:S(2)}, u32[]{:S(2)}) collective-permute-start(bf16[512,768]{1,0:T(8,128)(2,1)} %pad_maximum_fusion.10), channel_id=1, source_target_pairs={{0,1},{1,0},{2,3},{3,2},{4,5},{5,4},{6,7},{7,6},{8,9},{9,8},{10,11... | collective-permute-start | bytes 2359304 | tf_op jit(solution)/shard_map/ppermute | solution.py:46
  73.0 11.8 %collective-permute-start.14 = (bf16[4,48,1920]{2,1,0:T(8,128)(2,1)S(1)}, bf16[4,48,1920]{2,1,0:T(8,128)(2,1)}, u32[]{:S(2)}, u32[]{:S(2)}) collective-permute-start(bf16[4,48,1920]{2,1,0:T(8,128)(2,1)S(1)} %pad_maximum_fusion.11.refs_0_), channel_id=1, source_target_pairs={{0,4},{1,3},{2,6},{3,1},{4,0},{5,7},{6,2},{7,5},{8,12},{9,11},{10,... | collective-permute-start | bytes 2211848 | tf_op jit(solution)/shard_map/ppermute | solution.py:46
  80.4 25.5 %collective-permute-start.15 = (bf16[2,48,2560]{2,1,0:T(8,128)(2,1)S(1)}, bf16[2,48,2560]{2,1,0:T(8,128)(2,1)}, u32[]{:S(2)}, u32[]{:S(2)}) collective-permute-start(bf16[2,48,2560]{2,1,0:T(8,128)(2,1)S(1)} %pad_maximum_fusion.15), channel_id=1, source_target_pairs={{0,16},{1,17},{2,18},{3,19},{4,20},{5,21},{6,22},{7,23},{8,24},{9,... | collective-permute-start | bytes 1474568 | tf_op jit(solution)/shard_map/ppermute | solution.py:46
  81.4 24.8 %collective-permute-start.17 = (bf16[4,48,1920]{2,1,0:T(8,128)(2,1)S(1)}, bf16[4,48,1920]{2,1,0:T(8,128)(2,1)}, u32[]{:S(2)}, u32[]{:S(2)}) collective-permute-start(bf16[4,48,1920]{2,1,0:T(8,128)(2,1)S(1)} %pad_maximum_fusion.11.refs_0_), channel_id=1, source_target_pairs={{0,2},{1,5},{2,0},{3,7},{4,6},{5,1},{6,4},{7,3},{8,10},{9,13},{10,... | collective-permute-start | bytes 2211848 | tf_op jit(solution)/shard_map/ppermute | solution.py:46
  84.8 21.4 %collective-permute-start.18 = (bf16[4,48,1920]{2,1,0:T(8,128)(2,1)}, bf16[4,48,1920]{2,1,0:T(8,128)(2,1)}, u32[]{:S(2)}, u32[]{:S(2)}) collective-permute-start(bf16[4,48,1920]{2,1,0:T(8,128)(2,1)} %collective-permute-done.14.refs_1_), channel_id=1, source_target_pairs={{0,2},{1,5},{2,0},{3,7},{4,6},{5,1},{6,4},{7,3},{8,10},{9,13},{10,... | collective-permute-start | bytes 2211848 | tf_op jit(solution)/shard_map/ppermute | solution.py:46
  111.5 19.4 %collective-permute-start.21 = (bf16[4,48,2560]{2,1,0:T(8,128)(2,1)S(1)}, bf16[4,48,2560]{2,1,0:T(8,128)(2,1)S(1)}, u32[]{:S(2)}, u32[]{:S(2)}) collective-permute-start(bf16[4,48,2560]{2,1,0:T(8,128)(2,1)S(1)} %pad_maximum_fusion.9.refs_0_), channel_id=1, source_target_pairs={{0,4},{1,3},{2,6},{3,1},{4,0},{5,7},{6,2},{7,5},{8,12},{9,11},{10,... | collective-permute-start | bytes 2949128 | tf_op jit(solution)/shard_map/ppermute | solution.py:46
  117.3 16.8 %collective-permute-start.20 = (bf16[512,768]{0,1:T(8,128)(2,1)S(1)}, bf16[512,768]{0,1:T(8,128)(2,1)S(1)}, u32[]{:S(2)}, u32[]{:S(2)}) collective-permute-start(bf16[512,768]{0,1:T(8,128)(2,1)S(1)} %add_convert_fusion), channel_id=1, source_target_pairs={{0,1},{1,0},{2,3},{3,2},{4,5},{5,4},{6,7},{7,6},{8,9},{9,8},{10,11... | collective-permute-start | bytes 2359304 | tf_op jit(solution)/shard_map/ppermute | solution.py:46
  117.4 23.3 %collective-permute-start.22 = (bf16[4,48,2560]{2,1,0:T(8,128)(2,1)S(1)}, bf16[4,48,2560]{2,1,0:T(8,128)(2,1)S(1)}, u32[]{:S(2)}, u32[]{:S(2)}) collective-permute-start(bf16[4,48,2560]{2,1,0:T(8,128)(2,1)S(1)} %pad_maximum_fusion.9.refs_0_), channel_id=1, source_target_pairs={{0,2},{1,5},{2,0},{3,7},{4,6},{5,1},{6,4},{7,3},{8,10},{9,13},{10,... | collective-permute-start | bytes 2949128 | tf_op jit(solution)/shard_map/ppermute | solution.py:46
  130.9 15.3 %collective-permute-start.23 = (bf16[4,48,2560]{2,1,0:T(8,128)(2,1)S(1)}, bf16[4,48,2560]{2,1,0:T(8,128)(2,1)}, u32[]{:S(2)}, u32[]{:S(2)}) collective-permute-start(bf16[4,48,2560]{2,1,0:T(8,128)(2,1)S(1)} %collective-permute-done.21.refs_1_), channel_id=1, source_target_pairs={{0,2},{1,5},{2,0},{3,7},{4,6},{5,1},{6,4},{7,3},{8,10},{9,13},{10,... | collective-permute-start | bytes 2949128 | tf_op jit(solution)/shard_map/ppermute | solution.py:46
  195.2 16.4 %collective-permute-start.29 = (bf16[512,768]{0,1:T(8,128)(2,1)}, bf16[512,768]{0,1:T(8,128)(2,1)}, u32[]{:S(2)}, u32[]{:S(2)}) collective-permute-start(bf16[512,768]{0,1:T(8,128)(2,1)} %get-tuple-element.163), channel_id=1, source_target_pairs={{0,1},{1,0},{2,3},{3,2},{4,5},{5,4},{6,7},{7,6},{8,9},{9,8},{10,11... | collective-permute-start | bytes 2359304 | tf_op jit(solution)/shard_map/ppermute | solution.py:46
  204.0 42.3 %collective-permute-start.30 = (bf16[4,2,48,2560]{3,2,1,0:T(8,128)(2,1)}, bf16[4,2,48,2560]{3,2,1,0:T(8,128)(2,1)}, u32[]{:S(2)}, u32[]{:S(2)}) collective-permute-start(bf16[4,2,48,2560]{3,2,1,0:T(8,128)(2,1)} %scatter_give.5), channel_id=1, source_target_pairs={{0,2},{1,5},{2,0},{3,7},{4,6},{5,1},{6,4},{7,3},{8,10},{9,13},{10,... | collective-permute-start | bytes 5898248 | tf_op jit(solution)/shard_map/ppermute | solution.py:46
  218.4 32.8 %collective-permute-start.31 = (bf16[4,2,48,1920]{3,2,1,0:T(8,128)(2,1)}, bf16[4,2,48,1920]{3,2,1,0:T(8,128)(2,1)S(1)}, u32[]{:S(2)}, u32[]{:S(2)}) collective-permute-start(bf16[4,2,48,1920]{3,2,1,0:T(8,128)(2,1)} %scatter_give.4), channel_id=1, source_target_pairs={{0,2},{1,5},{2,0},{3,7},{4,6},{5,1},{6,4},{7,3},{8,10},{9,13},{10,... | collective-permute-start | bytes 4423688 | tf_op jit(solution)/shard_map/ppermute | solution.py:46
  258.5 26.1 %collective-permute-start.32 = (f32[512,768]{0,1:T(8,128)S(1)}, f32[512,768]{0,1:T(8,128)}, u32[]{:S(2)}, u32[]{:S(2)}) collective-permute-start(f32[512,768]{0,1:T(8,128)S(1)} %slice.276), channel_id=1, source_target_pairs={{0,1},{1,0},{2,3},{3,2},{4,5},{5,4},{6,7},{7,6},{8,9},{9,8},{10,11... | collective-permute-start | bytes 4718600 | tf_op jit(solution)/shard_map/ppermute | solution.py:46
  258.7 14.8 %collective-permute-start.43 = (bf16[4,48,2560]{2,1,0:T(8,128)(2,1)}, bf16[4,48,2560]{2,1,0:T(8,128)(2,1)}, u32[]{:S(2)}, u32[]{:S(2)}) collective-permute-start(bf16[4,48,2560]{2,1,0:T(8,128)(2,1)} %get-tuple-element.103), channel_id=1, source_target_pairs={{0,4},{1,3},{2,6},{3,1},{4,0},{5,7},{6,2},{7,5},{8,12},{9,11},{10,... | collective-permute-start | bytes 2949128 | tf_op jit(solution)/shard_map/ppermute | solution.py:46
  269.3 36.0 %collective-permute-start.38 = (bf16[4,2,48,1152]{3,2,1,0:T(8,128)(2,1)}, bf16[4,2,48,1152]{3,2,1,0:T(8,128)(2,1)}, u32[]{:S(2)}, u32[]{:S(2)}) collective-permute-start(bf16[4,2,48,1152]{3,2,1,0:T(8,128)(2,1)} %scatter_give.7), channel_id=1, source_target_pairs={{0,2},{1,5},{2,0},{3,7},{4,6},{5,1},{6,4},{7,3},{8,10},{9,13},{10,... | collective-permute-start | bytes 2654216 | tf_op jit(solution)/shard_map/ppermute | solution.py:46
  281.8 17.4 %collective-permute-start.44 = (bf16[4,48,1920]{2,1,0:T(8,128)(2,1)}, bf16[4,48,1920]{2,1,0:T(8,128)(2,1)}, u32[]{:S(2)}, u32[]{:S(2)}) collective-permute-start(bf16[4,48,1920]{2,1,0:T(8,128)(2,1)} %get-tuple-element.108), channel_id=1, source_target_pairs={{0,4},{1,3},{2,6},{3,1},{4,0},{5,7},{6,2},{7,5},{8,12},{9,11},{10,... | collective-permute-start | bytes 2211848 | tf_op jit(solution)/shard_map/ppermute | solution.py:46
  284.1 31.5 %collective-permute-start.48 = (bf16[2,48,2560]{2,1,0:T(8,128)(2,1)}, bf16[2,48,2560]{2,1,0:T(8,128)(2,1)}, u32[]{:S(2)}, u32[]{:S(2)}) collective-permute-start(bf16[2,48,2560]{2,1,0:T(8,128)(2,1)} %get-tuple-element.113), channel_id=1, source_target_pairs={{0,16},{1,17},{2,18},{3,19},{4,20},{5,21},{6,22},{7,23},{8,24},{9,... | collective-permute-start | bytes 1474568 | tf_op jit(solution)/shard_map/ppermute | solution.py:46
  295.8 13.0 %collective-permute-start.34 = (bf16[4,2,48,512]{3,2,1,0:T(8,128)(2,1)}, bf16[4,2,48,512]{3,2,1,0:T(8,128)(2,1)S(1)}, u32[]{:S(2)}, u32[]{:S(2)}) collective-permute-start(bf16[4,2,48,512]{3,2,1,0:T(8,128)(2,1)} %scatter_give.6), channel_id=1, source_target_pairs={{0,2},{1,5},{2,0},{3,7},{4,6},{5,1},{6,4},{7,3},{8,10},{9,13},{10,... | collective-permute-start | bytes 1179656 | tf_op jit(solution)/shard_map/ppermute | solution.py:46
  302.5 23.1 %collective-permute-start.45 = (bf16[2,48,1920]{2,1,0:T(8,128)(2,1)}, bf16[2,48,1920]{2,1,0:T(8,128)(2,1)S(1)}, u32[]{:S(2)}, u32[]{:S(2)}) collective-permute-start(bf16[2,48,1920]{2,1,0:T(8,128)(2,1)} %get-tuple-element.111), channel_id=1, source_target_pairs={{0,16},{1,17},{2,18},{3,19},{4,20},{5,21},{6,22},{7,23},{8,24},{9,... | collective-permute-start | bytes 1105928 | tf_op jit(solution)/shard_map/ppermute | solution.py:46
  312.4 10.8 %collective-permute-start.35 = (bf16[4,48,512]{2,1,0:T(8,128)(2,1)}, bf16[4,48,512]{2,1,0:T(8,128)(2,1)}, u32[]{:S(2)}, u32[]{:S(2)}) collective-permute-start(bf16[4,48,512]{2,1,0:T(8,128)(2,1)} %get-tuple-element.95), channel_id=1, source_target_pairs={{0,4},{1,3},{2,6},{3,1},{4,0},{5,7},{6,2},{7,5},{8,12},{9,11},{10,... | collective-permute-start | bytes 589832 | tf_op jit(solution)/shard_map/ppermute | solution.py:46
  317.5 13.3 %collective-permute-start.49 = (bf16[48,2560]{1,0:T(8,128)(2,1)}, bf16[48,2560]{1,0:T(8,128)(2,1)S(1)}, u32[]{:S(2)}, u32[]{:S(2)}) collective-permute-start(bf16[48,2560]{1,0:T(8,128)(2,1)} %fusion.44), channel_id=1, source_target_pairs={{0,8},{1,9},{2,10},{3,11},{4,12},{5,13},{6,14},{7,15},{8,0},{9,1},... | collective-permute-start | bytes 737288 | tf_op jit(solution)/shard_map/ppermute | solution.py:46
  321.2 15.9 %collective-permute-start.40 = (bf16[2,48,1152]{2,1,0:T(8,128)(2,1)}, bf16[2,48,1152]{2,1,0:T(8,128)(2,1)S(1)}, u32[]{:S(2)}, u32[]{:S(2)}) collective-permute-start(bf16[2,48,1152]{2,1,0:T(8,128)(2,1)} %get-tuple-element.102), channel_id=1, source_target_pairs={{0,16},{1,17},{2,18},{3,19},{4,20},{5,21},{6,22},{7,23},{8,24},{9,... | collective-permute-start | bytes 663560 | tf_op jit(solution)/shard_map/ppermute | solution.py:46
  325.7 17.4 %collective-permute-start.46 = (bf16[48,1920]{1,0:T(8,128)(2,1)S(1)}, bf16[48,1920]{1,0:T(8,128)(2,1)S(1)}, u32[]{:S(2)}, u32[]{:S(2)}) collective-permute-start(bf16[48,1920]{1,0:T(8,128)(2,1)S(1)} %fusion.50), channel_id=1, source_target_pairs={{0,8},{1,9},{2,10},{3,11},{4,12},{5,13},{6,14},{7,15},{8,0},{9,1},... | collective-permute-start | bytes 552968 | tf_op jit(solution)/shard_map/ppermute | solution.py:46
  326.9 11.3 %collective-permute-start.36 = (bf16[2,48,512]{2,1,0:T(8,128)(2,1)S(1)}, bf16[2,48,512]{2,1,0:T(8,128)(2,1)S(1)}, u32[]{:S(2)}, u32[]{:S(2)}) collective-permute-start(bf16[2,48,512]{2,1,0:T(8,128)(2,1)S(1)} %copy-done.80), channel_id=1, source_target_pairs={{0,16},{1,17},{2,18},{3,19},{4,20},{5,21},{6,22},{7,23},{8,24},{9,... | collective-permute-start | bytes 294920 | tf_op jit(solution)/shard_map/ppermute | solution.py:46
  331.0 11.5 %collective-permute-start.50 = (f32[24,1024]{1,0:T(8,128)S(1)}, f32[24,1024]{1,0:T(8,128)S(1)}, u32[]{:S(2)}, u32[]{:S(2)}) collective-permute-start(f32[24,1024]{1,0:T(8,128)S(1)} %get-tuple-element.192), channel_id=1, source_target_pairs={{0,1},{1,0},{2,3},{3,2},{4,5},{5,4},{6,7},{7,6},{8,9},{9,8},{10,11... | collective-permute-start | bytes 294920 | tf_op jit(solution)/shard_map/ppermute | solution.py:46
  (108 other events, 764.2 us)

commit v4 on v3

--- a/solution.py
+++ b/solution.py
@@ -71,11 +71,12 @@
     return (dp // 2, dp % 2, seq // 2, seq % 2)
 
 
-def total_of(value):
-    for bit in range((lax.axis_size("seq") - 1).bit_length()):
-        value = value + exchange(value, lambda d, s, bit=bit: (d, s ^ (1 << bit)))
-    for bit in range((lax.axis_size("dp") - 1).bit_length()):
-        value = value + exchange(value, lambda d, s, bit=bit: (d ^ (1 << bit), s))
+def total_of(value, beside=()):
+    hops = [(0, 1 << b) for b in range((lax.axis_size("seq") - 1).bit_length())]
+    hops += [(1 << b, 0) for b in range((lax.axis_size("dp") - 1).bit_length())]
+    for n, (of_dp, of_seq) in enumerate(hops):
+        got = exchange(value, lambda d, s: (d ^ of_dp, s ^ of_seq))
+        value = value + after(got, *beside[n : n + 1])
     return value
 
 
@@ -109,9 +110,8 @@
     return in_core_order(core, value[:count], swap(value[count:]), 1)
 
 
-def reduce_tokens(value):
-    count = value.shape[0] // 2
-    return value[:count] + swap(value[count:])
+def with_other(product):
+    return product, swap(product[product.shape[0] // 2 :])
 
 
 def cost(flops, byte_count):
@@ -415,18 +415,17 @@
     return at(halves, core, 0), swap(at(halves, 1 - core, 0))
 
 
-def first_done(state, classes):
+def first_done(unit, classes):
     core = lax.axis_index("seq") % 2
-    unit = scatter_end(state)
     shrink = jnp.concatenate([unit[:, :D], unit[:, D : 2 * D]], 0)
     mine, other = own_rows(core, unit[:, 2 * D :])
     return shrink, in_core_order(core, mine[None], other[None], 0)[:, :, :classes]
 
 
-def second_done(state, wide):
+def second_done(unit, wide):
     core = lax.axis_index("seq") % 2
     chips = lax.axis_size("dp") * lax.axis_size("seq") // 2
-    mine, other = own_rows(core, scatter_end(state))
+    mine, other = own_rows(core, unit)
     return (
         join_halves(core, mine[:, :wide], other[:, :wide], chips),
         join_halves(core, mine[:, wide:], other[:, wide:], 1),
@@ -441,20 +440,12 @@
     return vec.reshape(like.shape[:4] + (128,))
 
 
-def last_done(attend, embedder, tall, thin):
+def last_done(attend, embedder):
     core = lax.axis_index("seq") % 2
-    attend, unit = scatter_end(attend), scatter_end(embedder)
-    rows = attend.shape[0] // 2
-    pieces = unit[:tall, HALF : HALF + 2 * thin].reshape(tall, 2, thin)
-    halves = jnp.concatenate([unit[:, :HALF], attend], 1).reshape(2, rows, -1)
-    mine = at(halves, core, 0)
-    sent = jnp.pad(at(pieces, 1 - core, 1), ((0, rows - tall), (0, 128 - thin)))
-    got = swap(jnp.concatenate([at(halves, 1 - core, 0), sent], 1))
-    wide = mine.shape[1]
+    mine, other = own_rows(core, jnp.concatenate([embedder[:, :HALF], attend], 1))
     return (
-        join_halves(core, mine[:, :HALF], got[:, :HALF], 1),
-        join_halves(core, mine[:, HALF:], got[:, HALF:wide], 3),
-        at(pieces, core, 1) + got[:tall, wide : wide + thin],
+        join_halves(core, mine[:, :HALF], other[:, :HALF], 1),
+        join_halves(core, mine[:, HALF:], other[:, HALF:], 3),
     )
 
 
@@ -480,7 +471,7 @@
         spread(expand, chips),
         reduced(tall, 0),
         reduced(pair, 1)[:, :, :classes],
-        reduced(vectors, 1),
+        reduced(vectors * 0.5, 1),
     )
 
 
@@ -588,13 +579,17 @@
             outs[2][...] = grad_values[...]
 
 
+def queries_of(count):
+    return 512 if count % 512 == 0 else tile_of(count)
+
+
 def tile_of(count):
     return 256 if count % 256 == 0 else count
 
 
 def mix_tokens(projected, around, mask_q, mask_k):
     nq, nk = projected.shape[0], around.shape[0]
-    tile = tile_of(nq)
+    tile = queries_of(nq)
     rows = lambda part: pl.BlockSpec((tile, 128), lambda i, j: (j, part * PAIRS + i))
     tall = lambda part: pl.BlockSpec((nk, 128), lambda i, j: (0, part * PAIRS + i))
     return pl.pallas_call(
@@ -625,7 +620,7 @@
 
 def mix_back(projected, around, grad, exact, lse, mask_q, mask_k):
     nq, nk = projected.shape[0], around.shape[0]
-    tile, joined = tile_of(nq), nq == nk
+    tile, joined = queries_of(nq), nq == nk
     rows = lambda part: pl.BlockSpec((tile, 128), lambda i, j: (j, part * PAIRS + i))
     tall = lambda part: pl.BlockSpec((nk, 128), lambda i, j: (0, part * PAIRS + i))
     if joined:
@@ -680,6 +675,43 @@
         - unit * jnp.mean(inner_grad * unit, -1, keepdims=True)
     )
     return (back, jnp.sum(grad * unit, 0), jnp.sum(grad, 0))
+
+
+def norm_back_body(x_ref, gain_ref, mine_ref, got_ref, more_ref, kind_ref, out_ref, low_ref, sum_ref):
+    grad = mine_ref[...] + got_ref[...]
+    back, _, _ = norm_back(x_ref[...], gain_ref[...], grad)
+    unit, _ = norm_parts(x_ref[...])
+    total = more_ref[...] + back
+    out_ref[...] = total
+    low_ref[...] = (total * kind_ref[:, :1]).astype(BF)
+
+    @pl.when(pl.program_id(0) == 0)
+    def _():
+        sum_ref[...] = jnp.zeros_like(sum_ref)
+
+    rows = (grad * unit, grad, total * kind_ref[:, 1:2], total * kind_ref[:, 2:3])
+    for n, row in enumerate(rows):
+        sum_ref[n : n + 1, :] += jnp.sum(row, 0, keepdims=True)
+
+
+def norm_back_sum(x, gain, mine, got, more, kinds):
+    count = x.shape[0]
+    tile = tile_of(count)
+    rows = pl.BlockSpec((tile, D), lambda i: (i, 0))
+    return pl.pallas_call(
+        norm_back_body,
+        grid=(count // tile,),
+        in_specs=[rows, pl.BlockSpec((1, D), lambda i: (0, 0)), rows, rows, rows]
+        + [pl.BlockSpec((tile, 128), lambda i: (i, 0))],
+        out_specs=[rows, rows, pl.BlockSpec((8, D), lambda i: (0, 0))],
+        out_shape=[
+            jax.ShapeDtypeStruct((count, D), F32),
+            jax.ShapeDtypeStruct((count, D), BF),
+            jax.ShapeDtypeStruct((8, D), F32),
+        ],
+        cost_estimate=cost(0, count * D),
+        name="norm_back",
+    )(x, gain[None, :], mine, got, more, kinds)
 
 
 def matmul(left, right):
@@ -844,7 +876,8 @@
     cdf = 0.5 * (1.0 + lax.erf(hidden_in * (0.5**0.5)))
     hidden = (hidden_in * cdf).astype(BF)
     slope = cdf + hidden_in * jnp.exp(-0.5 * hidden_in * hidden_in) * ((0.5 / jnp.pi) ** 0.5)
-    x_last = x_mid + reduce_tokens(matmul(hidden, shrink_w))
+    mine, got = with_other(matmul(hidden, shrink_w))
+    x_last = x_mid + (mine[:count] + got)
 
     label_hot = (row_labels[:, None] == jnp.arange(classes, dtype=jnp.int32)).astype(F32)
     teach_log = jax.nn.log_softmax(row_teacher, -1)
@@ -880,48 +913,39 @@
         first = scatter_give(parts, unit_rows)
     grad_pre = (inner(grad_branch, shrink_w) * slope).astype(BF)
     grad_expand = outer(normed, grad_pre).astype(BF)
-    grad_normed, gain_two, shift_two = norm_back(
-        x_mid, vector_f[2], reduce_tokens(inner(grad_pre, expand_w))
-    )
-    grad_mid = grad_out + grad_normed
-    grad_attn = both_tokens(grad_mid.astype(BF))
+    mine, got = with_other(inner(grad_pre, expand_w))
+    kinds = jnp.stack([is_patch, is_cls, is_dist], 1)
+    kinds = jnp.pad(kinds, ((0, 0), (0, 125)))
+    every = jnp.ones_like(kinds)
+    grad_mid, low_mid, sums_two = norm_back_sum(x_mid, vector_f[2], mine, got, grad_out, every)
+    grad_attn = both_tokens(low_mid)
     attn_half = at(grad_attn.reshape(-1, 2, HALF), core, 1)
     grad_merger = outer(mixed, attn_half).astype(BF)
     if fast:
         second = scatter_give([blocks(grad_expand), blocks(grad_merger)], unit_rows)
     grad_mixed = inner(grad_attn, at(merger_w.reshape(2, HALF, D), core, 0)).astype(BF)
     if fast:
-        grad_mixed = after(grad_mixed, second[3])
+        first = scatter_near(first, second[3])
+        grad_mixed = after(grad_mixed, first[0])
     grads = mix_back(projected, around, grad_mixed, exact, lse, mask_q, mask_k)
     if len(grads) == 1:
         grad_proj = grads[0]
     else:
         grad_proj = jnp.concatenate([grads[0]] + [row_return(g).astype(BF) for g in grads[1:]], 1)
     if fast:
-        first = scatter_near(first, grad_proj)
-        grad_proj = after(grad_proj, first[0], second[2])
-    grad_a = inner(grad_proj, attend_w)
+        grad_proj = after(grad_proj, first[1], second[2])
+    mine, got = with_other(inner(grad_proj, attend_w))
     grad_attend = outer(a, grad_proj).astype(BF)
     if fast:
         third = scatter_give([blocks(grad_attend)], unit_rows)
         first = scatter_column(first, third[3])
         second = scatter_near(second, first[0])
-    grad_input, gain_one, shift_one = norm_back(x, vector_f[0], reduce_tokens(grad_a))
-    grad_x = grad_mid + grad_input
-    grad_patch = (grad_x * is_patch[:, None]).astype(BF)
+    _, grad_patch, sums_one = norm_back_sum(x, vector_f[0], mine, got, grad_mid, kinds)
     grad_embed = outer(all_pixels, to_columns(core, grad_patch)).astype(BF)
-    grad_vectors = jnp.stack(
-        [
-            gain_one,
-            shift_one,
-            gain_two,
-            shift_two,
-            gain_out / span,
-            shift_out / span,
-            jnp.sum(grad_x * is_cls[:, None], 0),
-            jnp.sum(grad_x * is_dist[:, None], 0),
-        ]
-    )
+    grad_vectors = jnp.concatenate(
+        [sums_one[:2], sums_two[:2], jnp.stack([gain_out, shift_out]) / span, sums_one[2:4]], 0
+    )
+    grad_vectors = grad_vectors + swap(grad_vectors)
     if fast:
         parts = [blocks(grad_embed)]
         fourth = scatter_give(parts + [vector_blocks(grad_vectors, parts[0])], unit_rows)
@@ -933,9 +957,13 @@
         fourth = scatter_column(fourth)
         second = scatter_pair(second, fourth[0])
         third, fourth = scatter_pair(third), scatter_pair(fourth)
-        sum_shrink, sum_readout = first_done(first, classes)
-        sum_expand, sum_merger = second_done(second, grad_expand.shape[1])
-        sum_embed, sum_attend, sum_vectors = last_done(third, fourth, *vectors.shape)
+        units = [scatter_end(state) for state in (first, second, third, fourth)]
+        tall, thin = vectors.shape
+        sum_vectors = at(units[3][:tall, HALF : HALF + 2 * thin].reshape(tall, 2, thin), core, 1)
+        squares_of = units[:3] + [units[3][:, :HALF], sum_vectors]
+        sum_shrink, sum_readout = first_done(units[0], classes)
+        sum_expand, sum_merger = second_done(units[1], grad_expand.shape[1])
+        sum_embed, sum_attend = last_done(units[2], units[3])
     else:
         sum_embed, sum_attend, sum_merger, sum_expand, sum_shrink, sum_readout, sum_vectors = (
             scatter_plain(
@@ -944,9 +972,12 @@
                 classes,
             )
         )
+        squares_of = [sum_embed, sum_attend, sum_merger, sum_expand, sum_shrink, sum_readout]
+        squares_of.append(sum_vectors)
     reduced = (sum_embed, sum_attend, sum_merger, sum_expand, sum_shrink, sum_readout)
-    square_sum = sum((jnp.sum(g * g) for g in reduced)) + jnp.sum(sum_vectors * sum_vectors)
-    both = total_of(jnp.stack([square_sum, loss_local])[None, :])
+    square_sum = sum((jnp.sum(g * g) for g in squares_of))
+    beside = [(sum_shrink, sum_readout), (sum_expand,), (sum_merger, sum_embed), (sum_attend,)]
+    both = total_of(jnp.stack([square_sum, loss_local])[None, :], beside)
     grad_norm = jnp.sqrt(both[0, 0])
     factor = jnp.minimum(1.0, CLIP_AT / (grad_norm + 1e-06))
 

time: 392 us -> 384 us (0.980)
  starting transfers between devices: 61.9 us -> 43.5 us
  waiting for transfers between devices: 86.4 us -> 103 us
  other arithmetic: 42.6 us -> 29.2 us
  local copies, waits for them, and re-layouts: 28.1 us -> 36.3 us
  Pallas kernels: 91.6 us -> 95.6 us
    ppermute x56 -> x57, starting transfers between devices: 61.9 us -> 43.5 us  [exchange(): return lax.ppermute(value, AXES, pairs(move))]
    ppermute x56 -> x57, waiting for transfers between devices: 86.4 us -> 103 us  [exchange(): return lax.ppermute(value, AXES, pairs(move))]
    pallas_call x0 -> x2, Pallas kernels: none -> 9.65 us  [norm_back_sum(): pl.pallas_call(norm_back_body, grid=(count // tile,), in_specs=[rows, pl....]
    reduce_sum x10 -> x5, other arithmetic: 11.1 us -> 3.31 us  [on_device(): square_sum = sum((jnp.sum(g * g) for g in squares_of))]
    unnamed x183 -> x160, local copies, waits for them, and re-layouts: 12.3 us -> 13.4 us
  transfers between devices with their start and end apart: 56 -> 57, of which waited for: 26 -> 23; matrix products, arithmetic and copies ran while one was open for 19% -> 21% of each run, Pallas kernels for 23% -> 24%
where the time goes in v4:
time: 384 us; the launch traced here: 379 us
  waiting for transfers between devices  103 us (27%)
  Pallas kernels  95.6 us (25%)
  matrix products  62.3 us (16%)
  starting transfers between devices  43.5 us (11%)
  local copies, waits for them, and re-layouts  36.3 us (9%)
  other arithmetic  29.2 us (8%)
  between operations  9.45 us (2%)
    ppermute x57, waiting for transfers between devices, exchange(): return lax.ppermute(value, AXES, pairs(move))  103 us
    ppermute x57, starting transfers between devices, exchange(): return lax.ppermute(value, AXES, pairs(move))  43.5 us
    pallas_call x1, Pallas kernels, mix_back(): pl.pallas_call(partial(attend_backward, joined), grid=(PAIRS, nq // tile)...  21.2 us
    dot_general x5, matrix products, outer(): lax.dot_general(left, right, (((0,), (0,)), ((), ())), preferred_element_...  20.6 us
    dot_general x6, matrix products, matmul(): return jnp.dot(left, right, preferred_element_type=F32)  18.2 us
    dot_general x4, matrix products, inner(): lax.dot_general(grad, weight, (((1,), (1,)), ((), ())), preferred_element...  16.6 us
    pallas_call x4, Pallas kernels, scatter_near(): pl.pallas_call(body, out_shape=[jax.ShapeDtypeStruct((depth, rows, lanes)...  15.5 us
    unnamed x160, local copies, waits for them, and re-layouts  13.4 us
  transfers between devices with their start and end apart: 57, of which 23 were waited for; matrix products, arithmetic and copies ran while one was open for 21% of the time, Pallas kernels for 24%

profile of v4, /device:TPU:0, one launch (start us, length us, event | category | flops | bytes accessed | tf_op | source)
XLA Modules:
  0.0 379.0 jit_solution(2306160268556870791)
XLA Ops:
  10.6 4.1 %collective-permute-done.1 = bf16[48,1664]{1,0:T(8,128)(2,1)S(1)} collective-permute-done((bf16[48,1664]{1,0:T(8,128)(2,1)S(1)}, bf16[48,1664]{1,0:T(8,128)(2,1)S(1)}, u32[]{:S(2)}, u32[]{:S(2)}) %collective-permute-start.1) | collective-permute-done | bytes 159776 | tf_op jit(solution)/shard_map/ppermute | solution.py:46
  22.0 4.0 %collective-permute-done.6 = bf16[48,1920]{1,0:T(8,128)(2,1)S(1)} collective-permute-done((bf16[48,1920]{1,0:T(8,128)(2,1)S(1)}, bf16[48,1920]{1,0:T(8,128)(2,1)S(1)}, u32[]{:S(2)}, u32[]{:S(2)}) %collective-permute-start.6) | collective-permute-done | bytes 184352 | tf_op jit(solution)/shard_map/ppermute | solution.py:46
  26.1 6.8 %collective-permute-done.7 = bf16[48,2560]{1,0:T(8,128)(2,1)S(1)} collective-permute-done((bf16[48,2560]{1,0:T(8,128)(2,1)S(1)}, bf16[48,2560]{1,0:T(8,128)(2,1)S(1)}, u32[]{:S(2)}, u32[]{:S(2)}) %collective-permute-start.7) | collective-permute-done | bytes 245792 | tf_op jit(solution)/shard_map/ppermute | solution.py:46
  40.4 11.5 %collective-permute-done.10 = bf16[2,48,1920]{2,1,0:T(8,128)(2,1)} collective-permute-done((bf16[2,48,1920]{2,1,0:T(8,128)(2,1)S(1)}, bf16[2,48,1920]{2,1,0:T(8,128)(2,1)}, u32[]{:S(2)}, u32[]{:S(2)}) %collective-permute-start.10) | collective-permute-done | bytes 368672 | tf_op jit(solution)/shard_map/ppermute | solution.py:46
  54.7 9.0 %collective-permute-done.11.refs_3_ = bf16[4,48,1664]{2,1,0:T(8,128)(2,1)S(1)} collective-permute-done((bf16[4,48,1664]{2,1,0:T(8,128)(2,1)}, bf16[4,48,1664]{2,1,0:T(8,128)(2,1)S(1)}, u32[]{:S(2)}, u32[]{:S(2)}) %collective-permute-start.11) | collective-permute-done | bytes 639008 | tf_op jit(solution)/shard_map/ppermute | solution.py:46
  64.6 4.1 %assemble.3 = (bf16[4,2,2,48,384]{4,3,2,1,0:T(8,128)(2,1)}, bf16[4,2,2,48,128]{4,3,2,1,0:T(8,128)(2,1)}, bf16[4,2,2,48,1152]{4,3,2,1,0:T(8,128)(2,1)}) custom-call(s32[9]{0:T(128)} %concatenate.209.where, bf16[4,48,1664]{2,1,0:T(8,128)(2,1)} %copy-done.11, bf16[4,48,1664]{2,1,0:T(8,128)(2,1)} %collective-permute-done.8.refs_1_, ...), custom_call_target="tpu_custom_call" | custom-call | bytes 5111808 | tf_op jit(solution)/shard_map/assemble/pallas_call | solution.py:155
  85.2 3.7 convolution_convert_fusion.q_ref.k_ref.v_ref
  88.9 12.6 %attend_forward.1 = (bf16[1024,384]{1,0:T(8,128)(2,1)}, f32[1024,384]{1,0:T(8,128)}, f32[3,2,1024]{2,1,0:T(2,128)}) custom-call(bf16[1024,1152]{1,0:T(8,128)(2,1)} %convolution_convert_fusion.q_ref.k_ref.v_ref, bf16[1024,1152]{1,0:T(8,128)(2,1)} %convolution_convert_fusion.q_ref.k_ref.v_ref, bf16[1024,1152]{1,0:T(8,128)(2,1)} %convolution_convert_fusion.q_ref.k_ref.v_ref, ...), custom_call_target="tpu_custom_call" | custom-call | flops 402653184 | bytes 393216 | tf_op jit(solution)/shard_map/attend_forward/pallas_call | solution.py:595
  104.6 3.7 assemble.4
  116.0 13.9 %collective-permute-done.21.refs_1_ = bf16[4,48,2560]{2,1,0:T(8,128)(2,1)S(1)} collective-permute-done((bf16[4,48,2560]{2,1,0:T(8,128)(2,1)S(1)}, bf16[4,48,2560]{2,1,0:T(8,128)(2,1)S(1)}, u32[]{:S(2)}, u32[]{:S(2)}) %collective-permute-start.21) | collective-permute-done | bytes 983072 | tf_op jit(solution)/shard_map/ppermute | solution.py:46
  131.3 5.6 %multiply_convert_fusion = (bf16[1024,1536]{1,0:T(8,128)(2,1)}, f32[1024,1536]{1,0:T(8,128)}) fusion(bf16[1024,768]{1,0:T(8,128)(2,1)S(1)} %pad_maximum_fusion.2, bf16[768,1536]{1,0:T(8,128)(2,1)S(1)} %bitcast.252), kind=kOutput, calls=%fused_computation.7 | convolution fusion | flops 2423783424 | bytes 13369344 | tf_op jit(solution)/shard_map/dot_general | solution.py:718
  137.9 6.6 %collective-permute-done.23.refs_3_ = bf16[4,48,2560]{2,1,0:T(8,128)(2,1)} collective-permute-done((bf16[4,48,2560]{2,1,0:T(8,128)(2,1)S(1)}, bf16[4,48,2560]{2,1,0:T(8,128)(2,1)}, u32[]{:S(2)}, u32[]{:S(2)}) %collective-permute-start.23) | collective-permute-done | bytes 983072 | tf_op jit(solution)/shard_map/ppermute | solution.py:46
  144.5 4.4 %assemble.5 = (bf16[4,2,2,96,768]{4,3,2,1,0:T(8,128)(2,1)}, bf16[4,2,2,48,1024]{4,3,2,1,0:T(8,128)(2,1)}) custom-call(s32[9]{0:T(128)} %concatenate.209.where, bf16[4,48,2560]{2,1,0:T(8,128)(2,1)} %copy-done.7, bf16[4,48,2560]{2,1,0:T(8,128)(2,1)} %copy-done.24, bf16[4,48,2560]{2,1,0:T(8,128)(2,1)} %copy-done.25, ...), custom_call_target="tpu_custom_call" | custom-call | bytes 7864320 | tf_op jit(solution)/shard_map/assemble/pallas_call | solution.py:155
  148.8 5.2 %fusion.110 = f32[1024,768]{1,0:T(8,128)S(1)} fusion(bf16[1024,1536]{1,0:T(8,128)(2,1)} %get-tuple-element.217, bf16[1536,768]{1,0:T(8,128)(2,1)} %bitcast.254), kind=kOutput, calls=%fused_computation.280 | convolution fusion | flops 2415919104 | bytes 8650752 | tf_op jit(solution)/shard_map/dot_general | solution.py:718
  168.9 6.6 %fusion.5 = bf16[1024,1536]{1,0:T(8,128)(2,1)S(1)} fusion(f32[1024,1536]{1,0:T(8,128)} %get-tuple-element.218, bf16[1536,768]{1,0:T(8,128)(2,1)S(1)} %bitcast.255, bf16[512,768]{1,0:T(8,128)(2,1)S(1)} %collective-permute-done.27, bf16[512,768]{1,0:T(8,128)(2,1)S(1)} %get-tuple-element.222), kind=kOutput, calls=%fused_computation.6 | convolution fusion | flops 2434793472 | bytes 13369344 | tf_op jit(solution)/shard_map/dot_general | solution.py:726
  184.2 4.0 %convolution_convert_fusion.2 = bf16[1536,768]{1,0:T(8,128)(2,1)} fusion(bf16[1024,1536]{1,0:T(8,128)(2,1)S(1)} %copy-done.74, bf16[512,768]{1,0:T(8,128)(2,1)S(1)} %collective-permute-done.27, bf16[512,768]{1,0:T(8,128)(2,1)S(1)} %get-tuple-element.222), kind=kOutput, calls=%fused_computation.11 | convolution fusion | flops 2420244480 | bytes 7077888 | tf_op jit(solution)/shard_map/dot_general | solution.py:722
  193.3 4.9 %norm_back.2 = (f32[512,768]{1,0:T(8,128)}, bf16[512,768]{1,0:T(8,128)(2,1)}, f32[8,768]{1,0:T(8,128)}) custom-call(f32[512,768]{1,0:T(8,128)} %copy-done.3, f32[1,768]{1,0:T(1,128)} %slice.217.gain_ref, f32[1024,768]{1,0:T(8,128)} %copy-done.5, f32[512,768]{1,0:T(8,128)} %collective-permute-done.28.got_ref, f32[512,768]{1,0:T(8,128)} %get-tuple-element.223.more_ref, ...), custom_call_target="tpu_custom_call" | custom-call | bytes 393216 | tf_op jit(solution)/shard_map/norm_back/pallas_call | solution.py:701
  198.9 6.0 %convolution_convert_fusion.1 = bf16[768,1536]{1,0:T(8,128)(2,1)} fusion(bf16[1024,1536]{1,0:T(8,128)(2,1)} %copy-done.73, bf16[512,768]{1,0:T(8,128)(2,1)S(1)} %copy-done.34, bf16[512,768]{1,0:T(8,128)(2,1)S(1)} %copy-done.9), kind=kOutput, calls=%fused_computation.10 | convolution fusion | flops 2420244480 | bytes 7077888 | tf_op jit(solution)/shard_map/dot_general | solution.py:722
  212.8 3.5 collective-permute-done.30.refs_2_
  216.3 4.8 %scatter_near.4 = (bf16[4,48,2560]{2,1,0:T(8,128)(2,1)}, f32[4,48,2560]{2,1,0:T(8,128)}) custom-call(s32[4]{0:T(128)} %pad_add_fusion.2.w, bf16[4,2,2,96,768]{4,3,2,1,0:T(8,128)(2,1)} %bitcast.208, bf16[4,2,2,48,1024]{4,3,2,1,0:T(8,128)(2,1)} %bitcast.206, bf16[4,2,48,2560]{3,2,1,0:T(8,128)(2,1)} %collective-permute-done.30.refs_2_), custom_call_target="tpu_custom_call" | custom-call | bytes 6881280 | tf_op jit(solution)/shard_map/scatter_near/pallas_call | solution.py:362
  225.4 21.2 %attend_backward.1 = bf16[1024,1152]{1,0:T(8,128)(2,1)} custom-call(bf16[1024,1152]{1,0:T(8,128)(2,1)} %convolution_convert_fusion.q_ref.k_ref.v_ref, bf16[1024,1152]{1,0:T(8,128)(2,1)} %convolution_convert_fusion.q_ref.k_ref.v_ref, bf16[1024,1152]{1,0:T(8,128)(2,1)} %convolution_convert_fusion.q_ref.k_ref.v_ref, ...), custom_call_target="tpu_custom_call" | custom-call | flops 402653184 | bytes 393216 | tf_op jit(solution)/shard_map/attend_backward/pallas_call | solution.py:633
  247.6 4.4 %fusion.112.mine_ref = f32[1024,768]{1,0:T(8,128)S(1)} fusion(bf16[1024,1152]{1,0:T(8,128)(2,1)} %attend_backward.1, bf16[768,1152]{1,0:T(8,128)(2,1)} %bitcast.256), kind=kOutput, calls=%fused_computation.282 | convolution fusion | flops 1811939328 | bytes 7274496 | tf_op jit(solution)/shard_map/dot_general | solution.py:726
  256.5 5.6 %convolution_convert_fusion.3 = bf16[768,1152]{1,0:T(8,128)(2,1)} fusion(bf16[1024,1152]{1,0:T(8,128)(2,1)} %attend_backward.1, bf16[512,768]{1,0:T(8,128)(2,1)} %copy-done.68, bf16[512,768]{1,0:T(8,128)(2,1)} %copy-done.32), kind=kOutput, calls=%fused_computation.12 | convolution fusion | flops 1815969792 | bytes 5701632 | tf_op jit(solution)/shard_map/dot_general | solution.py:722
  265.8 4.8 %norm_back.3 = (f32[512,768]{1,0:T(8,128)}, bf16[512,768]{1,0:T(8,128)(2,1)}, f32[8,768]{1,0:T(8,128)}) custom-call(f32[512,768]{1,0:T(8,128)} %copy-done.2, f32[1,768]{1,0:T(1,128)} %slice.211.gain_ref, f32[1024,768]{1,0:T(8,128)} %copy-done.4, f32[512,768]{1,0:T(8,128)} %collective-permute-done.33.got_ref, f32[512,768]{1,0:T(8,128)} %get-tuple-element.103.more_ref, ...), custom_call_target="tpu_custom_call" | custom-call | bytes 393216 | tf_op jit(solution)/shard_map/norm_back/pallas_call | solution.py:701
  275.7 3.7 scatter_column.6
  279.4 4.3 %scatter_near.7 = (bf16[4,48,1920]{2,1,0:T(8,128)(2,1)}, f32[4,48,1920]{2,1,0:T(8,128)}) custom-call(s32[4]{0:T(128)} %pad_add_fusion.2.w, bf16[4,2,2,48,1536]{4,3,2,1,0:T(8,128)(2,1)} %bitcast.210, bf16[4,2,2,48,384]{4,3,2,1,0:T(8,128)(2,1)} %bitcast.216, bf16[4,2,48,1920]{3,2,1,0:T(8,128)(2,1)} %collective-permute-done.32.refs_2_), custom_call_target="tpu_custom_call" | custom-call | bytes 5160960 | tf_op jit(solution)/shard_map/scatter_near/pallas_call | solution.py:362
  294.1 3.4 scatter_near.6
  299.7 3.5 scatter_column.7
  320.2 9.7 %collective-permute-done.48 = bf16[2,48,1920]{2,1,0:T(8,128)(2,1)S(1)} collective-permute-done((bf16[2,48,1920]{2,1,0:T(8,128)(2,1)}, bf16[2,48,1920]{2,1,0:T(8,128)(2,1)S(1)}, u32[]{:S(2)}, u32[]{:S(2)}) %collective-permute-start.48) | collective-permute-done | bytes 368672 | tf_op jit(solution)/shard_map/ppermute | solution.py:46
  331.0 3.8 %collective-permute-done.42 = bf16[2,48,1152]{2,1,0:T(8,128)(2,1)} collective-permute-done((bf16[2,48,1152]{2,1,0:T(8,128)(2,1)}, bf16[2,48,1152]{2,1,0:T(8,128)(2,1)}, u32[]{:S(2)}, u32[]{:S(2)}) %collective-permute-start.42) | collective-permute-done | bytes 221216 | tf_op jit(solution)/shard_map/ppermute | solution.py:46
  358.4 3.5 collective-permute-done.54
  361.9 4.5 %collective-permute-done.55 = f32[1,2]{1,0:T(1,128)S(1)} collective-permute-done((f32[1,2]{1,0:T(1,128)S(1)}, f32[1,2]{1,0:T(1,128)S(1)}, u32[]{:S(2)}, u32[]{:S(2)}) %collective-permute-start.55) | collective-permute-done | bytes 40 | tf_op jit(solution)/shard_map/ppermute | solution.py:46
  (465 shorter events, 172.0 us)
Async XLA Ops:
  16.6 16.4 %collective-permute-start.4 = (bf16[2,48,1664]{2,1,0:T(8,128)(2,1)S(1)}, bf16[2,48,1664]{2,1,0:T(8,128)(2,1)S(1)}, u32[]{:S(2)}, u32[]{:S(2)}) collective-permute-start(bf16[2,48,1664]{2,1,0:T(8,128)(2,1)S(1)} %pad_maximum_fusion.16), channel_id=1, source_target_pairs={{0,16},{1,17},{2,18},{3,19},{4,20},{5,21},{6,22},{7,23},{8,24},{9,... | collective-permute-start | bytes 958472 | tf_op jit(solution)/shard_map/ppermute | solution.py:46
  19.2 13.7 %collective-permute-start.7 = (bf16[48,2560]{1,0:T(8,128)(2,1)S(1)}, bf16[48,2560]{1,0:T(8,128)(2,1)S(1)}, u32[]{:S(2)}, u32[]{:S(2)}) collective-permute-start(bf16[48,2560]{1,0:T(8,128)(2,1)S(1)} %get-tuple-element.78), channel_id=1, source_target_pairs={{0,8},{1,9},{2,10},{3,11},{4,12},{5,13},{6,14},{7,15},{8,0},{9,1},... | collective-permute-start | bytes 737288 | tf_op jit(solution)/shard_map/ppermute | solution.py:46
  20.5 18.9 %collective-permute-start.2 = (bf16[256,768]{1,0:T(8,128)(2,1)}, bf16[256,768]{1,0:T(8,128)(2,1)S(1)}, u32[]{:S(2)}, u32[]{:S(2)}) collective-permute-start(bf16[256,768]{1,0:T(8,128)(2,1)} %get-tuple-element.176), channel_id=1, source_target_pairs={{0,2},{1,3},{2,0},{3,1},{4,6},{5,7},{6,4},{7,5},{8,10},{9,11},{10,... | collective-permute-start | bytes 1179656 | tf_op jit(solution)/shard_map/ppermute | solution.py:46
  33.0 20.0 %collective-permute-start.8 = (bf16[4,48,1664]{2,1,0:T(8,128)(2,1)S(1)}, bf16[4,48,1664]{2,1,0:T(8,128)(2,1)}, u32[]{:S(2)}, u32[]{:S(2)}) collective-permute-start(bf16[4,48,1664]{2,1,0:T(8,128)(2,1)S(1)} %pad_maximum_fusion.13.refs_0_), channel_id=1, source_target_pairs={{0,4},{1,3},{2,6},{3,1},{4,0},{5,7},{6,2},{7,5},{8,12},{9,11},{10,... | collective-permute-start | bytes 1916936 | tf_op jit(solution)/shard_map/ppermute | solution.py:46
  34.4 17.5 %collective-permute-start.10 = (bf16[2,48,1920]{2,1,0:T(8,128)(2,1)S(1)}, bf16[2,48,1920]{2,1,0:T(8,128)(2,1)}, u32[]{:S(2)}, u32[]{:S(2)}) collective-permute-start(bf16[2,48,1920]{2,1,0:T(8,128)(2,1)S(1)} %pad_maximum_fusion.15), channel_id=1, source_target_pairs={{0,16},{1,17},{2,18},{3,19},{4,20},{5,21},{6,22},{7,23},{8,24},{9,... | collective-permute-start | bytes 1105928 | tf_op jit(solution)/shard_map/ppermute | solution.py:46
  37.9 16.0 %collective-permute-start.9 = (bf16[4,48,1664]{2,1,0:T(8,128)(2,1)S(1)}, bf16[4,48,1664]{2,1,0:T(8,128)(2,1)S(1)}, u32[]{:S(2)}, u32[]{:S(2)}) collective-permute-start(bf16[4,48,1664]{2,1,0:T(8,128)(2,1)S(1)} %pad_maximum_fusion.13.refs_0_), channel_id=1, source_target_pairs={{0,2},{1,5},{2,0},{3,7},{4,6},{5,1},{6,4},{7,3},{8,10},{9,13},{10,... | collective-permute-start | bytes 1916936 | tf_op jit(solution)/shard_map/ppermute | solution.py:46
  40.4 28.3 %collective-permute-start.3 = (bf16[512,768]{1,0:T(8,128)(2,1)}, bf16[512,768]{1,0:T(8,128)(2,1)}, u32[]{:S(2)}, u32[]{:S(2)}) collective-permute-start(bf16[512,768]{1,0:T(8,128)(2,1)} %pad_maximum_fusion.9), channel_id=1, source_target_pairs={{0,1},{1,0},{2,3},{3,2},{4,5},{5,4},{6,7},{7,6},{8,9},{9,8},{10,11... | collective-permute-start | bytes 2359304 | tf_op jit(solution)/shard_map/ppermute | solution.py:46
  71.9 11.8 %collective-permute-start.14 = (bf16[4,48,1920]{2,1,0:T(8,128)(2,1)S(1)}, bf16[4,48,1920]{2,1,0:T(8,128)(2,1)}, u32[]{:S(2)}, u32[]{:S(2)}) collective-permute-start(bf16[4,48,1920]{2,1,0:T(8,128)(2,1)S(1)} %pad_maximum_fusion.10.refs_0_), channel_id=1, source_target_pairs={{0,4},{1,3},{2,6},{3,1},{4,0},{5,7},{6,2},{7,5},{8,12},{9,11},{10,... | collective-permute-start | bytes 2211848 | tf_op jit(solution)/shard_map/ppermute | solution.py:46
  79.2 25.2 %collective-permute-start.15 = (bf16[2,48,2560]{2,1,0:T(8,128)(2,1)S(1)}, bf16[2,48,2560]{2,1,0:T(8,128)(2,1)}, u32[]{:S(2)}, u32[]{:S(2)}) collective-permute-start(bf16[2,48,2560]{2,1,0:T(8,128)(2,1)S(1)} %pad_maximum_fusion.14), channel_id=1, source_target_pairs={{0,16},{1,17},{2,18},{3,19},{4,20},{5,21},{6,22},{7,23},{8,24},{9,... | collective-permute-start | bytes 1474568 | tf_op jit(solution)/shard_map/ppermute | solution.py:46
  80.2 24.4 %collective-permute-start.17 = (bf16[4,48,1920]{2,1,0:T(8,128)(2,1)S(1)}, bf16[4,48,1920]{2,1,0:T(8,128)(2,1)}, u32[]{:S(2)}, u32[]{:S(2)}) collective-permute-start(bf16[4,48,1920]{2,1,0:T(8,128)(2,1)S(1)} %pad_maximum_fusion.10.refs_0_), channel_id=1, source_target_pairs={{0,2},{1,5},{2,0},{3,7},{4,6},{5,1},{6,4},{7,3},{8,10},{9,13},{10,... | collective-permute-start | bytes 2211848 | tf_op jit(solution)/shard_map/ppermute | solution.py:46
  83.7 20.9 %collective-permute-start.18 = (bf16[4,48,1920]{2,1,0:T(8,128)(2,1)}, bf16[4,48,1920]{2,1,0:T(8,128)(2,1)}, u32[]{:S(2)}, u32[]{:S(2)}) collective-permute-start(bf16[4,48,1920]{2,1,0:T(8,128)(2,1)} %collective-permute-done.14.refs_1_), channel_id=1, source_target_pairs={{0,2},{1,5},{2,0},{3,7},{4,6},{5,1},{6,4},{7,3},{8,10},{9,13},{10,... | collective-permute-start | bytes 2211848 | tf_op jit(solution)/shard_map/ppermute | solution.py:46
  110.0 19.9 %collective-permute-start.21 = (bf16[4,48,2560]{2,1,0:T(8,128)(2,1)S(1)}, bf16[4,48,2560]{2,1,0:T(8,128)(2,1)S(1)}, u32[]{:S(2)}, u32[]{:S(2)}) collective-permute-start(bf16[4,48,2560]{2,1,0:T(8,128)(2,1)S(1)} %pad_maximum_fusion.8.refs_0_), channel_id=1, source_target_pairs={{0,4},{1,3},{2,6},{3,1},{4,0},{5,7},{6,2},{7,5},{8,12},{9,11},{10,... | collective-permute-start | bytes 2949128 | tf_op jit(solution)/shard_map/ppermute | solution.py:46
  115.3 15.1 %collective-permute-start.20 = (bf16[512,768]{1,0:T(8,128)(2,1)S(1)}, bf16[512,768]{1,0:T(8,128)(2,1)S(1)}, u32[]{:S(2)}, u32[]{:S(2)}) collective-permute-start(bf16[512,768]{1,0:T(8,128)(2,1)S(1)} %add_convert_fusion), channel_id=1, source_target_pairs={{0,1},{1,0},{2,3},{3,2},{4,5},{5,4},{6,7},{7,6},{8,9},{9,8},{10,11... | collective-permute-start | bytes 2359304 | tf_op jit(solution)/shard_map/ppermute | solution.py:46
  115.4 21.5 %collective-permute-start.22 = (bf16[4,48,2560]{2,1,0:T(8,128)(2,1)S(1)}, bf16[4,48,2560]{2,1,0:T(8,128)(2,1)S(1)}, u32[]{:S(2)}, u32[]{:S(2)}) collective-permute-start(bf16[4,48,2560]{2,1,0:T(8,128)(2,1)S(1)} %pad_maximum_fusion.8.refs_0_), channel_id=1, source_target_pairs={{0,2},{1,5},{2,0},{3,7},{4,6},{5,1},{6,4},{7,3},{8,10},{9,13},{10,... | collective-permute-start | bytes 2949128 | tf_op jit(solution)/shard_map/ppermute | solution.py:46
  129.9 14.6 %collective-permute-start.23 = (bf16[4,48,2560]{2,1,0:T(8,128)(2,1)S(1)}, bf16[4,48,2560]{2,1,0:T(8,128)(2,1)}, u32[]{:S(2)}, u32[]{:S(2)}) collective-permute-start(bf16[4,48,2560]{2,1,0:T(8,128)(2,1)S(1)} %collective-permute-done.21.refs_1_), channel_id=1, source_target_pairs={{0,2},{1,5},{2,0},{3,7},{4,6},{5,1},{6,4},{7,3},{8,10},{9,13},{10,... | collective-permute-start | bytes 2949128 | tf_op jit(solution)/shard_map/ppermute | solution.py:46
  180.6 12.0 %collective-permute-start.28 = (f32[512,768]{1,0:T(8,128)}, f32[512,768]{1,0:T(8,128)}, u32[]{:S(2)}, u32[]{:S(2)}) collective-permute-start(f32[512,768]{1,0:T(8,128)} %slice.280), channel_id=1, source_target_pairs={{0,1},{1,0},{2,3},{3,2},{4,5},{5,4},{6,7},{7,6},{8,9},{9,8},{10,11... | collective-permute-start | bytes 4718600 | tf_op jit(solution)/shard_map/ppermute | solution.py:46
  191.4 24.9 %collective-permute-start.30 = (bf16[4,2,48,2560]{3,2,1,0:T(8,128)(2,1)}, bf16[4,2,48,2560]{3,2,1,0:T(8,128)(2,1)}, u32[]{:S(2)}, u32[]{:S(2)}) collective-permute-start(bf16[4,2,48,2560]{3,2,1,0:T(8,128)(2,1)} %scatter_give.4), channel_id=1, source_target_pairs={{0,2},{1,5},{2,0},{3,7},{4,6},{5,1},{6,4},{7,3},{8,10},{9,13},{10,... | collective-permute-start | bytes 5898248 | tf_op jit(solution)/shard_map/ppermute | solution.py:46
  211.9 35.7 %collective-permute-start.32 = (bf16[4,2,48,1920]{3,2,1,0:T(8,128)(2,1)}, bf16[4,2,48,1920]{3,2,1,0:T(8,128)(2,1)}, u32[]{:S(2)}, u32[]{:S(2)}) collective-permute-start(bf16[4,2,48,1920]{3,2,1,0:T(8,128)(2,1)} %scatter_give.5), channel_id=1, source_target_pairs={{0,2},{1,5},{2,0},{3,7},{4,6},{5,1},{6,4},{7,3},{8,10},{9,13},{10,... | collective-permute-start | bytes 4423688 | tf_op jit(solution)/shard_map/ppermute | solution.py:46
  221.2 25.5 %collective-permute-start.31 = (bf16[4,48,2560]{2,1,0:T(8,128)(2,1)}, bf16[4,48,2560]{2,1,0:T(8,128)(2,1)S(1)}, u32[]{:S(2)}, u32[]{:S(2)}) collective-permute-start(bf16[4,48,2560]{2,1,0:T(8,128)(2,1)} %get-tuple-element.101), channel_id=1, source_target_pairs={{0,4},{1,3},{2,6},{3,1},{4,0},{5,7},{6,2},{7,5},{8,12},{9,11},{10,... | collective-permute-start | bytes 2949128 | tf_op jit(solution)/shard_map/ppermute | solution.py:46
  254.2 11.6 %collective-permute-start.33 = (f32[512,768]{1,0:T(8,128)}, f32[512,768]{1,0:T(8,128)}, u32[]{:S(2)}, u32[]{:S(2)}) collective-permute-start(f32[512,768]{1,0:T(8,128)} %slice.281), channel_id=1, source_target_pairs={{0,1},{1,0},{2,3},{3,2},{4,5},{5,4},{6,7},{7,6},{8,9},{9,8},{10,11... | collective-permute-start | bytes 4718600 | tf_op jit(solution)/shard_map/ppermute | solution.py:46
  265.3 27.9 %collective-permute-start.40 = (bf16[4,2,48,1152]{3,2,1,0:T(8,128)(2,1)}, bf16[4,2,48,1152]{3,2,1,0:T(8,128)(2,1)S(1)}, u32[]{:S(2)}, u32[]{:S(2)}) collective-permute-start(bf16[4,2,48,1152]{3,2,1,0:T(8,128)(2,1)} %scatter_give.7), channel_id=1, source_target_pairs={{0,2},{1,5},{2,0},{3,7},{4,6},{5,1},{6,4},{7,3},{8,10},{9,13},{10,... | collective-permute-start | bytes 2654216 | tf_op jit(solution)/shard_map/ppermute | solution.py:46
  275.1 11.5 %collective-permute-start.34 = (bf16[512,384]{1,0:T(8,128)(2,1)}, bf16[512,384]{1,0:T(8,128)(2,1)}, u32[]{:S(2)}, u32[]{:S(2)}) collective-permute-start(bf16[512,384]{1,0:T(8,128)(2,1)} %bitcast.198), channel_id=1, source_target_pairs={{0,1},{1,0},{2,3},{3,2},{4,5},{5,4},{6,7},{7,6},{8,9},{9,8},{10,11... | collective-permute-start | bytes 1179656 | tf_op jit(solution)/shard_map/ppermute | solution.py:46
  279.4 31.2 %collective-permute-start.45 = (bf16[2,48,2560]{2,1,0:T(8,128)(2,1)}, bf16[2,48,2560]{2,1,0:T(8,128)(2,1)}, u32[]{:S(2)}, u32[]{:S(2)}) collective-permute-start(bf16[2,48,2560]{2,1,0:T(8,128)(2,1)} %get-tuple-element.118), channel_id=1, source_target_pairs={{0,16},{1,17},{2,18},{3,19},{4,20},{5,21},{6,22},{7,23},{8,24},{9,... | collective-permute-start | bytes 1474568 | tf_op jit(solution)/shard_map/ppermute | solution.py:46
  283.6 15.2 %collective-permute-start.47 = (bf16[4,48,1920]{2,1,0:T(8,128)(2,1)}, bf16[4,48,1920]{2,1,0:T(8,128)(2,1)S(1)}, u32[]{:S(2)}, u32[]{:S(2)}) collective-permute-start(bf16[4,48,1920]{2,1,0:T(8,128)(2,1)} %get-tuple-element.122), channel_id=1, source_target_pairs={{0,4},{1,3},{2,6},{3,1},{4,0},{5,7},{6,2},{7,5},{8,12},{9,11},{10,... | collective-permute-start | bytes 2211848 | tf_op jit(solution)/shard_map/ppermute | solution.py:46
  292.2 13.9 %collective-permute-start.36 = (bf16[4,2,48,512]{3,2,1,0:T(8,128)(2,1)}, bf16[4,2,48,512]{3,2,1,0:T(8,128)(2,1)S(1)}, u32[]{:S(2)}, u32[]{:S(2)}) collective-permute-start(bf16[4,2,48,512]{3,2,1,0:T(8,128)(2,1)} %scatter_give.6), channel_id=1, source_target_pairs={{0,2},{1,5},{2,0},{3,7},{4,6},{5,1},{6,4},{7,3},{8,10},{9,13},{10,... | collective-permute-start | bytes 1179656 | tf_op jit(solution)/shard_map/ppermute | solution.py:46
  297.5 14.3 %collective-permute-start.41 = (bf16[4,48,1152]{2,1,0:T(8,128)(2,1)}, bf16[4,48,1152]{2,1,0:T(8,128)(2,1)}, u32[]{:S(2)}, u32[]{:S(2)}) collective-permute-start(bf16[4,48,1152]{2,1,0:T(8,128)(2,1)} %get-tuple-element.113), channel_id=1, source_target_pairs={{0,4},{1,3},{2,6},{3,1},{4,0},{5,7},{6,2},{7,5},{8,12},{9,11},{10,... | collective-permute-start | bytes 1327112 | tf_op jit(solution)/shard_map/ppermute | solution.py:46
  303.2 26.7 %collective-permute-start.48 = (bf16[2,48,1920]{2,1,0:T(8,128)(2,1)}, bf16[2,48,1920]{2,1,0:T(8,128)(2,1)S(1)}, u32[]{:S(2)}, u32[]{:S(2)}) collective-permute-start(bf16[2,48,1920]{2,1,0:T(8,128)(2,1)} %get-tuple-element.125), channel_id=1, source_target_pairs={{0,16},{1,17},{2,18},{3,19},{4,20},{5,21},{6,22},{7,23},{8,24},{9,... | collective-permute-start | bytes 1105928 | tf_op jit(solution)/shard_map/ppermute | solution.py:46
  311.8 18.4 %collective-permute-start.46 = (bf16[48,2560]{1,0:T(8,128)(2,1)S(1)}, bf16[48,2560]{1,0:T(8,128)(2,1)S(1)}, u32[]{:S(2)}, u32[]{:S(2)}) collective-permute-start(bf16[48,2560]{1,0:T(8,128)(2,1)S(1)} %fusion.42), channel_id=1, source_target_pairs={{0,8},{1,9},{2,10},{3,11},{4,12},{5,13},{6,14},{7,15},{8,0},{9,1},... | collective-permute-start | bytes 737288 | tf_op jit(solution)/shard_map/ppermute | solution.py:46
  314.8 20.0 %collective-permute-start.42 = (bf16[2,48,1152]{2,1,0:T(8,128)(2,1)}, bf16[2,48,1152]{2,1,0:T(8,128)(2,1)}, u32[]{:S(2)}, u32[]{:S(2)}) collective-permute-start(bf16[2,48,1152]{2,1,0:T(8,128)(2,1)} %get-tuple-element.115), channel_id=1, source_target_pairs={{0,16},{1,17},{2,18},{3,19},{4,20},{5,21},{6,22},{7,23},{8,24},{9,... | collective-permute-start | bytes 663560 | tf_op jit(solution)/shard_map/ppermute | solution.py:46
  318.8 17.1 %collective-permute-start.38 = (bf16[2,48,512]{2,1,0:T(8,128)(2,1)}, bf16[2,48,512]{2,1,0:T(8,128)(2,1)S(1)}, u32[]{:S(2)}, u32[]{:S(2)}) collective-permute-start(bf16[2,48,512]{2,1,0:T(8,128)(2,1)} %get-tuple-element.110), channel_id=1, source_target_pairs={{0,16},{1,17},{2,18},{3,19},{4,20},{5,21},{6,22},{7,23},{8,24},{9,... | collective-permute-start | bytes 294920 | tf_op jit(solution)/shard_map/ppermute | solution.py:46
  330.0 12.2 %collective-permute-start.49 = (bf16[48,1920]{1,0:T(8,128)(2,1)S(1)}, bf16[48,1920]{1,0:T(8,128)(2,1)S(1)}, u32[]{:S(2)}, u32[]{:S(2)}) collective-permute-start(bf16[48,1920]{1,0:T(8,128)(2,1)S(1)} %fusion.48), channel_id=1, source_target_pairs={{0,8},{1,9},{2,10},{3,11},{4,12},{5,13},{6,14},{7,15},{8,0},{9,1},... | collective-permute-start | bytes 552968 | tf_op jit(solution)/shard_map/ppermute | solution.py:46
  343.0 30.1 %collective-permute-start.56 = (f32[24,1920]{1,0:T(8,128)S(1)}, f32[24,1920]{1,0:T(8,128)S(1)}, u32[]{:S(2)}, u32[]{:S(2)}) collective-permute-start(f32[24,1920]{1,0:T(8,128)S(1)} %get-tuple-element.180), channel_id=1, source_target_pairs={{0,1},{1,0},{2,3},{3,2},{4,5},{5,4},{6,7},{7,6},{8,9},{9,8},{10,11... | collective-permute-start | bytes 552968 | tf_op jit(solution)/shard_map/ppermute | solution.py:46
  (100 other events, 909.5 us)

commit v5 on v4

--- a/solution.py
+++ b/solution.py
@@ -580,7 +580,7 @@
 
 
 def queries_of(count):
-    return 512 if count % 512 == 0 else tile_of(count)
+    return 1024 if count % 1024 == 0 else tile_of(count)
 
 
 def tile_of(count):

time: 384 us -> 383 us (level)
  no operation moved by 1% of the time
where the time goes in v5:
time: 383 us; the launch traced here: 378 us
  waiting for transfers between devices  104 us (27%)
  Pallas kernels  93.7 us (24%)
  matrix products  62.3 us (16%)
  starting transfers between devices  43.5 us (11%)
  local copies, waits for them, and re-layouts  36.3 us (9%)
  other arithmetic  29.2 us (8%)
  between operations  9.47 us (2%)
    ppermute x57, waiting for transfers between devices, exchange(): return lax.ppermute(value, AXES, pairs(move))  104 us
    ppermute x57, starting transfers between devices, exchange(): return lax.ppermute(value, AXES, pairs(move))  43.5 us
    pallas_call x1, Pallas kernels, mix_back(): pl.pallas_call(partial(attend_backward, joined), grid=(PAIRS, nq // tile)...  20.8 us
    dot_general x5, matrix products, outer(): lax.dot_general(left, right, (((0,), (0,)), ((), ())), preferred_element_...  20.6 us
    dot_general x6, matrix products, matmul(): return jnp.dot(left, right, preferred_element_type=F32)  18.2 us
    dot_general x4, matrix products, inner(): lax.dot_general(grad, weight, (((1,), (1,)), ((), ())), preferred_element...  16.6 us
    pallas_call x4, Pallas kernels, scatter_near(): pl.pallas_call(body, out_shape=[jax.ShapeDtypeStruct((depth, rows, lanes)...  15.5 us
    unnamed x160, local copies, waits for them, and re-layouts  13.4 us
  transfers between devices with their start and end apart: 57, of which 23 were waited for; matrix products, arithmetic and copies ran while one was open for 21% of the time, Pallas kernels for 24%

profile of v5, /device:TPU:0, one launch (start us, length us, event | category | flops | bytes accessed | tf_op | source)
XLA Modules:
  0.0 378.2 jit_solution(3843085843981394335)
XLA Ops:
  10.6 4.1 %collective-permute-done.1 = bf16[48,1664]{1,0:T(8,128)(2,1)S(1)} collective-permute-done((bf16[48,1664]{1,0:T(8,128)(2,1)S(1)}, bf16[48,1664]{1,0:T(8,128)(2,1)S(1)}, u32[]{:S(2)}, u32[]{:S(2)}) %collective-permute-start.1) | collective-permute-done | bytes 159776 | tf_op jit(solution)/shard_map/ppermute | solution.py:46
  22.0 4.0 %collective-permute-done.6 = bf16[48,1920]{1,0:T(8,128)(2,1)S(1)} collective-permute-done((bf16[48,1920]{1,0:T(8,128)(2,1)S(1)}, bf16[48,1920]{1,0:T(8,128)(2,1)S(1)}, u32[]{:S(2)}, u32[]{:S(2)}) %collective-permute-start.6) | collective-permute-done | bytes 184352 | tf_op jit(solution)/shard_map/ppermute | solution.py:46
  26.1 6.8 %collective-permute-done.7 = bf16[48,2560]{1,0:T(8,128)(2,1)S(1)} collective-permute-done((bf16[48,2560]{1,0:T(8,128)(2,1)S(1)}, bf16[48,2560]{1,0:T(8,128)(2,1)S(1)}, u32[]{:S(2)}, u32[]{:S(2)}) %collective-permute-start.7) | collective-permute-done | bytes 245792 | tf_op jit(solution)/shard_map/ppermute | solution.py:46
  40.4 11.5 %collective-permute-done.10 = bf16[2,48,1920]{2,1,0:T(8,128)(2,1)} collective-permute-done((bf16[2,48,1920]{2,1,0:T(8,128)(2,1)S(1)}, bf16[2,48,1920]{2,1,0:T(8,128)(2,1)}, u32[]{:S(2)}, u32[]{:S(2)}) %collective-permute-start.10) | collective-permute-done | bytes 368672 | tf_op jit(solution)/shard_map/ppermute | solution.py:46
  54.7 9.0 %collective-permute-done.11.refs_3_ = bf16[4,48,1664]{2,1,0:T(8,128)(2,1)S(1)} collective-permute-done((bf16[4,48,1664]{2,1,0:T(8,128)(2,1)}, bf16[4,48,1664]{2,1,0:T(8,128)(2,1)S(1)}, u32[]{:S(2)}, u32[]{:S(2)}) %collective-permute-start.11) | collective-permute-done | bytes 639008 | tf_op jit(solution)/shard_map/ppermute | solution.py:46
  64.6 4.1 %assemble.3 = (bf16[4,2,2,48,384]{4,3,2,1,0:T(8,128)(2,1)}, bf16[4,2,2,48,128]{4,3,2,1,0:T(8,128)(2,1)}, bf16[4,2,2,48,1152]{4,3,2,1,0:T(8,128)(2,1)}) custom-call(s32[9]{0:T(128)} %concatenate.209.where, bf16[4,48,1664]{2,1,0:T(8,128)(2,1)} %copy-done.11, bf16[4,48,1664]{2,1,0:T(8,128)(2,1)} %collective-permute-done.8.refs_1_, ...), custom_call_target="tpu_custom_call" | custom-call | bytes 5111808 | tf_op jit(solution)/shard_map/assemble/pallas_call | solution.py:155
  85.2 3.7 convolution_convert_fusion.q_ref.k_ref.v_ref
  88.9 11.6 %attend_forward.1 = (bf16[1024,384]{1,0:T(8,128)(2,1)}, f32[1024,384]{1,0:T(8,128)}, f32[3,2,1024]{2,1,0:T(2,128)}) custom-call(bf16[1024,1152]{1,0:T(8,128)(2,1)} %convolution_convert_fusion.q_ref.k_ref.v_ref, bf16[1024,1152]{1,0:T(8,128)(2,1)} %convolution_convert_fusion.q_ref.k_ref.v_ref, bf16[1024,1152]{1,0:T(8,128)(2,1)} %convolution_convert_fusion.q_ref.k_ref.v_ref, ...), custom_call_target="tpu_custom_call" | custom-call | flops 402653184 | bytes 393216 | tf_op jit(solution)/shard_map/attend_forward/pallas_call | solution.py:595
  100.5 4.0 %collective-permute-done.15 = bf16[2,48,2560]{2,1,0:T(8,128)(2,1)} collective-permute-done((bf16[2,48,2560]{2,1,0:T(8,128)(2,1)S(1)}, bf16[2,48,2560]{2,1,0:T(8,128)(2,1)}, u32[]{:S(2)}, u32[]{:S(2)}) %collective-permute-start.15) | collective-permute-done | bytes 491552 | tf_op jit(solution)/shard_map/ppermute | solution.py:46
  104.6 3.7 assemble.4
  116.0 13.9 %collective-permute-done.21.refs_1_ = bf16[4,48,2560]{2,1,0:T(8,128)(2,1)S(1)} collective-permute-done((bf16[4,48,2560]{2,1,0:T(8,128)(2,1)S(1)}, bf16[4,48,2560]{2,1,0:T(8,128)(2,1)S(1)}, u32[]{:S(2)}, u32[]{:S(2)}) %collective-permute-start.21) | collective-permute-done | bytes 983072 | tf_op jit(solution)/shard_map/ppermute | solution.py:46
  131.3 5.6 %multiply_convert_fusion = (bf16[1024,1536]{1,0:T(8,128)(2,1)}, f32[1024,1536]{1,0:T(8,128)}) fusion(bf16[1024,768]{1,0:T(8,128)(2,1)S(1)} %pad_maximum_fusion.2, bf16[768,1536]{1,0:T(8,128)(2,1)S(1)} %bitcast.252), kind=kOutput, calls=%fused_computation.7 | convolution fusion | flops 2423783424 | bytes 13369344 | tf_op jit(solution)/shard_map/dot_general | solution.py:718
  137.9 6.6 %collective-permute-done.23.refs_3_ = bf16[4,48,2560]{2,1,0:T(8,128)(2,1)} collective-permute-done((bf16[4,48,2560]{2,1,0:T(8,128)(2,1)S(1)}, bf16[4,48,2560]{2,1,0:T(8,128)(2,1)}, u32[]{:S(2)}, u32[]{:S(2)}) %collective-permute-start.23) | collective-permute-done | bytes 983072 | tf_op jit(solution)/shard_map/ppermute | solution.py:46
  144.5 4.4 %assemble.5 = (bf16[4,2,2,96,768]{4,3,2,1,0:T(8,128)(2,1)}, bf16[4,2,2,48,1024]{4,3,2,1,0:T(8,128)(2,1)}) custom-call(s32[9]{0:T(128)} %concatenate.209.where, bf16[4,48,2560]{2,1,0:T(8,128)(2,1)} %copy-done.7, bf16[4,48,2560]{2,1,0:T(8,128)(2,1)} %copy-done.24, bf16[4,48,2560]{2,1,0:T(8,128)(2,1)} %copy-done.25, ...), custom_call_target="tpu_custom_call" | custom-call | bytes 7864320 | tf_op jit(solution)/shard_map/assemble/pallas_call | solution.py:155
  148.8 5.2 %fusion.110 = f32[1024,768]{1,0:T(8,128)S(1)} fusion(bf16[1024,1536]{1,0:T(8,128)(2,1)} %get-tuple-element.217, bf16[1536,768]{1,0:T(8,128)(2,1)} %bitcast.254), kind=kOutput, calls=%fused_computation.280 | convolution fusion | flops 2415919104 | bytes 8650752 | tf_op jit(solution)/shard_map/dot_general | solution.py:718
  168.9 6.6 %fusion.5 = bf16[1024,1536]{1,0:T(8,128)(2,1)S(1)} fusion(f32[1024,1536]{1,0:T(8,128)} %get-tuple-element.218, bf16[1536,768]{1,0:T(8,128)(2,1)S(1)} %bitcast.255, bf16[512,768]{1,0:T(8,128)(2,1)S(1)} %collective-permute-done.27, bf16[512,768]{1,0:T(8,128)(2,1)S(1)} %get-tuple-element.222), kind=kOutput, calls=%fused_computation.6 | convolution fusion | flops 2434793472 | bytes 13369344 | tf_op jit(solution)/shard_map/dot_general | solution.py:726
  184.2 4.0 %convolution_convert_fusion.2 = bf16[1536,768]{1,0:T(8,128)(2,1)} fusion(bf16[1024,1536]{1,0:T(8,128)(2,1)S(1)} %copy-done.74, bf16[512,768]{1,0:T(8,128)(2,1)S(1)} %collective-permute-done.27, bf16[512,768]{1,0:T(8,128)(2,1)S(1)} %get-tuple-element.222), kind=kOutput, calls=%fused_computation.11 | convolution fusion | flops 2420244480 | bytes 7077888 | tf_op jit(solution)/shard_map/dot_general | solution.py:722
  193.3 4.9 %norm_back.2 = (f32[512,768]{1,0:T(8,128)}, bf16[512,768]{1,0:T(8,128)(2,1)}, f32[8,768]{1,0:T(8,128)}) custom-call(f32[512,768]{1,0:T(8,128)} %copy-done.3, f32[1,768]{1,0:T(1,128)} %slice.217.gain_ref, f32[1024,768]{1,0:T(8,128)} %copy-done.5, f32[512,768]{1,0:T(8,128)} %collective-permute-done.28.got_ref, f32[512,768]{1,0:T(8,128)} %get-tuple-element.223.more_ref, ...), custom_call_target="tpu_custom_call" | custom-call | bytes 393216 | tf_op jit(solution)/shard_map/norm_back/pallas_call | solution.py:701
  198.9 6.0 %convolution_convert_fusion.1 = bf16[768,1536]{1,0:T(8,128)(2,1)} fusion(bf16[1024,1536]{1,0:T(8,128)(2,1)} %copy-done.73, bf16[512,768]{1,0:T(8,128)(2,1)S(1)} %copy-done.34, bf16[512,768]{1,0:T(8,128)(2,1)S(1)} %copy-done.9), kind=kOutput, calls=%fused_computation.10 | convolution fusion | flops 2420244480 | bytes 7077888 | tf_op jit(solution)/shard_map/dot_general | solution.py:722
  212.8 3.5 collective-permute-done.30.refs_2_
  216.3 4.8 %scatter_near.4 = (bf16[4,48,2560]{2,1,0:T(8,128)(2,1)}, f32[4,48,2560]{2,1,0:T(8,128)}) custom-call(s32[4]{0:T(128)} %pad_add_fusion.2.w, bf16[4,2,2,96,768]{4,3,2,1,0:T(8,128)(2,1)} %bitcast.208, bf16[4,2,2,48,1024]{4,3,2,1,0:T(8,128)(2,1)} %bitcast.206, bf16[4,2,48,2560]{3,2,1,0:T(8,128)(2,1)} %collective-permute-done.30.refs_2_), custom_call_target="tpu_custom_call" | custom-call | bytes 6881280 | tf_op jit(solution)/shard_map/scatter_near/pallas_call | solution.py:362
  225.4 20.8 %attend_backward.1 = bf16[1024,1152]{1,0:T(8,128)(2,1)} custom-call(bf16[1024,1152]{1,0:T(8,128)(2,1)} %convolution_convert_fusion.q_ref.k_ref.v_ref, bf16[1024,1152]{1,0:T(8,128)(2,1)} %convolution_convert_fusion.q_ref.k_ref.v_ref, bf16[1024,1152]{1,0:T(8,128)(2,1)} %convolution_convert_fusion.q_ref.k_ref.v_ref, ...), custom_call_target="tpu_custom_call" | custom-call | flops 402653184 | bytes 393216 | tf_op jit(solution)/shard_map/attend_backward/pallas_call | solution.py:633
  247.3 4.4 %fusion.112.mine_ref = f32[1024,768]{1,0:T(8,128)S(1)} fusion(bf16[1024,1152]{1,0:T(8,128)(2,1)} %attend_backward.1, bf16[768,1152]{1,0:T(8,128)(2,1)} %bitcast.256), kind=kOutput, calls=%fused_computation.282 | convolution fusion | flops 1811939328 | bytes 7274496 | tf_op jit(solution)/shard_map/dot_general | solution.py:726
  256.1 5.6 %convolution_convert_fusion.3 = bf16[768,1152]{1,0:T(8,128)(2,1)} fusion(bf16[1024,1152]{1,0:T(8,128)(2,1)} %attend_backward.1, bf16[512,768]{1,0:T(8,128)(2,1)} %copy-done.68, bf16[512,768]{1,0:T(8,128)(2,1)} %copy-done.32), kind=kOutput, calls=%fused_computation.12 | convolution fusion | flops 1815969792 | bytes 5701632 | tf_op jit(solution)/shard_map/dot_general | solution.py:722
  265.0 4.8 %norm_back.3 = (f32[512,768]{1,0:T(8,128)}, bf16[512,768]{1,0:T(8,128)(2,1)}, f32[8,768]{1,0:T(8,128)}) custom-call(f32[512,768]{1,0:T(8,128)} %copy-done.2, f32[1,768]{1,0:T(1,128)} %slice.211.gain_ref, f32[1024,768]{1,0:T(8,128)} %copy-done.4, f32[512,768]{1,0:T(8,128)} %collective-permute-done.33.got_ref, f32[512,768]{1,0:T(8,128)} %get-tuple-element.103.more_ref, ...), custom_call_target="tpu_custom_call" | custom-call | bytes 393216 | tf_op jit(solution)/shard_map/norm_back/pallas_call | solution.py:701
  274.9 3.7 scatter_column.6
  278.6 4.3 %scatter_near.7 = (bf16[4,48,1920]{2,1,0:T(8,128)(2,1)}, f32[4,48,1920]{2,1,0:T(8,128)}) custom-call(s32[4]{0:T(128)} %pad_add_fusion.2.w, bf16[4,2,2,48,1536]{4,3,2,1,0:T(8,128)(2,1)} %bitcast.210, bf16[4,2,2,48,384]{4,3,2,1,0:T(8,128)(2,1)} %bitcast.216, bf16[4,2,48,1920]{3,2,1,0:T(8,128)(2,1)} %collective-permute-done.32.refs_2_), custom_call_target="tpu_custom_call" | custom-call | bytes 5160960 | tf_op jit(solution)/shard_map/scatter_near/pallas_call | solution.py:362
  298.9 3.5 scatter_column.7
  319.4 9.7 %collective-permute-done.48 = bf16[2,48,1920]{2,1,0:T(8,128)(2,1)S(1)} collective-permute-done((bf16[2,48,1920]{2,1,0:T(8,128)(2,1)}, bf16[2,48,1920]{2,1,0:T(8,128)(2,1)S(1)}, u32[]{:S(2)}, u32[]{:S(2)}) %collective-permute-start.48) | collective-permute-done | bytes 368672 | tf_op jit(solution)/shard_map/ppermute | solution.py:46
  330.3 3.8 %collective-permute-done.42 = bf16[2,48,1152]{2,1,0:T(8,128)(2,1)} collective-permute-done((bf16[2,48,1152]{2,1,0:T(8,128)(2,1)}, bf16[2,48,1152]{2,1,0:T(8,128)(2,1)}, u32[]{:S(2)}, u32[]{:S(2)}) %collective-permute-start.42) | collective-permute-done | bytes 221216 | tf_op jit(solution)/shard_map/ppermute | solution.py:46
  357.6 3.5 collective-permute-done.54
  361.1 4.5 %collective-permute-done.55 = f32[1,2]{1,0:T(1,128)S(1)} collective-permute-done((f32[1,2]{1,0:T(1,128)S(1)}, f32[1,2]{1,0:T(1,128)S(1)}, u32[]{:S(2)}, u32[]{:S(2)}) %collective-permute-start.55) | collective-permute-done | bytes 40 | tf_op jit(solution)/shard_map/ppermute | solution.py:46
  (465 shorter events, 172.1 us)
Async XLA Ops:
  14.8 11.2 %collective-permute-start.6 = (bf16[48,1920]{1,0:T(8,128)(2,1)S(1)}, bf16[48,1920]{1,0:T(8,128)(2,1)S(1)}, u32[]{:S(2)}, u32[]{:S(2)}) collective-permute-start(bf16[48,1920]{1,0:T(8,128)(2,1)S(1)} %get-tuple-element.77), channel_id=1, source_target_pairs={{0,8},{1,9},{2,10},{3,11},{4,12},{5,13},{6,14},{7,15},{8,0},{9,1},... | collective-permute-start | bytes 552968 | tf_op jit(solution)/shard_map/ppermute | solution.py:46
  16.6 16.4 %collective-permute-start.4 = (bf16[2,48,1664]{2,1,0:T(8,128)(2,1)S(1)}, bf16[2,48,1664]{2,1,0:T(8,128)(2,1)S(1)}, u32[]{:S(2)}, u32[]{:S(2)}) collective-permute-start(bf16[2,48,1664]{2,1,0:T(8,128)(2,1)S(1)} %pad_maximum_fusion.16), channel_id=1, source_target_pairs={{0,16},{1,17},{2,18},{3,19},{4,20},{5,21},{6,22},{7,23},{8,24},{9,... | collective-permute-start | bytes 958472 | tf_op jit(solution)/shard_map/ppermute | solution.py:46
  19.2 13.7 %collective-permute-start.7 = (bf16[48,2560]{1,0:T(8,128)(2,1)S(1)}, bf16[48,2560]{1,0:T(8,128)(2,1)S(1)}, u32[]{:S(2)}, u32[]{:S(2)}) collective-permute-start(bf16[48,2560]{1,0:T(8,128)(2,1)S(1)} %get-tuple-element.78), channel_id=1, source_target_pairs={{0,8},{1,9},{2,10},{3,11},{4,12},{5,13},{6,14},{7,15},{8,0},{9,1},... | collective-permute-start | bytes 737288 | tf_op jit(solution)/shard_map/ppermute | solution.py:46
  20.5 18.9 %collective-permute-start.2 = (bf16[256,768]{1,0:T(8,128)(2,1)}, bf16[256,768]{1,0:T(8,128)(2,1)S(1)}, u32[]{:S(2)}, u32[]{:S(2)}) collective-permute-start(bf16[256,768]{1,0:T(8,128)(2,1)} %get-tuple-element.176), channel_id=1, source_target_pairs={{0,2},{1,3},{2,0},{3,1},{4,6},{5,7},{6,4},{7,5},{8,10},{9,11},{10,... | collective-permute-start | bytes 1179656 | tf_op jit(solution)/shard_map/ppermute | solution.py:46
  33.0 20.0 %collective-permute-start.8 = (bf16[4,48,1664]{2,1,0:T(8,128)(2,1)S(1)}, bf16[4,48,1664]{2,1,0:T(8,128)(2,1)}, u32[]{:S(2)}, u32[]{:S(2)}) collective-permute-start(bf16[4,48,1664]{2,1,0:T(8,128)(2,1)S(1)} %pad_maximum_fusion.13.refs_0_), channel_id=1, source_target_pairs={{0,4},{1,3},{2,6},{3,1},{4,0},{5,7},{6,2},{7,5},{8,12},{9,11},{10,... | collective-permute-start | bytes 1916936 | tf_op jit(solution)/shard_map/ppermute | solution.py:46
  34.4 17.5 %collective-permute-start.10 = (bf16[2,48,1920]{2,1,0:T(8,128)(2,1)S(1)}, bf16[2,48,1920]{2,1,0:T(8,128)(2,1)}, u32[]{:S(2)}, u32[]{:S(2)}) collective-permute-start(bf16[2,48,1920]{2,1,0:T(8,128)(2,1)S(1)} %pad_maximum_fusion.15), channel_id=1, source_target_pairs={{0,16},{1,17},{2,18},{3,19},{4,20},{5,21},{6,22},{7,23},{8,24},{9,... | collective-permute-start | bytes 1105928 | tf_op jit(solution)/shard_map/ppermute | solution.py:46
  37.9 16.0 %collective-permute-start.9 = (bf16[4,48,1664]{2,1,0:T(8,128)(2,1)S(1)}, bf16[4,48,1664]{2,1,0:T(8,128)(2,1)S(1)}, u32[]{:S(2)}, u32[]{:S(2)}) collective-permute-start(bf16[4,48,1664]{2,1,0:T(8,128)(2,1)S(1)} %pad_maximum_fusion.13.refs_0_), channel_id=1, source_target_pairs={{0,2},{1,5},{2,0},{3,7},{4,6},{5,1},{6,4},{7,3},{8,10},{9,13},{10,... | collective-permute-start | bytes 1916936 | tf_op jit(solution)/shard_map/ppermute | solution.py:46
  40.4 28.3 %collective-permute-start.3 = (bf16[512,768]{1,0:T(8,128)(2,1)}, bf16[512,768]{1,0:T(8,128)(2,1)}, u32[]{:S(2)}, u32[]{:S(2)}) collective-permute-start(bf16[512,768]{1,0:T(8,128)(2,1)} %pad_maximum_fusion.9), channel_id=1, source_target_pairs={{0,1},{1,0},{2,3},{3,2},{4,5},{5,4},{6,7},{7,6},{8,9},{9,8},{10,11... | collective-permute-start | bytes 2359304 | tf_op jit(solution)/shard_map/ppermute | solution.py:46
  71.9 11.8 %collective-permute-start.14 = (bf16[4,48,1920]{2,1,0:T(8,128)(2,1)S(1)}, bf16[4,48,1920]{2,1,0:T(8,128)(2,1)}, u32[]{:S(2)}, u32[]{:S(2)}) collective-permute-start(bf16[4,48,1920]{2,1,0:T(8,128)(2,1)S(1)} %pad_maximum_fusion.10.refs_0_), channel_id=1, source_target_pairs={{0,4},{1,3},{2,6},{3,1},{4,0},{5,7},{6,2},{7,5},{8,12},{9,11},{10,... | collective-permute-start | bytes 2211848 | tf_op jit(solution)/shard_map/ppermute | solution.py:46
  79.2 25.2 %collective-permute-start.15 = (bf16[2,48,2560]{2,1,0:T(8,128)(2,1)S(1)}, bf16[2,48,2560]{2,1,0:T(8,128)(2,1)}, u32[]{:S(2)}, u32[]{:S(2)}) collective-permute-start(bf16[2,48,2560]{2,1,0:T(8,128)(2,1)S(1)} %pad_maximum_fusion.14), channel_id=1, source_target_pairs={{0,16},{1,17},{2,18},{3,19},{4,20},{5,21},{6,22},{7,23},{8,24},{9,... | collective-permute-start | bytes 1474568 | tf_op jit(solution)/shard_map/ppermute | solution.py:46
  80.2 24.4 %collective-permute-start.17 = (bf16[4,48,1920]{2,1,0:T(8,128)(2,1)S(1)}, bf16[4,48,1920]{2,1,0:T(8,128)(2,1)}, u32[]{:S(2)}, u32[]{:S(2)}) collective-permute-start(bf16[4,48,1920]{2,1,0:T(8,128)(2,1)S(1)} %pad_maximum_fusion.10.refs_0_), channel_id=1, source_target_pairs={{0,2},{1,5},{2,0},{3,7},{4,6},{5,1},{6,4},{7,3},{8,10},{9,13},{10,... | collective-permute-start | bytes 2211848 | tf_op jit(solution)/shard_map/ppermute | solution.py:46
  83.7 20.9 %collective-permute-start.18 = (bf16[4,48,1920]{2,1,0:T(8,128)(2,1)}, bf16[4,48,1920]{2,1,0:T(8,128)(2,1)}, u32[]{:S(2)}, u32[]{:S(2)}) collective-permute-start(bf16[4,48,1920]{2,1,0:T(8,128)(2,1)} %collective-permute-done.14.refs_1_), channel_id=1, source_target_pairs={{0,2},{1,5},{2,0},{3,7},{4,6},{5,1},{6,4},{7,3},{8,10},{9,13},{10,... | collective-permute-start | bytes 2211848 | tf_op jit(solution)/shard_map/ppermute | solution.py:46
  110.0 19.9 %collective-permute-start.21 = (bf16[4,48,2560]{2,1,0:T(8,128)(2,1)S(1)}, bf16[4,48,2560]{2,1,0:T(8,128)(2,1)S(1)}, u32[]{:S(2)}, u32[]{:S(2)}) collective-permute-start(bf16[4,48,2560]{2,1,0:T(8,128)(2,1)S(1)} %pad_maximum_fusion.8.refs_0_), channel_id=1, source_target_pairs={{0,4},{1,3},{2,6},{3,1},{4,0},{5,7},{6,2},{7,5},{8,12},{9,11},{10,... | collective-permute-start | bytes 2949128 | tf_op jit(solution)/shard_map/ppermute | solution.py:46
  115.3 15.1 %collective-permute-start.20 = (bf16[512,768]{1,0:T(8,128)(2,1)S(1)}, bf16[512,768]{1,0:T(8,128)(2,1)S(1)}, u32[]{:S(2)}, u32[]{:S(2)}) collective-permute-start(bf16[512,768]{1,0:T(8,128)(2,1)S(1)} %add_convert_fusion), channel_id=1, source_target_pairs={{0,1},{1,0},{2,3},{3,2},{4,5},{5,4},{6,7},{7,6},{8,9},{9,8},{10,11... | collective-permute-start | bytes 2359304 | tf_op jit(solution)/shard_map/ppermute | solution.py:46
  115.4 21.5 %collective-permute-start.22 = (bf16[4,48,2560]{2,1,0:T(8,128)(2,1)S(1)}, bf16[4,48,2560]{2,1,0:T(8,128)(2,1)S(1)}, u32[]{:S(2)}, u32[]{:S(2)}) collective-permute-start(bf16[4,48,2560]{2,1,0:T(8,128)(2,1)S(1)} %pad_maximum_fusion.8.refs_0_), channel_id=1, source_target_pairs={{0,2},{1,5},{2,0},{3,7},{4,6},{5,1},{6,4},{7,3},{8,10},{9,13},{10,... | collective-permute-start | bytes 2949128 | tf_op jit(solution)/shard_map/ppermute | solution.py:46
  129.9 14.6 %collective-permute-start.23 = (bf16[4,48,2560]{2,1,0:T(8,128)(2,1)S(1)}, bf16[4,48,2560]{2,1,0:T(8,128)(2,1)}, u32[]{:S(2)}, u32[]{:S(2)}) collective-permute-start(bf16[4,48,2560]{2,1,0:T(8,128)(2,1)S(1)} %collective-permute-done.21.refs_1_), channel_id=1, source_target_pairs={{0,2},{1,5},{2,0},{3,7},{4,6},{5,1},{6,4},{7,3},{8,10},{9,13},{10,... | collective-permute-start | bytes 2949128 | tf_op jit(solution)/shard_map/ppermute | solution.py:46
  180.6 12.0 %collective-permute-start.28 = (f32[512,768]{1,0:T(8,128)}, f32[512,768]{1,0:T(8,128)}, u32[]{:S(2)}, u32[]{:S(2)}) collective-permute-start(f32[512,768]{1,0:T(8,128)} %slice.280), channel_id=1, source_target_pairs={{0,1},{1,0},{2,3},{3,2},{4,5},{5,4},{6,7},{7,6},{8,9},{9,8},{10,11... | collective-permute-start | bytes 4718600 | tf_op jit(solution)/shard_map/ppermute | solution.py:46
  191.4 24.9 %collective-permute-start.30 = (bf16[4,2,48,2560]{3,2,1,0:T(8,128)(2,1)}, bf16[4,2,48,2560]{3,2,1,0:T(8,128)(2,1)}, u32[]{:S(2)}, u32[]{:S(2)}) collective-permute-start(bf16[4,2,48,2560]{3,2,1,0:T(8,128)(2,1)} %scatter_give.4), channel_id=1, source_target_pairs={{0,2},{1,5},{2,0},{3,7},{4,6},{5,1},{6,4},{7,3},{8,10},{9,13},{10,... | collective-permute-start | bytes 5898248 | tf_op jit(solution)/shard_map/ppermute | solution.py:46
  211.9 35.4 %collective-permute-start.32 = (bf16[4,2,48,1920]{3,2,1,0:T(8,128)(2,1)}, bf16[4,2,48,1920]{3,2,1,0:T(8,128)(2,1)}, u32[]{:S(2)}, u32[]{:S(2)}) collective-permute-start(bf16[4,2,48,1920]{3,2,1,0:T(8,128)(2,1)} %scatter_give.5), channel_id=1, source_target_pairs={{0,2},{1,5},{2,0},{3,7},{4,6},{5,1},{6,4},{7,3},{8,10},{9,13},{10,... | collective-permute-start | bytes 4423688 | tf_op jit(solution)/shard_map/ppermute | solution.py:46
  221.2 25.1 %collective-permute-start.31 = (bf16[4,48,2560]{2,1,0:T(8,128)(2,1)}, bf16[4,48,2560]{2,1,0:T(8,128)(2,1)S(1)}, u32[]{:S(2)}, u32[]{:S(2)}) collective-permute-start(bf16[4,48,2560]{2,1,0:T(8,128)(2,1)} %get-tuple-element.101), channel_id=1, source_target_pairs={{0,4},{1,3},{2,6},{3,1},{4,0},{5,7},{6,2},{7,5},{8,12},{9,11},{10,... | collective-permute-start | bytes 2949128 | tf_op jit(solution)/shard_map/ppermute | solution.py:46
  264.5 27.9 %collective-permute-start.40 = (bf16[4,2,48,1152]{3,2,1,0:T(8,128)(2,1)}, bf16[4,2,48,1152]{3,2,1,0:T(8,128)(2,1)S(1)}, u32[]{:S(2)}, u32[]{:S(2)}) collective-permute-start(bf16[4,2,48,1152]{3,2,1,0:T(8,128)(2,1)} %scatter_give.7), channel_id=1, source_target_pairs={{0,2},{1,5},{2,0},{3,7},{4,6},{5,1},{6,4},{7,3},{8,10},{9,13},{10,... | collective-permute-start | bytes 2654216 | tf_op jit(solution)/shard_map/ppermute | solution.py:46
  274.3 11.5 %collective-permute-start.34 = (bf16[512,384]{1,0:T(8,128)(2,1)}, bf16[512,384]{1,0:T(8,128)(2,1)}, u32[]{:S(2)}, u32[]{:S(2)}) collective-permute-start(bf16[512,384]{1,0:T(8,128)(2,1)} %bitcast.198), channel_id=1, source_target_pairs={{0,1},{1,0},{2,3},{3,2},{4,5},{5,4},{6,7},{7,6},{8,9},{9,8},{10,11... | collective-permute-start | bytes 1179656 | tf_op jit(solution)/shard_map/ppermute | solution.py:46
  278.6 31.2 %collective-permute-start.45 = (bf16[2,48,2560]{2,1,0:T(8,128)(2,1)}, bf16[2,48,2560]{2,1,0:T(8,128)(2,1)}, u32[]{:S(2)}, u32[]{:S(2)}) collective-permute-start(bf16[2,48,2560]{2,1,0:T(8,128)(2,1)} %get-tuple-element.118), channel_id=1, source_target_pairs={{0,16},{1,17},{2,18},{3,19},{4,20},{5,21},{6,22},{7,23},{8,24},{9,... | collective-permute-start | bytes 1474568 | tf_op jit(solution)/shard_map/ppermute | solution.py:46
  282.9 15.2 %collective-permute-start.47 = (bf16[4,48,1920]{2,1,0:T(8,128)(2,1)}, bf16[4,48,1920]{2,1,0:T(8,128)(2,1)S(1)}, u32[]{:S(2)}, u32[]{:S(2)}) collective-permute-start(bf16[4,48,1920]{2,1,0:T(8,128)(2,1)} %get-tuple-element.122), channel_id=1, source_target_pairs={{0,4},{1,3},{2,6},{3,1},{4,0},{5,7},{6,2},{7,5},{8,12},{9,11},{10,... | collective-permute-start | bytes 2211848 | tf_op jit(solution)/shard_map/ppermute | solution.py:46
  291.4 13.9 %collective-permute-start.36 = (bf16[4,2,48,512]{3,2,1,0:T(8,128)(2,1)}, bf16[4,2,48,512]{3,2,1,0:T(8,128)(2,1)S(1)}, u32[]{:S(2)}, u32[]{:S(2)}) collective-permute-start(bf16[4,2,48,512]{3,2,1,0:T(8,128)(2,1)} %scatter_give.6), channel_id=1, source_target_pairs={{0,2},{1,5},{2,0},{3,7},{4,6},{5,1},{6,4},{7,3},{8,10},{9,13},{10,... | collective-permute-start | bytes 1179656 | tf_op jit(solution)/shard_map/ppermute | solution.py:46
  296.7 14.3 %collective-permute-start.41 = (bf16[4,48,1152]{2,1,0:T(8,128)(2,1)}, bf16[4,48,1152]{2,1,0:T(8,128)(2,1)}, u32[]{:S(2)}, u32[]{:S(2)}) collective-permute-start(bf16[4,48,1152]{2,1,0:T(8,128)(2,1)} %get-tuple-element.113), channel_id=1, source_target_pairs={{0,4},{1,3},{2,6},{3,1},{4,0},{5,7},{6,2},{7,5},{8,12},{9,11},{10,... | collective-permute-start | bytes 1327112 | tf_op jit(solution)/shard_map/ppermute | solution.py:46
  302.4 26.7 %collective-permute-start.48 = (bf16[2,48,1920]{2,1,0:T(8,128)(2,1)}, bf16[2,48,1920]{2,1,0:T(8,128)(2,1)S(1)}, u32[]{:S(2)}, u32[]{:S(2)}) collective-permute-start(bf16[2,48,1920]{2,1,0:T(8,128)(2,1)} %get-tuple-element.125), channel_id=1, source_target_pairs={{0,16},{1,17},{2,18},{3,19},{4,20},{5,21},{6,22},{7,23},{8,24},{9,... | collective-permute-start | bytes 1105928 | tf_op jit(solution)/shard_map/ppermute | solution.py:46
  311.0 18.4 %collective-permute-start.46 = (bf16[48,2560]{1,0:T(8,128)(2,1)S(1)}, bf16[48,2560]{1,0:T(8,128)(2,1)S(1)}, u32[]{:S(2)}, u32[]{:S(2)}) collective-permute-start(bf16[48,2560]{1,0:T(8,128)(2,1)S(1)} %fusion.42), channel_id=1, source_target_pairs={{0,8},{1,9},{2,10},{3,11},{4,12},{5,13},{6,14},{7,15},{8,0},{9,1},... | collective-permute-start | bytes 737288 | tf_op jit(solution)/shard_map/ppermute | solution.py:46
  314.1 20.0 %collective-permute-start.42 = (bf16[2,48,1152]{2,1,0:T(8,128)(2,1)}, bf16[2,48,1152]{2,1,0:T(8,128)(2,1)}, u32[]{:S(2)}, u32[]{:S(2)}) collective-permute-start(bf16[2,48,1152]{2,1,0:T(8,128)(2,1)} %get-tuple-element.115), channel_id=1, source_target_pairs={{0,16},{1,17},{2,18},{3,19},{4,20},{5,21},{6,22},{7,23},{8,24},{9,... | collective-permute-start | bytes 663560 | tf_op jit(solution)/shard_map/ppermute | solution.py:46
  318.0 17.1 %collective-permute-start.38 = (bf16[2,48,512]{2,1,0:T(8,128)(2,1)}, bf16[2,48,512]{2,1,0:T(8,128)(2,1)S(1)}, u32[]{:S(2)}, u32[]{:S(2)}) collective-permute-start(bf16[2,48,512]{2,1,0:T(8,128)(2,1)} %get-tuple-element.110), channel_id=1, source_target_pairs={{0,16},{1,17},{2,18},{3,19},{4,20},{5,21},{6,22},{7,23},{8,24},{9,... | collective-permute-start | bytes 294920 | tf_op jit(solution)/shard_map/ppermute | solution.py:46
  329.3 12.2 %collective-permute-start.49 = (bf16[48,1920]{1,0:T(8,128)(2,1)S(1)}, bf16[48,1920]{1,0:T(8,128)(2,1)S(1)}, u32[]{:S(2)}, u32[]{:S(2)}) collective-permute-start(bf16[48,1920]{1,0:T(8,128)(2,1)S(1)} %fusion.48), channel_id=1, source_target_pairs={{0,8},{1,9},{2,10},{3,11},{4,12},{5,13},{6,14},{7,15},{8,0},{9,1},... | collective-permute-start | bytes 552968 | tf_op jit(solution)/shard_map/ppermute | solution.py:46
  342.2 30.1 %collective-permute-start.56 = (f32[24,1920]{1,0:T(8,128)S(1)}, f32[24,1920]{1,0:T(8,128)S(1)}, u32[]{:S(2)}, u32[]{:S(2)}) collective-permute-start(f32[24,1920]{1,0:T(8,128)S(1)} %get-tuple-element.180), channel_id=1, source_target_pairs={{0,1},{1,0},{2,3},{3,2},{4,5},{5,4},{6,7},{7,6},{8,9},{9,8},{10,11... | collective-permute-start | bytes 552968 | tf_op jit(solution)/shard_map/ppermute | solution.py:46
  (100 other events, 909.5 us)
